TPU v7x, 128 devices: a whole 4x4x4 slice. The times are simulated.
128 devices in a mesh: batch: 4 (over z), head: 2 (over core), seq: 16 (over x, y).
Axes of the slice: x: 4, y: 4, z: 4, core: 2. Of those that a mesh axis runs over, the one named last changes fastest.
Arguments:
- hidden: float32 [32768, 8192], P(('batch', 'seq')), parts along dimension 0, may hold values from -6 to 6
- row_scale: float32 [32768], P(('batch', 'seq')), parts along dimension 0, may hold values from 0.25 to 4
- key_value_weight: float32 [8192, 8, 256], P('seq', 'head'), may hold values from -0.0625 to 0.0625
- outlier: int32 [512, 8], P(('batch', 'seq'), 'head'), parts along dimension 0, may hold values 0 or 1
- sketch_sign_flags: int32 [8, 2, 128, 64], P('head'), may hold values from 0 to 1
Outputs:
- left: bfloat16 [8, 32768, 128], P('head', ('batch', 'seq')), parts along dimension 1
- right: float32 [32, 128, 128], P(('batch', 'head')), parts along dimension 0
There are 4 independent parts, one for each index of `batch`. A program takes and returns all parts, laid end to end along the dimension named above; an argument that names none is the same for every part. Nothing has to cross between parts.
All inputs are finite; a program needn't handle non-finite values. No bound on the sum of `outlier` on one device may be relied on, other than what follows from the above.
Results may differ from a plain program's by a relative error of at most 0.0015.
Values sent between devices are 32-bit elements; how exact they have to be, the bound alone decides.
No kernel may reach another device: no remote copies, remote signals or barrier semaphores. Data moves between devices by JAX's collectives and lax.ppermute only.
A program may use at most 192 MiB of HBM per device.

v0:
```python
import functools
import math

import jax
import jax.numpy as jnp
from jax import lax
from jax.experimental import pallas as pl
from jax.experimental.pallas import tpu as pltpu
from jax.sharding import PartitionSpec as P

GROUP = 64
RANK = 64
RING = 4
STEPS = 4
PERMUTED = 512
VMEM_LIMIT = 56 << 20
F32 = jnp.float32
BF16 = jnp.bfloat16
HIGHEST = lax.Precision.HIGHEST

SINE = [(-1) ** n * (2.0 * math.pi) ** (2 * n + 1) / math.factorial(2 * n + 1) for n in range(7)]


def split(x):
    high = x.astype(BF16)
    low = (x - high.astype(F32)).astype(BF16)
    return high, low


def sine_of_cycles(u):
    r = u - jnp.floor(u + 0.5)
    r = jnp.where(r > 0.25, 0.5 - r, jnp.where(r < -0.25, -0.5 - r, r))
    t = r * r
    p = jnp.full_like(t, SINE[-1])
    for c in SINE[-2::-1]:
        p = p * t + c
    return r * p


def dot(a, b, contract):
    return lax.dot_general(
        a, b, ((contract[:1], contract[1:]), ((), ())), precision=HIGHEST, preferred_element_type=F32
    )


def three_products(x, w):
    xh, xl = split(x)
    wh, wl = split(w)
    return jnp.dot(
        jnp.concatenate([xh, xl, xh], axis=1),
        jnp.concatenate([wh, wh, wl], axis=0),
        preferred_element_type=F32,
    )


def residual(kv, keep):
    tokens, cols = kv.shape
    grouped = kv.reshape(tokens // GROUP, GROUP, cols)
    step = jnp.max(jnp.abs(grouped), axis=1, keepdims=True) / 7.0 + 1e-06
    s = sine_of_cycles(grouped * (1.0 / step)) * keep[:, None, :]
    return s.reshape(tokens, cols)


def accumulate_kernel(shapes, first, *refs):
    refs = list(refs[1:])
    out_ref = refs.pop()
    if not first:
        base_ref = refs.pop()

    @pl.when(pl.program_id(0) == 0)
    def _():
        out_ref[...] = jnp.zeros_like(out_ref) if first else base_ref[...]

    total = None
    for parts in shapes:
        xs, refs = refs[:parts], refs[parts:]
        w_ref = refs.pop(0)
        x = xs[0][...] if parts == 1 else jnp.concatenate([r[...] for r in xs], axis=1)
        term = three_products(x, w_ref[...])
        total = term if total is None else total + term
    out_ref[...] += total


def block_specs(tokens, blocks):
    specs, at = [], 0
    for w, index, parts in blocks:
        rows = w.shape[0] // STEPS
        for i in range(parts):
            specs.append(
                pl.BlockSpec((tokens, rows // parts), lambda j, ix, a=at, n=parts, i=i: (0, ix[a + j * n + i]))
            )
        specs.append(pl.BlockSpec((rows, w.shape[1]), lambda j, ix: (j, 0)))
        at += STEPS * parts
    return specs, jnp.concatenate([index for _, index, _ in blocks])


def block_operands(hidden, blocks):
    return [x for w, _, parts in blocks for x in [hidden] * parts + [w]]


def cost(tokens, blocks):
    macs = sum(w.size for w, _, _ in blocks) * tokens
    return pl.CostEstimate(flops=6 * macs, bytes_accessed=sum(4 * w.size for w, _, _ in blocks) + 4 * tokens * 4096, transcendentals=0)


def accumulate(name, hidden, total, blocks):
    tokens = hidden.shape[0]
    cols = blocks[0][0].shape[1]
    specs, index = block_specs(tokens, blocks)
    whole = pl.BlockSpec((tokens, cols), lambda j, ix: (0, 0))
    return pl.pallas_call(
        functools.partial(accumulate_kernel, [parts for _, _, parts in blocks], total is None),
        grid_spec=pltpu.PrefetchScalarGridSpec(
            num_scalar_prefetch=1,
            grid=(STEPS,),
            in_specs=specs + ([] if total is None else [whole]),
            out_specs=whole,
        ),
        out_shape=jax.ShapeDtypeStruct((tokens, cols), F32),
        compiler_params=pltpu.CompilerParams(vmem_limit_bytes=VMEM_LIMIT, dimension_semantics=("arbitrary",)),
        name=name,
        cost_estimate=cost(tokens, blocks),
    )(index, *block_operands(hidden, blocks), *([] if total is None else [total]))


def accumulate_all_kernel(x_ref, w_ref, out_ref):
    @pl.when(pl.program_id(0) == 0)
    def _():
        out_ref[...] = jnp.zeros_like(out_ref)

    rows = w_ref.shape[0] * w_ref.shape[2]
    out_ref[...] += three_products(x_ref[...], w_ref[...].reshape(rows, w_ref.shape[3]))


def accumulate_all(hidden, weight):
    tokens = hidden.shape[0]
    batch, seq, quarter, cols = weight.shape
    return pl.pallas_call(
        accumulate_all_kernel,
        grid=(seq,),
        in_specs=[
            pl.BlockSpec((tokens, batch * quarter), lambda k: (0, k)),
            pl.BlockSpec((batch, 1, quarter, cols), lambda k: (0, k, 0, 0)),
        ],
        out_specs=pl.BlockSpec((tokens, cols), lambda k: (0, 0)),
        out_shape=jax.ShapeDtypeStruct((tokens, cols), F32),
        compiler_params=pltpu.CompilerParams(vmem_limit_bytes=VMEM_LIMIT, dimension_semantics=("arbitrary",)),
        name="cd",
        cost_estimate=pl.CostEstimate(
            flops=6 * tokens * weight.size, bytes_accessed=4 * (weight.size + hidden.size), transcendentals=0
        ),
    )(hidden, weight)


def project_kernel(index_ref, xa, wa, xb, wb, ab_ref, cd_ref, scale_ref, keep_ref, high_ref, low_ref, gram_ref, ab_acc):
    step = pl.program_id(0)

    @pl.when(step == 0)
    def _():
        ab_acc[...] = ab_ref[...]

    ab_acc[...] += three_products(xa[...], wa[...]) + three_products(xb[...], wb[...])

    @pl.when(step == STEPS - 1)
    def _():
        at = 0
        for part in (ab_acc, cd_ref):
            for p in range(part.shape[1] // 128):
                cols = slice(at, at + 128)
                r = residual(part[:, 128 * p : 128 * p + 128] * scale_ref[...], keep_ref[:, cols])
                rh, rl = split(r)
                high_ref[:, cols] = rh
                low_ref[:, cols] = rl
                both = lax.dot_general(
                    rh,
                    jnp.concatenate([rh, rl], axis=1),
                    (((0,), (0,)), ((), ())),
                    preferred_element_type=F32,
                )
                cross = both[:, 128:]
                gram_ref[cols, :] = both[:, :128] + (cross + cross.T)
                at += 128


def inverse_factors(grams):
    n = len(grams)
    lane = lax.broadcasted_iota(jnp.int32, (RANK, 128), 1)
    row = lax.broadcasted_iota(jnp.int32, (RANK, 128), 0)
    unit = jnp.where(lane - RANK == row, 1.0, 0.0).astype(F32)
    full = jnp.stack([jnp.where(lane < RANK, g, unit) for g in grams])
    blocks = [full[:, 8 * i : 8 * i + 8, :] for i in range(RANK // 8)]
    sub = lax.broadcasted_iota(jnp.int32, (n, 8, 1), 1)
    for j in range(RANK):
        jb, js = divmod(j, 8)
        pivot_row = blocks[jb][:, js : js + 1, :]
        scaled = pivot_row * (1.0 / pivot_row[:, :, j : j + 1])
        for i in range(jb, RANK // 8):
            column = blocks[i][:, :, j : j + 1]
            if i == jb:
                column = jnp.where(sub > js, column, 0.0)
            blocks[i] = blocks[i] - column * scaled
    full = jnp.concatenate(blocks, axis=1)
    out = []
    for p in range(n):
        a = full[p]
        pivots = jnp.sum(jnp.where(lane == row, a, 0.0), axis=1, keepdims=True)
        out.append(jnp.where(lane < RANK, 0.0, a) * lax.rsqrt(pivots))
    return out


def basis_start_kernel(sign_ref, out_ref):
    pairs = sign_ref.shape[0]
    inverses = inverse_factors([dot(sign_ref[p], sign_ref[p], (0, 0))[:RANK] for p in range(pairs)])
    for p in range(pairs):
        out_ref[p] = dot(sign_ref[p], jnp.concatenate([inverses[p]] * 2, axis=0), (1, 1))


def factor_kernel(root_length, gram_ref, start_ref, high_ref, low_ref, left_ref, right_ref):
    pairs = start_ref.shape[0]
    eye = lax.broadcasted_iota(jnp.int32, (128, 128), 0) == lax.broadcasted_iota(jnp.int32, (128, 128), 1)
    scales, ys, zs, grams = [], [], [], []
    for p in range(pairs):
        g = gram_ref[128 * p : 128 * p + 128, :]
        size = jnp.sum(jnp.sum(jnp.where(eye, g, 0.0), axis=1, keepdims=True), axis=0, keepdims=True) / 128.0
        g = g * (1.0 / size)
        y = dot(g, start_ref[p], (1, 0))
        z = dot(g, y, (1, 0))
        scales.append(size)
        ys.append(y)
        zs.append(z)
        grams.append(dot(y, z, (0, 0))[:RANK])
    inverses = inverse_factors(grams)
    zero = jnp.zeros((RANK, 128), F32)
    for h in range(pairs // 2):
        tops, rights = [], None
        for e in range(2):
            p = 2 * h + e
            wide = jnp.concatenate([inverses[p], zero] if e == 0 else [zero, inverses[p]], axis=0)
            tops.append(dot(ys[p], wide, (1, 1)) * (lax.rsqrt(scales[p]) * root_length))
            part = dot(zs[p], wide, (1, 1)) * (jnp.sqrt(scales[p]) * (1.0 / root_length))
            rights = part if rights is None else rights + part
        right_ref[h] = rights
        th, tl = split(jnp.concatenate(tops, axis=0))
        cols = slice(256 * h, 256 * h + 256)
        rh = high_ref[:, cols]
        rl = low_ref[:, cols]
        left_ref[h] = jnp.dot(
            jnp.concatenate([rh, rl, rh], axis=1),
            jnp.concatenate([th, th, tl], axis=0),
            preferred_element_type=F32,
        ).astype(BF16)


def partner(v, head, which):
    near, far = v ^ 1, 3 - v
    return jnp.where(head == which, near, far)


def around(v, head):
    second = partner(v, head, 1)
    return [v, partner(v, head, 0), second, partner(second, head, 0)]


def flat_partner(v, head, which):
    return (v ^ 1) if head == which else 3 - v


def plane_pairs(axis, which):
    pairs = []
    for h in range(2):
        for x in range(RING):
            for y in range(RING):
                tx, ty = (flat_partner(x, h, which), y) if axis == "x" else (x, flat_partner(y, h, which))
                pairs.append(((h * RING + x) * RING + y, (h * RING + tx) * RING + ty))
    return pairs


def gather_blocks(weight, multiply, start):
    def send(v, axis, which):
        return lax.ppermute(v, ("head", "seq"), plane_pairs(axis, which))

    join = lambda a, b: jnp.concatenate([a, b], axis=0)
    half = weight.shape[0] // 2
    a, b = weight[:half], weight[half:]
    for which in range(2):
        a, b = lax.optimization_barrier((a, b))
        a1, b1 = lax.optimization_barrier((send(a, "x", which), send(b, "y", which)))
        a, b = join(a, a1), join(b, b1)
    a, b = lax.optimization_barrier((a, b))
    a1, b1, a2, b2 = send(a, "y", 0), send(b, "x", 0), send(a, "y", 1), send(b, "x", 1)
    total = multiply(None, [(a, b, 0)])
    a1, b1, a2, b2, total, start = lax.optimization_barrier((a1, b1, a2, b2, total, start))
    a3, b3 = send(a1, "y", 1), send(b1, "x", 1)
    total = multiply(total, [(a1, b1, 1), (a2, b2, 2)])
    return a3, b3, total, start


def shards(hidden, row_scale, key_value_weight, outlier, sketch_sign_flags):
    tokens, width = hidden.shape
    rows, heads, kv_cols = key_value_weight.shape
    cols = heads * kv_cols
    pairs = 2 * heads
    groups = outlier.shape[0]
    seq = lax.axis_size("seq")
    root_length = math.sqrt(tokens * seq)

    signs = (2 * sketch_sign_flags - 1).astype(F32).reshape(pairs, 128, RANK)
    start = pl.pallas_call(
        basis_start_kernel,
        out_shape=jax.ShapeDtypeStruct((pairs, 128, 128), F32),
        name="start",
        cost_estimate=pl.CostEstimate(flops=10**8, bytes_accessed=10**6, transcendentals=0),
    )(jnp.concatenate([signs, signs], axis=2))

    head, place, plane = lax.axis_index("head"), lax.axis_index("seq"), lax.axis_index("batch")
    xs, ys = around(place // RING, head), around(place % RING, head)
    shard = lambda x, y: x * RING + y

    def blocks_of(a, b, k):
        return [
            (a, jnp.stack([2 * shard(x, ys[k]) for x in xs]), 1),
            (b, jnp.stack([2 * shard(xs[k], y) + 1 for y in ys]), 1),
        ]

    def multiply(total, arrivals):
        name = "ab0" if total is None else "ab1"
        return accumulate(name, hidden, total, [block for arrival in arrivals for block in blocks_of(*arrival)])

    flat = key_value_weight.reshape(rows, cols)
    quarter = rows // RING
    own = lax.dynamic_slice_in_dim(flat[:, PERMUTED:], plane * quarter, quarter, 0)
    rest = lax.all_gather(own, ("batch", "seq"), axis=0).reshape(RING, seq, quarter, cols - PERMUTED)
    a3, b3, ab, start = gather_blocks(flat[:, :PERMUTED], multiply, start)
    rest, ab = lax.optimization_barrier((rest, ab))
    cd = accumulate_all(hidden, rest)

    last = blocks_of(a3, b3, 3)
    specs, index = block_specs(tokens, last)
    keep = jnp.repeat((1 - outlier).astype(F32), kv_cols, axis=1)
    whole = lambda *shape: pl.BlockSpec(shape, lambda j, ix: (0,) * len(shape))
    high, low, gram = pl.pallas_call(
        project_kernel,
        grid_spec=pltpu.PrefetchScalarGridSpec(
            num_scalar_prefetch=1,
            grid=(STEPS,),
            in_specs=specs
            + [whole(tokens, t.shape[1]) for t in (ab, cd)]
            + [whole(tokens, 1), whole(groups, cols)],
            out_specs=[whole(tokens, cols), whole(tokens, cols), whole(128 * pairs, 128)],
            scratch_shapes=[pltpu.VMEM(ab.shape, F32)],
        ),
        out_shape=[
            jax.ShapeDtypeStruct((tokens, cols), BF16),
            jax.ShapeDtypeStruct((tokens, cols), BF16),
            jax.ShapeDtypeStruct((128 * pairs, 128), F32),
        ],
        compiler_params=pltpu.CompilerParams(vmem_limit_bytes=VMEM_LIMIT, dimension_semantics=("arbitrary",)),
        name="project",
        cost_estimate=cost(tokens, last),
    )(index, *block_operands(hidden, last), ab, cd, row_scale[:, None], keep)

    pieces = lax.all_to_all(gram, "seq", 0, 0, tiled=True)
    piece = jnp.sum(pieces.reshape(seq, 128 * pairs // seq, 128), axis=0)
    gram = lax.all_to_all(jnp.broadcast_to(piece, (seq,) + piece.shape), "seq", 0, 0).reshape(128 * pairs, 128)

    return pl.pallas_call(
        functools.partial(factor_kernel, root_length),
        out_shape=[
            jax.ShapeDtypeStruct((heads, tokens, 2 * RANK), BF16),
            jax.ShapeDtypeStruct((heads, 128, 2 * RANK), F32),
        ],
        compiler_params=pltpu.CompilerParams(vmem_limit_bytes=40 << 20),
        name="factor",
        cost_estimate=pl.CostEstimate(flops=10**9, bytes_accessed=4 << 20, transcendentals=0),
    )(gram, start, high, low)


def solution(mesh):
    return jax.shard_map(
        shards,
        mesh=mesh,
        in_specs=(
            P(("batch", "seq"), None),
            P(("batch", "seq")),
            P("seq", "head", None),
            P(("batch", "seq"), "head"),
            P("head", None, None, None),
        ),
        out_specs=(P("head", ("batch", "seq"), None), P(("batch", "head"), None, None)),
        check_vma=False,
    )
```

profile of v0, /device:TPU:0, one launch (start us, length us, event | category | flops | bytes accessed | tf_op | source)
XLA Modules:
  0.0 247.2 jit_solution(30111036288766908)
XLA Ops:
  7.2 0.0 all-gather.3.cloned.1.call-start
  7.2 2.1 copy.10
  9.3 0.1 slice.17
  9.4 0.7 constant_dynamic-slice_fusion
  10.1 0.0 all-gather.3.cloned.1.call-update
  10.1 0.1 fusion
  10.2 1.7 collective-permute-start
  11.9 1.6 collective-permute-start.1
  13.4 6.0 %collective-permute-done = f32[256,512]{1,0:T(8,128)S(1)} collective-permute-done((f32[256,512]{1,0:T(8,128)S(1)}, f32[256,512]{1,0:T(8,128)S(1)}, u32[]{:S(2)}, u32[]{:S(2)}) %collective-permute-start) | collective-permute-done | bytes 524320 | tf_op jit(solution)/shard_map/ppermute | solution.py:280
  19.5 1.6 collective-permute-done.1
  21.0 0.2 pad_maximum_fusion.2
  21.2 2.2 collective-permute-start.2
  23.4 3.0 %collective-permute-start.3 = (f32[512,512]{1,0:T(8,128)S(1)}, f32[512,512]{1,0:T(8,128)S(1)}, u32[]{:S(2)}, u32[]{:S(2)}) collective-permute-start(f32[512,512]{1,0:T(8,128)S(1)} %get-tuple-element.28), channel_id=1, source_target_pairs={{0,3},{1,2},{2,1},{3,0},{4,7},{5,6},{6,5},{7,4},{8,11},{9,10},{10,... | collective-permute-start | bytes 3145736 | tf_op jit(solution)/shard_map/ppermute | solution.py:280
  26.4 13.7 %collective-permute-done.2 = f32[512,512]{1,0:T(8,128)S(1)} collective-permute-done((f32[512,512]{1,0:T(8,128)S(1)}, f32[512,512]{1,0:T(8,128)S(1)}, u32[]{:S(2)}, u32[]{:S(2)}) %collective-permute-start.2) | collective-permute-done | bytes 1048608 | tf_op jit(solution)/shard_map/ppermute | solution.py:280
  40.1 2.1 collective-permute-done.3
  42.2 0.2 pad_maximum_fusion.1.refs_4_
  42.4 0.0 copy-start.3
  42.4 0.0 copy-start.5
  42.4 1.6 pad_maximum_fusion.refs_2_
  44.0 0.4 collective-permute-start.4
  44.3 0.6 collective-permute-start.5
  44.9 2.2 collective-permute-start.6
  47.1 1.2 collective-permute-start.7
  48.3 0.0 copy-done.3
  48.3 0.0 copy-done.5
  48.3 0.2 copy.8
  48.5 0.7 concatenate.29.refs_0_
  49.2 1.0 pad_maximum_fusion.4.sign_ref
  50.2 11.2 %start.1.start_ref = f32[8,128,128]{2,1,0:T(8,128)} custom-call(f32[8,128,128]{2,1,0:T(8,128)} %pad_maximum_fusion.4.sign_ref), custom_call_target="tpu_custom_call" | custom-call | flops 100000000 | bytes 1000000 | tf_op jit(solution)/shard_map/start/pallas_call | solution.py:308
  61.4 0.0 copy-start.6
  61.4 0.0 copy-start.7
  61.4 8.1 %ab0.1.refs_9_ = f32[512,512]{1,0:T(8,128)} custom-call(s32[8]{0:T(128)} %concatenate.29.refs_0_, f32[512,8192]{1,0:T(8,128)} %xb.1, f32[1024,512]{1,0:T(8,128)} %pad_maximum_fusion.refs_2_, f32[512,8192]{1,0:T(8,128)} %xb.1, f32[1024,512]{1,0:T(8,128)} %copy-done.3), custom_call_target="tpu_custom_call" | custom-call | flops 3221225472 | bytes 12582912 | tf_op jit(solution)/shard_map/ab0/pallas_call | solution.py:111
  69.6 55.7 %collective-permute-done.4.refs_2_ = f32[1024,512]{1,0:T(8,128)} collective-permute-done((f32[1024,512]{1,0:T(8,128)}, f32[1024,512]{1,0:T(8,128)}, u32[]{:S(2)}, u32[]{:S(2)}) %collective-permute-start.4) | collective-permute-done | bytes 2097184 | tf_op jit(solution)/shard_map/ppermute | solution.py:280
  125.3 0.0 collective-permute-done.5.refs_4_
  125.3 0.0 collective-permute-done.6.refs_6_
  125.3 1.0 collective-permute-done.7.refs_8_
  126.3 0.7 collective-permute-start.8
  127.0 0.7 collective-permute-start.9
  127.7 0.0 copy-done.6
  127.7 0.8 copy.9.scale_ref
  128.6 0.7 concatenate.24.index_ref
  129.3 0.6 concatenate.31.refs_0_
  129.9 0.0 copy-done.7
  129.9 12.8 %ab1.1.ab_ref = f32[512,512]{1,0:T(8,128)} custom-call(s32[16]{0:T(128)} %concatenate.31.refs_0_, f32[512,8192]{1,0:T(8,128)} %xb.1, f32[1024,512]{1,0:T(8,128)} %collective-permute-done.4.refs_2_, f32[512,8192]{1,0:T(8,128)} %xb.1, f32[1024,512]{1,0:T(8,128)} %collective-permute-done.5.refs_4_, f32[512,8192]{1,0:T(8,128)} %xb.1, ...), custom_call_target="tpu_custom_call" | custom-call | flops 6442450944 | bytes 16777216 | tf_op jit(solution)/shard_map/ab1/pallas_call | solution.py:111
  142.7 16.9 %all-gather.3.cloned.1.call-done = f32[8192,512]{1,0:T(8,128)} async-done(((f32[128,512]{1,0:T(8,128)}), f32[8192,512]{1,0:T(8,128)}) %all-gather.3.cloned.1.call-update) | async-done | bytes 16777232 | tf_op jit(solution)/shard_map/all_gather | solution.py:332
  159.5 23.0 %cd.1.cd_ref = f32[512,512]{1,0:T(8,128)} custom-call(f32[512,8192]{1,0:T(8,128)} %xb.1, f32[4,16,128,512]{3,2,1,0:T(8,128)} %bitcast.48), custom_call_target="tpu_custom_call" | custom-call | flops 12884901888 | bytes 33554432 | tf_op jit(solution)/shard_map/cd/pallas_call | solution.py:138
  182.5 0.0 collective-permute-done.8.wa
  182.5 0.0 copy-start.4
  182.5 0.0 collective-permute-done.9.wb
  182.5 0.8 broadcast_in_dim.10
  183.3 0.5 copy-done.4
  183.8 12.4 %project.1 = (bf16[512,1024]{1,0:T(8,128)(2,1)}, bf16[512,1024]{1,0:T(8,128)(2,1)}, f32[1024,128]{1,0:T(8,128)}) custom-call(s32[8]{0:T(128)} %concatenate.24.index_ref, f32[512,8192]{1,0:T(8,128)} %xb.1, f32[1024,512]{1,0:T(8,128)} %copy-done.4, f32[512,8192]{1,0:T(8,128)} %xb.1, f32[1024,512]{1,0:T(8,128)} %collective-permute-done.9.wb, ...), custom_call_target="tpu_custom_call" | custom-call | flops 3221225472 | bytes 12582912 | tf_op jit(solution)/shard_map/project/pallas_call | solution.py:341
  196.2 0.0 copy-start
  196.2 0.0 copy-start.1
  196.2 0.0 copy-start.2
  196.2 18.0 %all_to_all.14 = f32[16,64,128]{2,1,0:T(8,128)S(1)} all-to-all(f32[16,64,128]{2,1,0:T(8,128)} %bitcast.45), channel_id=1, replica_groups=mesh['batch'=4,'head'=2,'seq'=16] {'seq'}, dimensions={0} | all-to-all | bytes 1048576 | tf_op jit(solution)/shard_map/all_to_all | solution.py:362
  214.4 13.8 %all_to_all.15 = f32[16,64,128]{2,1,0:T(8,128)S(1)} all-to-all(f32[16,64,128]{2,1,0:T(8,128)S(1)} %broadcast_in_dim.11), channel_id=1, replica_groups=mesh['batch'=4,'head'=2,'seq'=16] {'seq'}, dimensions={0} | all-to-all | bytes 1048576 | tf_op jit(solution)/shard_map/all_to_all | solution.py:364
  228.1 0.0 copy-done
  228.2 0.0 copy-done.1
  228.2 0.0 copy-done.2
  228.2 12.2 %factor.1 = (bf16[4,512,128]{2,1,0:T(8,128)(2,1)}, f32[4,128,128]{2,1,0:T(8,128)}) custom-call(f32[1024,128]{1,0:T(8,128)S(1)} %bitcast.40, f32[8,128,128]{2,1,0:T(8,128)S(1)} %copy-done, bf16[512,1024]{1,0:T(8,128)(2,1)S(1)} %copy-done.1, bf16[512,1024]{1,0:T(8,128)(2,1)S(1)} %copy-done.2), custom_call_target="tpu_custom_call" | custom-call | flops 1000000000 | bytes 4194304 | tf_op jit(solution)/shard_map/factor/pallas_call | solution.py:366
  (4 shorter events, 0.1 us)
Async XLA Ops:
  7.2 152.4 %all-gather.3.cloned.1.call-start = ((), (), s32[]{:S(2)}) async-start(), calls=%async_computation.2 | async-start | bytes 17039360 | tf_op jit(solution)/shard_map/all_gather | solution.py:332
  10.2 9.3 %collective-permute-start = (f32[256,512]{1,0:T(8,128)S(1)}, f32[256,512]{1,0:T(8,128)S(1)}, u32[]{:S(2)}, u32[]{:S(2)}) collective-permute-start(f32[256,512]{1,0:T(8,128)S(1)} %get-tuple-element.23), channel_id=1, source_target_pairs={{0,4},{1,5},{2,6},{3,7},{4,0},{5,1},{6,2},{7,3},{8,12},{9,13},{10,... | collective-permute-start | bytes 1572872 | tf_op jit(solution)/shard_map/ppermute | solution.py:280
  11.9 9.2 %collective-permute-start.1 = (f32[256,512]{1,0:T(8,128)S(1)}, f32[256,512]{1,0:T(8,128)S(1)}, u32[]{:S(2)}, u32[]{:S(2)}) collective-permute-start(f32[256,512]{1,0:T(8,128)S(1)} %get-tuple-element.24), channel_id=1, source_target_pairs={{0,1},{1,0},{2,3},{3,2},{4,5},{5,4},{6,7},{7,6},{8,9},{9,8},{10,11... | collective-permute-start | bytes 1572872 | tf_op jit(solution)/shard_map/ppermute | solution.py:280
  21.2 18.9 %collective-permute-start.2 = (f32[512,512]{1,0:T(8,128)S(1)}, f32[512,512]{1,0:T(8,128)S(1)}, u32[]{:S(2)}, u32[]{:S(2)}) collective-permute-start(f32[512,512]{1,0:T(8,128)S(1)} %get-tuple-element.27), channel_id=1, source_target_pairs={{0,12},{1,13},{2,14},{3,15},{4,8},{5,9},{6,10},{7,11},{8,4},{9,5},... | collective-permute-start | bytes 3145736 | tf_op jit(solution)/shard_map/ppermute | solution.py:280
  23.4 18.8 %collective-permute-start.3 = (f32[512,512]{1,0:T(8,128)S(1)}, f32[512,512]{1,0:T(8,128)S(1)}, u32[]{:S(2)}, u32[]{:S(2)}) collective-permute-start(f32[512,512]{1,0:T(8,128)S(1)} %get-tuple-element.28), channel_id=1, source_target_pairs={{0,3},{1,2},{2,1},{3,0},{4,7},{5,6},{6,5},{7,4},{8,11},{9,10},{10,... | collective-permute-start | bytes 3145736 | tf_op jit(solution)/shard_map/ppermute | solution.py:280
  42.4 5.9 %copy-start.3 = (f32[1024,512]{1,0:T(8,128)}, f32[1024,512]{1,0:T(8,128)S(1)}, u32[]{:S(2)}) copy-start(f32[1024,512]{1,0:T(8,128)S(1)} %pad_maximum_fusion.1.refs_4_) | copy-start | bytes 6291460
  42.4 5.9 %copy-start.5 = (s32[4,2,128,64]{2,3,1,0:T(8,128)S(1)}, s32[4,2,128,64]{2,3,1,0:T(8,128)}, u32[]{:S(2)}) copy-start(s32[4,2,128,64]{2,3,1,0:T(8,128)} %param.9) | copy-start | bytes 786436
  44.0 81.3 %collective-permute-start.4 = (f32[1024,512]{1,0:T(8,128)}, f32[1024,512]{1,0:T(8,128)}, u32[]{:S(2)}, u32[]{:S(2)}) collective-permute-start(f32[1024,512]{1,0:T(8,128)} %pad_maximum_fusion.refs_2_), channel_id=1, source_target_pairs={{0,1},{1,0},{2,3},{3,2},{4,5},{5,4},{6,7},{7,6},{8,9},{9,8},{10,11... | collective-permute-start | bytes 6291464 | tf_op jit(solution)/shard_map/ppermute | solution.py:280
  44.3 81.0 %collective-permute-start.5 = (f32[1024,512]{1,0:T(8,128)S(1)}, f32[1024,512]{1,0:T(8,128)}, u32[]{:S(2)}, u32[]{:S(2)}) collective-permute-start(f32[1024,512]{1,0:T(8,128)S(1)} %pad_maximum_fusion.1.refs_4_), channel_id=1, source_target_pairs={{0,4},{1,5},{2,6},{3,7},{4,0},{5,1},{6,2},{7,3},{8,12},{9,13},{10,... | collective-permute-start | bytes 6291464 | tf_op jit(solution)/shard_map/ppermute | solution.py:280
  44.9 80.4 %collective-permute-start.6 = (f32[1024,512]{1,0:T(8,128)}, f32[1024,512]{1,0:T(8,128)}, u32[]{:S(2)}, u32[]{:S(2)}) collective-permute-start(f32[1024,512]{1,0:T(8,128)} %pad_maximum_fusion.refs_2_), channel_id=1, source_target_pairs={{0,3},{1,2},{2,1},{3,0},{4,7},{5,6},{6,5},{7,4},{8,11},{9,10},{10,... | collective-permute-start | bytes 6291464 | tf_op jit(solution)/shard_map/ppermute | solution.py:280
  47.1 79.3 %collective-permute-start.7 = (f32[1024,512]{1,0:T(8,128)S(1)}, f32[1024,512]{1,0:T(8,128)}, u32[]{:S(2)}, u32[]{:S(2)}) collective-permute-start(f32[1024,512]{1,0:T(8,128)S(1)} %pad_maximum_fusion.1.refs_4_), channel_id=1, source_target_pairs={{0,12},{1,13},{2,14},{3,15},{4,8},{5,9},{6,10},{7,11},{8,4},{9,5},... | collective-permute-start | bytes 6291464 | tf_op jit(solution)/shard_map/ppermute | solution.py:280
  61.4 66.3 %copy-start.6 = (f32[512]{0:T(512)S(1)}, f32[512]{0:T(512)}, u32[]{:S(2)}) copy-start(f32[512]{0:T(512)} %param.6) | copy-start | bytes 6148
  61.4 68.5 %copy-start.7 = (s32[8,4]{0,1:T(4,128)S(1)}, s32[8,4]{0,1:T(4,128)}, u32[]{:S(2)}) copy-start(s32[8,4]{0,1:T(4,128)} %param.8) | copy-start | bytes 388
  126.3 56.2 %collective-permute-start.8 = (f32[1024,512]{1,0:T(8,128)}, f32[1024,512]{1,0:T(8,128)S(1)}, u32[]{:S(2)}, u32[]{:S(2)}) collective-permute-start(f32[1024,512]{1,0:T(8,128)} %collective-permute-done.4.refs_2_), channel_id=1, source_target_pairs={{0,3},{1,2},{2,1},{3,0},{4,7},{5,6},{6,5},{7,4},{8,11},{9,10},{10,... | collective-permute-start | bytes 6291464 | tf_op jit(solution)/shard_map/ppermute | solution.py:280
  127.0 55.5 %collective-permute-start.9 = (f32[1024,512]{1,0:T(8,128)}, f32[1024,512]{1,0:T(8,128)}, u32[]{:S(2)}, u32[]{:S(2)}) collective-permute-start(f32[1024,512]{1,0:T(8,128)} %collective-permute-done.5.refs_4_), channel_id=1, source_target_pairs={{0,12},{1,13},{2,14},{3,15},{4,8},{5,9},{6,10},{7,11},{8,4},{9,5},... | collective-permute-start | bytes 6291464 | tf_op jit(solution)/shard_map/ppermute | solution.py:280
  182.5 1.3 copy-start.4
  196.2 31.9 %copy-start = (f32[8,128,128]{2,1,0:T(8,128)S(1)}, f32[8,128,128]{2,1,0:T(8,128)}, u32[]{:S(2)}) copy-start(f32[8,128,128]{2,1,0:T(8,128)} %start.1.start_ref) | copy-start | bytes 1572868
  196.2 31.9 %copy-start.1 = (bf16[512,1024]{1,0:T(8,128)(2,1)S(1)}, bf16[512,1024]{1,0:T(8,128)(2,1)}, u32[]{:S(2)}) copy-start(bf16[512,1024]{1,0:T(8,128)(2,1)} %get-tuple-element.42.high_ref) | copy-start | bytes 3145732
  196.2 31.9 %copy-start.2 = (bf16[512,1024]{1,0:T(8,128)(2,1)S(1)}, bf16[512,1024]{1,0:T(8,128)(2,1)}, u32[]{:S(2)}) copy-start(bf16[512,1024]{1,0:T(8,128)(2,1)} %get-tuple-element.43.low_ref) | copy-start | bytes 3145732
Sparse Core Ops, SparseCore 0:
  11.5 148.0 all-gather.2
where the time goes:
time: 248 us; the launch traced here: 247 us
  waiting for transfers between devices  97.1 us (39%)
  Pallas kernels  79.7 us (32%)
  blocking collectives  31.8 us (13%)
  starting transfers between devices  14.2 us (6%)
  between operations  14.1 us (6%)
  local copies, waits for them, and re-layouts  7.35 us (3%)
  other arithmetic  2.97 us (1%)
    ppermute x10, waiting for transfers between devices, send(): return lax.ppermute(v, ('head', 'seq'), plane_pairs(axis, which))  80.2 us
    pallas_call x1, Pallas kernels, accumulate_all(): pl.pallas_call(accumulate_all_kernel, grid=(seq,), in_specs=[pl.BlockSpec...  23 us
    pallas_call x2, Pallas kernels, accumulate(): pl.pallas_call(functools.partial(accumulate_kernel, [parts for _, _, part...  20.9 us
    all_to_all x1, blocking collectives, shards(): pieces = lax.all_to_all(gram, 'seq', 0, 0, tiled=True)  18 us
    all_gather x1, waiting for transfers between devices, shards(): lax.all_gather(own, ('batch', 'seq'), axis=0)  16.9 us
    ppermute x10, starting transfers between devices, send(): return lax.ppermute(v, ('head', 'seq'), plane_pairs(axis, which))  14.1 us
    all_to_all x1, blocking collectives, shards(): lax.all_to_all(jnp.broadcast_to(piece, (seq,) + piece.shape), 'seq', 0, 0)  13.8 us
    pallas_call x1, Pallas kernels, shards(): pl.pallas_call(project_kernel, grid_spec=pltpu.PrefetchScalarGridSpec(num...  12.4 us
  transfers between devices with their start and end apart: 11, of which 7 were waited for; matrix products, arithmetic and copies ran while one was open for 2% of the time, Pallas kernels for 22%

commit v1 on v0

--- a/solution.py
+++ b/solution.py
@@ -12,7 +12,10 @@
 RANK = 64
 RING = 4
 STEPS = 4
-PERMUTED = 512
+PART = 256
+WIDE = 256
+UNROLL = 4
+ORDERS = ("xyz", "yzx", "xzy")
 VMEM_LIMIT = 56 << 20
 F32 = jnp.float32
 BF16 = jnp.bfloat16
@@ -54,14 +57,11 @@
 
 
 def residual(kv, keep):
-    tokens, cols = kv.shape
-    grouped = kv.reshape(tokens // GROUP, GROUP, cols)
-    step = jnp.max(jnp.abs(grouped), axis=1, keepdims=True) / 7.0 + 1e-06
-    s = sine_of_cycles(grouped * (1.0 / step)) * keep[:, None, :]
-    return s.reshape(tokens, cols)
-
-
-def accumulate_kernel(shapes, first, *refs):
+    step = jnp.max(jnp.abs(kv), axis=0, keepdims=True) / 7.0 + 1e-06
+    return sine_of_cycles(kv * (1.0 / step)) * keep
+
+
+def accumulate_kernel(parts, first, *refs):
     refs = list(refs[1:])
     out_ref = refs.pop()
     if not first:
@@ -71,45 +71,47 @@
     def _():
         out_ref[...] = jnp.zeros_like(out_ref) if first else base_ref[...]
 
-    total = None
-    for parts in shapes:
-        xs, refs = refs[:parts], refs[parts:]
-        w_ref = refs.pop(0)
-        x = xs[0][...] if parts == 1 else jnp.concatenate([r[...] for r in xs], axis=1)
-        term = three_products(x, w_ref[...])
-        total = term if total is None else total + term
-    out_ref[...] += total
+    add_blocks(parts, refs, out_ref)
+
+
+def add_blocks(parts, refs, total_ref):
+    terms = {}
+    for i, part in enumerate(parts):
+        xs, w_ref = refs[5 * i : 5 * i + 4], refs[5 * i + 4]
+        term = three_products(jnp.concatenate([r[...] for r in xs], axis=1), w_ref[...])
+        terms[part] = terms[part] + term if part in terms else term
+    for part, term in terms.items():
+        cols = term.shape[1]
+        total_ref[:, part * cols : part * cols + cols] += term
 
 
 def block_specs(tokens, blocks):
-    specs, at = [], 0
-    for w, index, parts in blocks:
+    specs = []
+    for b, (_, w, index) in enumerate(blocks):
         rows = w.shape[0] // STEPS
-        for i in range(parts):
-            specs.append(
-                pl.BlockSpec((tokens, rows // parts), lambda j, ix, a=at, n=parts, i=i: (0, ix[a + j * n + i]))
-            )
+        for i in range(4):
+            specs.append(pl.BlockSpec((tokens, rows // 4), lambda j, ix, a=b * 4 * STEPS + i: (0, ix[a + 4 * j])))
         specs.append(pl.BlockSpec((rows, w.shape[1]), lambda j, ix: (j, 0)))
-        at += STEPS * parts
-    return specs, jnp.concatenate([index for _, index, _ in blocks])
+    return specs, jnp.concatenate([index for _, _, index in blocks])
 
 
 def block_operands(hidden, blocks):
-    return [x for w, _, parts in blocks for x in [hidden] * parts + [w]]
+    return [x for _, w, _ in blocks for x in [hidden] * 4 + [w]]
 
 
 def cost(tokens, blocks):
-    macs = sum(w.size for w, _, _ in blocks) * tokens
-    return pl.CostEstimate(flops=6 * macs, bytes_accessed=sum(4 * w.size for w, _, _ in blocks) + 4 * tokens * 4096, transcendentals=0)
-
-
-def accumulate(name, hidden, total, blocks):
+    macs = sum(w.size for _, w, _ in blocks) * tokens
+    return pl.CostEstimate(
+        flops=6 * macs, bytes_accessed=sum(4 * w.size + 4 * tokens * w.shape[0] for _, w, _ in blocks), transcendentals=0
+    )
+
+
+def accumulate(name, hidden, total, cols, blocks):
     tokens = hidden.shape[0]
-    cols = blocks[0][0].shape[1]
     specs, index = block_specs(tokens, blocks)
     whole = pl.BlockSpec((tokens, cols), lambda j, ix: (0, 0))
     return pl.pallas_call(
-        functools.partial(accumulate_kernel, [parts for _, _, parts in blocks], total is None),
+        functools.partial(accumulate_kernel, [part for part, _, _ in blocks], total is None),
         grid_spec=pltpu.PrefetchScalarGridSpec(
             num_scalar_prefetch=1,
             grid=(STEPS,),
@@ -128,8 +130,10 @@
     def _():
         out_ref[...] = jnp.zeros_like(out_ref)
 
-    rows = w_ref.shape[0] * w_ref.shape[2]
-    out_ref[...] += three_products(x_ref[...], w_ref[...].reshape(rows, w_ref.shape[3]))
+    batch, shards_in, quarter, cols = w_ref.shape
+    rows = batch * quarter
+    for s in range(shards_in):
+        out_ref[...] += three_products(x_ref[:, s * rows : s * rows + rows], w_ref[:, s].reshape(rows, cols))
 
 
 def accumulate_all(hidden, weight):
@@ -137,49 +141,65 @@
     batch, seq, quarter, cols = weight.shape
     return pl.pallas_call(
         accumulate_all_kernel,
-        grid=(seq,),
+        grid=(seq // 2,),
         in_specs=[
-            pl.BlockSpec((tokens, batch * quarter), lambda k: (0, k)),
-            pl.BlockSpec((batch, 1, quarter, cols), lambda k: (0, k, 0, 0)),
+            pl.BlockSpec((tokens, 2 * batch * quarter), lambda k: (0, k)),
+            pl.BlockSpec((batch, 2, quarter, cols), lambda k: (0, k, 0, 0)),
         ],
         out_specs=pl.BlockSpec((tokens, cols), lambda k: (0, 0)),
         out_shape=jax.ShapeDtypeStruct((tokens, cols), F32),
         compiler_params=pltpu.CompilerParams(vmem_limit_bytes=VMEM_LIMIT, dimension_semantics=("arbitrary",)),
-        name="cd",
+        name="rest",
         cost_estimate=pl.CostEstimate(
             flops=6 * tokens * weight.size, bytes_accessed=4 * (weight.size + hidden.size), transcendentals=0
         ),
     )(hidden, weight)
 
 
-def project_kernel(index_ref, xa, wa, xb, wb, ab_ref, cd_ref, scale_ref, keep_ref, high_ref, low_ref, gram_ref, ab_acc):
+def project_kernel(parts, *refs):
+    refs = list(refs[1:])
+    blocks, refs = refs[: 5 * len(parts)], refs[5 * len(parts) :]
+    base_ref, rest_ref, scale_ref, keep_ref, high_ref, low_ref, gram_ref, total_ref = refs
     step = pl.program_id(0)
 
     @pl.when(step == 0)
     def _():
-        ab_acc[...] = ab_ref[...]
-
-    ab_acc[...] += three_products(xa[...], wa[...]) + three_products(xb[...], wb[...])
+        total_ref[...] = base_ref[...]
+
+    add_blocks(parts, blocks, total_ref)
 
     @pl.when(step == STEPS - 1)
     def _():
-        at = 0
-        for part in (ab_acc, cd_ref):
-            for p in range(part.shape[1] // 128):
-                cols = slice(at, at + 128)
-                r = residual(part[:, 128 * p : 128 * p + 128] * scale_ref[...], keep_ref[:, cols])
-                rh, rl = split(r)
-                high_ref[:, cols] = rh
-                low_ref[:, cols] = rl
+        epilogue(total_ref, rest_ref, scale_ref, keep_ref, high_ref, low_ref, gram_ref)
+
+
+def epilogue(total_ref, rest_ref, scale_ref, keep_ref, high_ref, low_ref, gram_ref):
+    tokens = total_ref.shape[0]
+    at = 0
+    for part in (total_ref, rest_ref):
+        for first in range(0, part.shape[1], WIDE):
+            here = slice(at, at + WIDE)
+
+            @pl.loop(0, tokens // GROUP, unroll=UNROLL)
+            def _(g, part=part, first=first, here=here):
+                rows = pl.ds(pl.multiple_of(g * GROUP, GROUP), GROUP)
+                kv = part[rows, first : first + WIDE] * scale_ref[rows, :]
+                keep = keep_ref[pl.ds(pl.multiple_of(g * 8, 8), 8), here][:1]
+                rh, rl = split(residual(kv, keep))
+                high_ref[rows, here] = rh
+                low_ref[rows, here] = rl
+
+            for cols in [slice(c, c + 128) for c in range(at, at + WIDE, 128)]:
+                rh = high_ref[:, cols]
                 both = lax.dot_general(
                     rh,
-                    jnp.concatenate([rh, rl], axis=1),
+                    jnp.concatenate([rh, low_ref[:, cols]], axis=1),
                     (((0,), (0,)), ((), ())),
                     preferred_element_type=F32,
                 )
                 cross = both[:, 128:]
                 gram_ref[cols, :] = both[:, :128] + (cross + cross.T)
-                at += 128
+            at += WIDE
 
 
 def inverse_factors(grams):
@@ -275,24 +295,37 @@
     return pairs
 
 
-def gather_blocks(weight, multiply, start):
-    def send(v, axis, which):
-        return lax.ppermute(v, ("head", "seq"), plane_pairs(axis, which))
-
-    join = lambda a, b: jnp.concatenate([a, b], axis=0)
-    half = weight.shape[0] // 2
-    a, b = weight[:half], weight[half:]
-    for which in range(2):
-        a, b = lax.optimization_barrier((a, b))
-        a1, b1 = lax.optimization_barrier((send(a, "x", which), send(b, "y", which)))
-        a, b = join(a, a1), join(b, b1)
-    a, b = lax.optimization_barrier((a, b))
-    a1, b1, a2, b2 = send(a, "y", 0), send(b, "x", 0), send(a, "y", 1), send(b, "x", 1)
-    total = multiply(None, [(a, b, 0)])
-    a1, b1, a2, b2, total, start = lax.optimization_barrier((a1, b1, a2, b2, total, start))
-    a3, b3 = send(a1, "y", 1), send(b1, "x", 1)
-    total = multiply(total, [(a1, b1, 1), (a2, b2, 2)])
-    return a3, b3, total, start
+def depth_pairs(which):
+    return [(z * 2 + h, flat_partner(z, h, which) * 2 + h) for z in range(RING) for h in range(2)]
+
+
+def send(v, axis, which):
+    if axis == "z":
+        return lax.ppermute(v, ("batch", "head"), depth_pairs(which))
+    return lax.ppermute(v, ("head", "seq"), plane_pairs(axis, which))
+
+
+def gather_blocks(parts, orders, multiply, start, rest):
+    barrier = lambda values: list(lax.optimization_barrier(tuple(values)))
+    both = range(len(parts))
+    for phase in range(2):
+        for which in range(2):
+            parts = barrier(parts)
+            came = barrier([send(v, order[phase], which) for v, order in zip(parts, orders)])
+            parts = [jnp.concatenate(pair, axis=0) for pair in zip(parts, came)]
+    first = barrier(parts)
+    came = [send(v, order[2], 0) for v, order in zip(first, orders)]
+    total = multiply(None, [(i, first[i], 0) for i in both])
+    *came, total, start = barrier(came + first + [total, start])
+    second, first = came[: len(parts)], came[len(parts) :]
+    came = [send(v, order[2], 1) for v, order in zip(first, orders)]
+    total = multiply(total, [(i, second[i], 1) for i in both])
+    *came, total = barrier(came + second + [total])
+    third, second = came[: len(parts)], came[len(parts) :]
+    last = [send(v, order[2], 1) for v, order in zip(second, orders)]
+    total = multiply(total, [(i, third[i], 2) for i in both])
+    total, rest = barrier([total, rest])
+    return last, total, start, rest
 
 
 def shards(hidden, row_scale, key_value_weight, outlier, sketch_sign_flags):
@@ -313,41 +346,47 @@
     )(jnp.concatenate([signs, signs], axis=2))
 
     head, place, plane = lax.axis_index("head"), lax.axis_index("seq"), lax.axis_index("batch")
-    xs, ys = around(place // RING, head), around(place % RING, head)
-    shard = lambda x, y: x * RING + y
-
-    def blocks_of(a, b, k):
-        return [
-            (a, jnp.stack([2 * shard(x, ys[k]) for x in xs]), 1),
-            (b, jnp.stack([2 * shard(xs[k], y) + 1 for y in ys]), 1),
-        ]
+    lists = {
+        "x": around(place // RING, head),
+        "y": around(place % RING, head),
+        "z": around(plane, head),
+    }
+    permuted = PART * len(ORDERS)
+
+    def block_of(part, w, k):
+        inner, outer, third = ORDERS[part]
+        index = []
+        for o in lists[outer]:
+            for i in lists[inner]:
+                at = {inner: i, outer: o, third: lists[third][k]}
+                index.append((at["x"] * RING + at["y"]) * RING + at["z"])
+        return part, w, jnp.stack(index)
 
     def multiply(total, arrivals):
-        name = "ab0" if total is None else "ab1"
-        return accumulate(name, hidden, total, [block for arrival in arrivals for block in blocks_of(*arrival)])
+        return accumulate("first" if total is None else "more", hidden, total, permuted, [block_of(*a) for a in arrivals])
 
     flat = key_value_weight.reshape(rows, cols)
     quarter = rows // RING
-    own = lax.dynamic_slice_in_dim(flat[:, PERMUTED:], plane * quarter, quarter, 0)
-    rest = lax.all_gather(own, ("batch", "seq"), axis=0).reshape(RING, seq, quarter, cols - PERMUTED)
-    a3, b3, ab, start = gather_blocks(flat[:, :PERMUTED], multiply, start)
-    rest, ab = lax.optimization_barrier((rest, ab))
-    cd = accumulate_all(hidden, rest)
-
-    last = blocks_of(a3, b3, 3)
+    own = lax.dynamic_slice_in_dim(flat, plane * quarter, quarter, 0)
+    rest = lax.all_gather(own[:, permuted:], ("batch", "seq"), axis=0).reshape(RING, seq, quarter, cols - permuted)
+    parts = [own[:, PART * i : PART * i + PART] for i in range(len(ORDERS))]
+    last, total, start, rest = gather_blocks(parts, ORDERS, multiply, start, rest)
+    rest = accumulate_all(hidden, rest)
+
+    last = [block_of(i, w, 3) for i, w in enumerate(last)]
     specs, index = block_specs(tokens, last)
-    keep = jnp.repeat((1 - outlier).astype(F32), kv_cols, axis=1)
+    keep = jnp.repeat(jnp.repeat((1 - outlier).astype(F32), kv_cols, axis=1), 8, axis=0)
     whole = lambda *shape: pl.BlockSpec(shape, lambda j, ix: (0,) * len(shape))
     high, low, gram = pl.pallas_call(
-        project_kernel,
+        functools.partial(project_kernel, [part for part, _, _ in last]),
         grid_spec=pltpu.PrefetchScalarGridSpec(
             num_scalar_prefetch=1,
             grid=(STEPS,),
             in_specs=specs
-            + [whole(tokens, t.shape[1]) for t in (ab, cd)]
-            + [whole(tokens, 1), whole(groups, cols)],
+            + [whole(tokens, t.shape[1]) for t in (total, rest)]
+            + [whole(tokens, 1), whole(8 * groups, cols)],
             out_specs=[whole(tokens, cols), whole(tokens, cols), whole(128 * pairs, 128)],
-            scratch_shapes=[pltpu.VMEM(ab.shape, F32)],
+            scratch_shapes=[pltpu.VMEM(total.shape, F32)],
         ),
         out_shape=[
             jax.ShapeDtypeStruct((tokens, cols), BF16),
@@ -357,7 +396,7 @@
         compiler_params=pltpu.CompilerParams(vmem_limit_bytes=VMEM_LIMIT, dimension_semantics=("arbitrary",)),
         name="project",
         cost_estimate=cost(tokens, last),
-    )(index, *block_operands(hidden, last), ab, cd, row_scale[:, None], keep)
+    )(index, *block_operands(hidden, last), total, rest, row_scale[:, None], keep)
 
     pieces = lax.all_to_all(gram, "seq", 0, 0, tiled=True)
     piece = jnp.sum(pieces.reshape(seq, 128 * pairs // seq, 128), axis=0)

time: 248 us -> 264 us (1.065)
  starting transfers between devices: 14.2 us -> 31.6 us
  Pallas kernels: 79.7 us -> 90 us
  waiting for transfers between devices: 97.1 us -> 88.1 us
  blocking collectives: 31.8 us -> 27.3 us
    ppermute x0 -> x7, waiting for transfers between devices: none -> 52.2 us  [send(): return lax.ppermute(v, ('batch', 'head'), depth_pairs(which))]
    ppermute x10 -> x14, waiting for transfers between devices: 80.2 us -> 35.9 us  [send(): return lax.ppermute(v, ('head', 'seq'), plane_pairs(axis, which))]
    all_gather x1, waiting for transfers between devices: 16.9 us -> 0.02 us  [shards(): lax.all_gather(own[:, permuted:], ('batch', 'seq'), axis=0)]
    ppermute x0 -> x7, starting transfers between devices: none -> 13.8 us  [send(): return lax.ppermute(v, ('batch', 'head'), depth_pairs(which))]
    pallas_call x4 -> x5, Pallas kernels: 56.3 us -> 66.6 us  [the longest x3 35.7 us: accumulate(): pl.pallas_call(functools.partial(accumulate_kernel, [part for part, _, _...]
    all_to_all x1, blocking collectives: 18 us -> 14 us  [shards(): pieces = lax.all_to_all(gram, 'seq', 0, 0, tiled=True)]
    ppermute x10 -> x14, starting transfers between devices: 14.1 us -> 17.7 us  [send(): return lax.ppermute(v, ('head', 'seq'), plane_pairs(axis, which))]
  transfers between devices with their start and end apart: 11 -> 22, of which waited for: 7 -> 16; matrix products, arithmetic and copies ran while one was open for 2% -> 3% of each run, Pallas kernels for 22% -> 23%
where the time goes in v1:
time: 264 us
  Pallas kernels  90 us (34%)
  waiting for transfers between devices  88.1 us (33%)
  starting transfers between devices  31.6 us (12%)
  blocking collectives  27.3 us (10%)
  between operations  14.4 us (5%)
  local copies, waits for them, and re-layouts  7.59 us (3%)
  other arithmetic  4.55 us (2%)
    ppermute x7, waiting for transfers between devices, send(): return lax.ppermute(v, ('batch', 'head'), depth_pairs(which))  52.2 us
    ppermute x14, waiting for transfers between devices, send(): return lax.ppermute(v, ('head', 'seq'), plane_pairs(axis, which))  35.9 us
    pallas_call x3, Pallas kernels, accumulate(): pl.pallas_call(functools.partial(accumulate_kernel, [part for part, _, _...  35.7 us
    ppermute x14, starting transfers between devices, send(): return lax.ppermute(v, ('head', 'seq'), plane_pairs(axis, which))  17.7 us
    pallas_call x1, Pallas kernels, shards(): pl.pallas_call(functools.partial(project_kernel, [part for part, _, _ in...  17.1 us
    all_to_all x1, blocking collectives, shards(): pieces = lax.all_to_all(gram, 'seq', 0, 0, tiled=True)  14 us
    pallas_call x1, Pallas kernels, accumulate_all(): pl.pallas_call(accumulate_all_kernel, grid=(seq // 2,), in_specs=[pl.Bloc...  13.8 us
    ppermute x7, starting transfers between devices, send(): return lax.ppermute(v, ('batch', 'head'), depth_pairs(which))  13.8 us
  transfers between devices with their start and end apart: 22, of which 16 were waited for; matrix products, arithmetic and copies ran while one was open for 3% of the time, Pallas kernels for 23%

profile of v1, /device:TPU:0, one launch (start us, length us, event | category | flops | bytes accessed | tf_op | source)
XLA Modules:
  0.0 263.5 jit_solution(2031589854284172804)
XLA Ops:
  7.2 0.0 all-gather.3.cloned.1.call-start
  7.2 2.1 copy.10
  9.3 0.7 fusion
  10.0 1.7 collective-permute-start
  11.7 1.6 collective-permute-start.1
  13.2 0.5 collective-permute-start.2
  13.8 1.3 collective-permute-done
  15.1 1.6 collective-permute-done.1
  16.6 1.6 collective-permute-done.2
  18.3 2.2 collective-permute-start.3
  20.4 2.2 collective-permute-start.4
  22.6 1.1 collective-permute-start.5
  23.8 2.2 collective-permute-done.3
  25.9 2.2 collective-permute-done.4
  28.2 2.6 collective-permute-done.5
  30.9 0.7 collective-permute-start.6
  31.6 2.0 collective-permute-start.7
  33.5 0.1 collective-permute-start.8
  33.6 6.9 %collective-permute-done.6 = f32[512,256]{1,0:T(8,128)S(1)} collective-permute-done((f32[512,256]{1,0:T(8,128)S(1)}, f32[512,256]{1,0:T(8,128)S(1)}, u32[]{:S(2)}, u32[]{:S(2)}) %collective-permute-start.6) | collective-permute-done | bytes 524320 | tf_op jit(solution)/shard_map/ppermute | solution.py:305
  40.5 0.5 collective-permute-done.7
  41.0 6.9 %collective-permute-done.8 = f32[512,256]{1,0:T(8,128)S(1)} collective-permute-done((f32[512,256]{1,0:T(8,128)S(1)}, f32[512,256]{1,0:T(8,128)S(1)}, u32[]{:S(2)}, u32[]{:S(2)}) %collective-permute-start.8) | collective-permute-done | bytes 524320 | tf_op jit(solution)/shard_map/ppermute | solution.py:304
  47.9 0.1 pad_maximum_fusion.3
  48.0 0.1 pad_maximum_fusion.4
  48.1 0.1 pad_maximum_fusion.5
  48.2 0.2 collective-permute-start.9
  48.4 4.7 %collective-permute-start.10 = (f32[1024,256]{1,0:T(8,128)S(1)}, f32[1024,256]{1,0:T(8,128)S(1)}, u32[]{:S(2)}, u32[]{:S(2)}) collective-permute-start(f32[1024,256]{1,0:T(8,128)S(1)} %pad_maximum_fusion.4), channel_id=1, source_target_pairs={{0,96},{16,48},{32,64},{48,16},{64,32},{80,112},{96,0},{112,80},{1... | collective-permute-start | bytes 3145736 | tf_op jit(solution)/shard_map/ppermute | solution.py:304
  53.1 14.0 %collective-permute-done.9 = f32[1024,256]{1,0:T(8,128)S(1)} collective-permute-done((f32[1024,256]{1,0:T(8,128)S(1)}, f32[1024,256]{1,0:T(8,128)S(1)}, u32[]{:S(2)}, u32[]{:S(2)}) %collective-permute-start.9) | collective-permute-done | bytes 1048608 | tf_op jit(solution)/shard_map/ppermute | solution.py:305
  67.1 0.6 collective-permute-done.10
  67.6 33.0 %collective-permute-done.11 = f32[1024,256]{1,0:T(8,128)S(1)} collective-permute-done((f32[1024,256]{1,0:T(8,128)S(1)}, f32[1024,256]{1,0:T(8,128)S(1)}, u32[]{:S(2)}, u32[]{:S(2)}) %collective-permute-start.11) | collective-permute-done | bytes 1048608 | tf_op jit(solution)/shard_map/ppermute | solution.py:304
  100.7 1.5 pad_maximum_fusion.refs_5_
  102.2 1.5 pad_maximum_fusion.1.refs_10_
  103.6 0.1 pad_maximum_fusion.2.refs_15_
  103.8 0.1 collective-permute-start.12
  103.9 0.1 collective-permute-start.13
  104.0 0.3 collective-permute-start.14
  104.4 0.2 copy-done.5
  104.6 0.2 copy.8
  104.8 0.7 concatenate.64.refs_0_
  105.5 1.0 pad_maximum_fusion.9.sign_ref
  106.5 11.2 %start.1.start_ref = f32[8,128,128]{2,1,0:T(8,128)} custom-call(f32[8,128,128]{2,1,0:T(8,128)} %pad_maximum_fusion.9.sign_ref), custom_call_target="tpu_custom_call" | custom-call | flops 100000000 | bytes 1000000 | tf_op jit(solution)/shard_map/start/pallas_call | solution.py:341
  117.7 11.5 %first.1.refs_16_ = f32[512,768]{1,0:T(8,128)} custom-call(s32[48]{0:T(128)} %concatenate.64.refs_0_, f32[512,8192]{1,0:T(8,128)} %refs_14_.7, f32[512,8192]{1,0:T(8,128)} %refs_14_.7, f32[512,8192]{1,0:T(8,128)} %refs_14_.7, f32[512,8192]{1,0:T(8,128)} %refs_14_.7, f32[2048,256]{1,0:T(8,128)} %pad_maximum_fusion.refs_5_, f32[512,8192]{1,0:T(8,128)} %refs_14_.7, ...), custom_call_target="tpu_custom_call" | custom-call | flops 4831838208 | bytes 18874368 | tf_op jit(solution)/shard_map/first/pallas_call | solution.py:113
  129.2 1.8 collective-permute-done.12.refs_5_
  131.0 0.2 collective-permute-done.13.refs_10_
  131.2 0.0 collective-permute-done.14.refs_15_
  131.3 6.9 %collective-permute-start.15 = (f32[2048,256]{1,0:T(8,128)}, f32[2048,256]{1,0:T(8,128)S(1)}, u32[]{:S(2)}, u32[]{:S(2)}) collective-permute-start(f32[2048,256]{1,0:T(8,128)} %pad_maximum_fusion.refs_5_), channel_id=1, source_target_pairs={{0,96},{16,48},{32,64},{48,16},{64,32},{80,112},{96,0},{112,80},{1... | collective-permute-start | bytes 6291464 | tf_op jit(solution)/shard_map/ppermute | solution.py:304
  138.2 2.0 collective-permute-start.17
  140.2 0.7 concatenate.66.refs_0_
  140.9 12.2 %more.2.refs_16_ = f32[512,768]{1,0:T(8,128)} custom-call(s32[48]{0:T(128)} %concatenate.66.refs_0_, f32[512,8192]{1,0:T(8,128)} %refs_14_.7, f32[512,8192]{1,0:T(8,128)} %refs_14_.7, f32[512,8192]{1,0:T(8,128)} %refs_14_.7, f32[512,8192]{1,0:T(8,128)} %refs_14_.7, f32[2048,256]{1,0:T(8,128)} %collective-permute-done.12.refs_5_, f32[512,8192]{1,0:T(8,128)} %refs_14_.7, ...), custom_call_target="tpu_custom_call" | custom-call | flops 4831838208 | bytes 18874368 | tf_op jit(solution)/shard_map/more/pallas_call | solution.py:113
  153.1 9.3 %collective-permute-done.15.refs_5_ = f32[2048,256]{1,0:T(8,128)S(1)} collective-permute-done((f32[2048,256]{1,0:T(8,128)}, f32[2048,256]{1,0:T(8,128)S(1)}, u32[]{:S(2)}, u32[]{:S(2)}) %collective-permute-start.15) | collective-permute-done | bytes 2097184 | tf_op jit(solution)/shard_map/ppermute | solution.py:304
  162.4 3.3 %collective-permute-done.16.refs_10_ = f32[2048,256]{1,0:T(8,128)} collective-permute-done((f32[2048,256]{1,0:T(8,128)}, f32[2048,256]{1,0:T(8,128)}, u32[]{:S(2)}, u32[]{:S(2)}) %collective-permute-start.16) | collective-permute-done | bytes 2097184 | tf_op jit(solution)/shard_map/ppermute | solution.py:305
  165.8 0.1 collective-permute-start.18
  165.8 3.2 %collective-permute-start.19 = (f32[2048,256]{1,0:T(8,128)}, f32[2048,256]{1,0:T(8,128)}, u32[]{:S(2)}, u32[]{:S(2)}) collective-permute-start(f32[2048,256]{1,0:T(8,128)} %collective-permute-done.13.refs_10_), channel_id=1, source_target_pairs={{0,12},{1,13},{2,14},{3,15},{4,8},{5,9},{6,10},{7,11},{8,4},{9,5},... | collective-permute-start | bytes 6291464 | tf_op jit(solution)/shard_map/ppermute | solution.py:305
  169.0 2.0 collective-permute-start.20
  171.0 0.7 concatenate.51.refs_0_
  171.7 0.7 concatenate.67.refs_0_
  172.3 0.9 copy.9.refs_18_
  173.2 0.1 broadcast_in_dim.13
  173.3 0.7 broadcast_bitcast_fusion.refs_19_
  174.0 12.1 %more.3.refs_16_ = f32[512,768]{1,0:T(8,128)} custom-call(s32[48]{0:T(128)} %concatenate.67.refs_0_, f32[512,8192]{1,0:T(8,128)} %refs_14_.7, f32[512,8192]{1,0:T(8,128)} %refs_14_.7, f32[512,8192]{1,0:T(8,128)} %refs_14_.7, f32[512,8192]{1,0:T(8,128)} %refs_14_.7, f32[2048,256]{1,0:T(8,128)} %copy-done.4, f32[512,8192]{1,0:T(8,128)} %refs_14_.7, ...), custom_call_target="tpu_custom_call" | custom-call | flops 4831838208 | bytes 18874368 | tf_op jit(solution)/shard_map/more/pallas_call | solution.py:113
  186.1 13.8 %rest.1.refs_17_ = f32[512,256]{1,0:T(8,128)} custom-call(f32[512,8192]{1,0:T(8,128)} %refs_14_.7, f32[4,16,128,256]{3,2,1,0:T(8,128)} %bitcast.75), custom_call_target="tpu_custom_call" | custom-call | flops 6442450944 | bytes 25165824 | tf_op jit(solution)/shard_map/rest/pallas_call | solution.py:142
  200.0 17.1 %project.1 = (bf16[512,1024]{1,0:T(8,128)(2,1)}, bf16[512,1024]{1,0:T(8,128)(2,1)}, f32[1024,128]{1,0:T(8,128)}) custom-call(s32[48]{0:T(128)} %concatenate.51.refs_0_, f32[512,8192]{1,0:T(8,128)} %refs_14_.7, f32[512,8192]{1,0:T(8,128)} %refs_14_.7, f32[512,8192]{1,0:T(8,128)} %refs_14_.7, f32[512,8192]{1,0:T(8,128)} %refs_14_.7, ...), custom_call_target="tpu_custom_call" | custom-call | flops 4831838208 | bytes 18874368 | tf_op jit(solution)/shard_map/project/pallas_call | solution.py:380
  217.0 14.0 %all_to_all.14 = f32[16,64,128]{2,1,0:T(8,128)S(1)} all-to-all(f32[16,64,128]{2,1,0:T(8,128)} %bitcast.79), channel_id=1, replica_groups=mesh['batch'=4,'head'=2,'seq'=16] {'seq'}, dimensions={0} | all-to-all | bytes 1048576 | tf_op jit(solution)/shard_map/all_to_all | solution.py:401
  231.1 13.3 %all_to_all.15 = f32[16,64,128]{2,1,0:T(8,128)S(1)} all-to-all(f32[16,64,128]{2,1,0:T(8,128)S(1)} %broadcast_in_dim.15), channel_id=1, replica_groups=mesh['batch'=4,'head'=2,'seq'=16] {'seq'}, dimensions={0} | all-to-all | bytes 1048576 | tf_op jit(solution)/shard_map/all_to_all | solution.py:403
  244.5 12.2 %factor.1 = (bf16[4,512,128]{2,1,0:T(8,128)(2,1)}, f32[4,128,128]{2,1,0:T(8,128)}) custom-call(f32[1024,128]{1,0:T(8,128)S(1)} %bitcast.74, f32[8,128,128]{2,1,0:T(8,128)S(1)} %copy-done, bf16[512,1024]{1,0:T(8,128)(2,1)S(1)} %copy-done.1, bf16[512,1024]{1,0:T(8,128)(2,1)S(1)} %copy-done.2), custom_call_target="tpu_custom_call" | custom-call | flops 1000000000 | bytes 4194304 | tf_op jit(solution)/shard_map/factor/pallas_call | solution.py:405
  (32 shorter events, 0.4 us)
Async XLA Ops:
  7.2 178.9 %all-gather.3.cloned.1.call-start = ((), (), s32[]{:S(2)}) async-start(), calls=%async_computation.2 | async-start | bytes 8519680 | tf_op jit(solution)/shard_map/all_gather | solution.py:371
  10.0 5.0 %collective-permute-start = (f32[128,256]{1,0:T(8,128)S(1)}, f32[128,256]{1,0:T(8,128)S(1)}, u32[]{:S(2)}, u32[]{:S(2)}) collective-permute-start(f32[128,256]{1,0:T(8,128)S(1)} %get-tuple-element.49), channel_id=1, source_target_pairs={{0,4},{1,5},{2,6},{3,7},{4,0},{5,1},{6,2},{7,3},{8,12},{9,13},{10,... | collective-permute-start | bytes 393224 | tf_op jit(solution)/shard_map/ppermute | solution.py:305
  11.7 5.0 %collective-permute-start.1 = (f32[128,256]{1,0:T(8,128)S(1)}, f32[128,256]{1,0:T(8,128)S(1)}, u32[]{:S(2)}, u32[]{:S(2)}) collective-permute-start(f32[128,256]{1,0:T(8,128)S(1)} %get-tuple-element.50), channel_id=1, source_target_pairs={{0,1},{1,0},{2,3},{3,2},{4,5},{5,4},{6,7},{7,6},{8,9},{9,8},{10,11... | collective-permute-start | bytes 393224 | tf_op jit(solution)/shard_map/ppermute | solution.py:305
  13.2 5.0 %collective-permute-start.2 = (f32[128,256]{1,0:T(8,128)S(1)}, f32[128,256]{1,0:T(8,128)S(1)}, u32[]{:S(2)}, u32[]{:S(2)}) collective-permute-start(f32[128,256]{1,0:T(8,128)S(1)} %get-tuple-element.51), channel_id=1, source_target_pairs={{0,4},{1,5},{2,6},{3,7},{4,0},{5,1},{6,2},{7,3},{8,12},{9,13},{10,... | collective-permute-start | bytes 393224 | tf_op jit(solution)/shard_map/ppermute | solution.py:305
  18.3 7.7 %collective-permute-start.3 = (f32[256,256]{1,0:T(8,128)S(1)}, f32[256,256]{1,0:T(8,128)S(1)}, u32[]{:S(2)}, u32[]{:S(2)}) collective-permute-start(f32[256,256]{1,0:T(8,128)S(1)} %get-tuple-element.55), channel_id=1, source_target_pairs={{0,12},{1,13},{2,14},{3,15},{4,8},{5,9},{6,10},{7,11},{8,4},{9,5},... | collective-permute-start | bytes 786440 | tf_op jit(solution)/shard_map/ppermute | solution.py:305
  20.4 7.7 %collective-permute-start.4 = (f32[256,256]{1,0:T(8,128)S(1)}, f32[256,256]{1,0:T(8,128)S(1)}, u32[]{:S(2)}, u32[]{:S(2)}) collective-permute-start(f32[256,256]{1,0:T(8,128)S(1)} %get-tuple-element.56), channel_id=1, source_target_pairs={{0,3},{1,2},{2,1},{3,0},{4,7},{5,6},{6,5},{7,4},{8,11},{9,10},{10,... | collective-permute-start | bytes 786440 | tf_op jit(solution)/shard_map/ppermute | solution.py:305
  22.6 8.1 %collective-permute-start.5 = (f32[256,256]{1,0:T(8,128)S(1)}, f32[256,256]{1,0:T(8,128)S(1)}, u32[]{:S(2)}, u32[]{:S(2)}) collective-permute-start(f32[256,256]{1,0:T(8,128)S(1)} %pad_maximum_fusion.12), channel_id=1, source_target_pairs={{0,12},{1,13},{2,14},{3,15},{4,8},{5,9},{6,10},{7,11},{8,4},{9,5},... | collective-permute-start | bytes 786440 | tf_op jit(solution)/shard_map/ppermute | solution.py:305
  30.9 9.7 %collective-permute-start.6 = (f32[512,256]{1,0:T(8,128)S(1)}, f32[512,256]{1,0:T(8,128)S(1)}, u32[]{:S(2)}, u32[]{:S(2)}) collective-permute-start(f32[512,256]{1,0:T(8,128)S(1)} %pad_maximum_fusion.6), channel_id=1, source_target_pairs={{0,1},{1,0},{2,3},{3,2},{4,5},{5,4},{6,7},{7,6},{8,9},{9,8},{10,11... | collective-permute-start | bytes 1572872 | tf_op jit(solution)/shard_map/ppermute | solution.py:305
  31.6 9.5 %collective-permute-start.7 = (f32[512,256]{1,0:T(8,128)S(1)}, f32[512,256]{1,0:T(8,128)S(1)}, u32[]{:S(2)}, u32[]{:S(2)}) collective-permute-start(f32[512,256]{1,0:T(8,128)S(1)} %pad_maximum_fusion.7), channel_id=1, source_target_pairs={{0,32},{16,112},{32,0},{48,80},{64,96},{80,48},{96,64},{112,16},{1... | collective-permute-start | bytes 1572872 | tf_op jit(solution)/shard_map/ppermute | solution.py:304
  33.5 14.4 %collective-permute-start.8 = (f32[512,256]{1,0:T(8,128)S(1)}, f32[512,256]{1,0:T(8,128)S(1)}, u32[]{:S(2)}, u32[]{:S(2)}) collective-permute-start(f32[512,256]{1,0:T(8,128)S(1)} %pad_maximum_fusion.8), channel_id=1, source_target_pairs={{0,32},{16,112},{32,0},{48,80},{64,96},{80,48},{96,64},{112,16},{1... | collective-permute-start | bytes 1572872 | tf_op jit(solution)/shard_map/ppermute | solution.py:304
  48.2 18.9 %collective-permute-start.9 = (f32[1024,256]{1,0:T(8,128)S(1)}, f32[1024,256]{1,0:T(8,128)S(1)}, u32[]{:S(2)}, u32[]{:S(2)}) collective-permute-start(f32[1024,256]{1,0:T(8,128)S(1)} %pad_maximum_fusion.3), channel_id=1, source_target_pairs={{0,3},{1,2},{2,1},{3,0},{4,7},{5,6},{6,5},{7,4},{8,11},{9,10},{10,... | collective-permute-start | bytes 3145736 | tf_op jit(solution)/shard_map/ppermute | solution.py:305
  48.4 19.2 %collective-permute-start.10 = (f32[1024,256]{1,0:T(8,128)S(1)}, f32[1024,256]{1,0:T(8,128)S(1)}, u32[]{:S(2)}, u32[]{:S(2)}) collective-permute-start(f32[1024,256]{1,0:T(8,128)S(1)} %pad_maximum_fusion.4), channel_id=1, source_target_pairs={{0,96},{16,48},{32,64},{48,16},{64,32},{80,112},{96,0},{112,80},{1... | collective-permute-start | bytes 3145736 | tf_op jit(solution)/shard_map/ppermute | solution.py:304
  53.0 47.6 %collective-permute-start.11 = (f32[1024,256]{1,0:T(8,128)S(1)}, f32[1024,256]{1,0:T(8,128)S(1)}, u32[]{:S(2)}, u32[]{:S(2)}) collective-permute-start(f32[1024,256]{1,0:T(8,128)S(1)} %pad_maximum_fusion.5), channel_id=1, source_target_pairs={{0,96},{16,48},{32,64},{48,16},{64,32},{80,112},{96,0},{112,80},{1... | collective-permute-start | bytes 3145736 | tf_op jit(solution)/shard_map/ppermute | solution.py:304
  103.6 0.9 copy-start.5
  103.8 13.9 %copy-start.3 = (f32[2048,256]{1,0:T(8,128)}, f32[2048,256]{1,0:T(8,128)S(1)}, u32[]{:S(2)}) copy-start(f32[2048,256]{1,0:T(8,128)S(1)} %pad_maximum_fusion.2.refs_15_) | copy-start | bytes 6291460
  103.8 27.3 %collective-permute-start.12 = (f32[2048,256]{1,0:T(8,128)}, f32[2048,256]{1,0:T(8,128)}, u32[]{:S(2)}, u32[]{:S(2)}) collective-permute-start(f32[2048,256]{1,0:T(8,128)} %pad_maximum_fusion.refs_5_), channel_id=1, source_target_pairs={{0,32},{16,112},{32,0},{48,80},{64,96},{80,48},{96,64},{112,16},{1... | collective-permute-start | bytes 6291464 | tf_op jit(solution)/shard_map/ppermute | solution.py:304
  103.9 27.3 %collective-permute-start.13 = (f32[2048,256]{1,0:T(8,128)}, f32[2048,256]{1,0:T(8,128)}, u32[]{:S(2)}, u32[]{:S(2)}) collective-permute-start(f32[2048,256]{1,0:T(8,128)} %pad_maximum_fusion.1.refs_10_), channel_id=1, source_target_pairs={{0,4},{1,5},{2,6},{3,7},{4,0},{5,1},{6,2},{7,3},{8,12},{9,13},{10,... | collective-permute-start | bytes 6291464 | tf_op jit(solution)/shard_map/ppermute | solution.py:305
  104.0 27.3 %collective-permute-start.14 = (f32[2048,256]{1,0:T(8,128)S(1)}, f32[2048,256]{1,0:T(8,128)}, u32[]{:S(2)}, u32[]{:S(2)}) collective-permute-start(f32[2048,256]{1,0:T(8,128)S(1)} %pad_maximum_fusion.2.refs_15_), channel_id=1, source_target_pairs={{0,1},{1,0},{2,3},{3,2},{4,5},{5,4},{6,7},{7,6},{8,9},{9,8},{10,11... | collective-permute-start | bytes 6291464 | tf_op jit(solution)/shard_map/ppermute | solution.py:305
  131.3 31.2 %collective-permute-start.15 = (f32[2048,256]{1,0:T(8,128)}, f32[2048,256]{1,0:T(8,128)S(1)}, u32[]{:S(2)}, u32[]{:S(2)}) collective-permute-start(f32[2048,256]{1,0:T(8,128)} %pad_maximum_fusion.refs_5_), channel_id=1, source_target_pairs={{0,96},{16,48},{32,64},{48,16},{64,32},{80,112},{96,0},{112,80},{1... | collective-permute-start | bytes 6291464 | tf_op jit(solution)/shard_map/ppermute | solution.py:304
  138.2 27.6 %collective-permute-start.16 = (f32[2048,256]{1,0:T(8,128)}, f32[2048,256]{1,0:T(8,128)}, u32[]{:S(2)}, u32[]{:S(2)}) collective-permute-start(f32[2048,256]{1,0:T(8,128)} %pad_maximum_fusion.1.refs_10_), channel_id=1, source_target_pairs={{0,12},{1,13},{2,14},{3,15},{4,8},{5,9},{6,10},{7,11},{8,4},{9,5},... | collective-permute-start | bytes 6291464 | tf_op jit(solution)/shard_map/ppermute | solution.py:305
  138.2 27.6 %collective-permute-start.17 = (f32[2048,256]{1,0:T(8,128)}, f32[2048,256]{1,0:T(8,128)}, u32[]{:S(2)}, u32[]{:S(2)}) collective-permute-start(f32[2048,256]{1,0:T(8,128)} %copy-done.3), channel_id=1, source_target_pairs={{0,3},{1,2},{2,1},{3,0},{4,7},{5,6},{6,5},{7,4},{8,11},{9,10},{10,... | collective-permute-start | bytes 6291464 | tf_op jit(solution)/shard_map/ppermute | solution.py:305
  140.9 31.4 %copy-start.6 = (f32[512]{0:T(512)S(1)}, f32[512]{0:T(512)}, u32[]{:S(2)}) copy-start(f32[512]{0:T(512)} %param.6) | copy-start | bytes 6148
  140.9 32.3 %copy-start.7 = (s32[8,4]{0,1:T(4,128)S(1)}, s32[8,4]{0,1:T(4,128)}, u32[]{:S(2)}) copy-start(s32[8,4]{0,1:T(4,128)} %param.8) | copy-start | bytes 388
  162.4 11.6 %copy-start.4 = (f32[2048,256]{1,0:T(8,128)}, f32[2048,256]{1,0:T(8,128)S(1)}, u32[]{:S(2)}) copy-start(f32[2048,256]{1,0:T(8,128)S(1)} %collective-permute-done.15.refs_5_) | copy-start | bytes 6291460
  165.8 34.2 %collective-permute-start.18 = (f32[2048,256]{1,0:T(8,128)}, f32[2048,256]{1,0:T(8,128)}, u32[]{:S(2)}, u32[]{:S(2)}) collective-permute-start(f32[2048,256]{1,0:T(8,128)} %collective-permute-done.12.refs_5_), channel_id=1, source_target_pairs={{0,96},{16,48},{32,64},{48,16},{64,32},{80,112},{96,0},{112,80},{1... | collective-permute-start | bytes 6291464 | tf_op jit(solution)/shard_map/ppermute | solution.py:304
  165.8 34.1 %collective-permute-start.19 = (f32[2048,256]{1,0:T(8,128)}, f32[2048,256]{1,0:T(8,128)}, u32[]{:S(2)}, u32[]{:S(2)}) collective-permute-start(f32[2048,256]{1,0:T(8,128)} %collective-permute-done.13.refs_10_), channel_id=1, source_target_pairs={{0,12},{1,13},{2,14},{3,15},{4,8},{5,9},{6,10},{7,11},{8,4},{9,5},... | collective-permute-start | bytes 6291464 | tf_op jit(solution)/shard_map/ppermute | solution.py:305
  169.0 30.9 %collective-permute-start.20 = (f32[2048,256]{1,0:T(8,128)}, f32[2048,256]{1,0:T(8,128)}, u32[]{:S(2)}, u32[]{:S(2)}) collective-permute-start(f32[2048,256]{1,0:T(8,128)} %collective-permute-done.14.refs_15_), channel_id=1, source_target_pairs={{0,3},{1,2},{2,1},{3,0},{4,7},{5,6},{6,5},{7,4},{8,11},{9,10},{10,... | collective-permute-start | bytes 6291464 | tf_op jit(solution)/shard_map/ppermute | solution.py:305
  217.0 27.5 %copy-start = (f32[8,128,128]{2,1,0:T(8,128)S(1)}, f32[8,128,128]{2,1,0:T(8,128)}, u32[]{:S(2)}) copy-start(f32[8,128,128]{2,1,0:T(8,128)} %start.1.start_ref) | copy-start | bytes 1572868
  217.0 27.5 %copy-start.1 = (bf16[512,1024]{1,0:T(8,128)(2,1)S(1)}, bf16[512,1024]{1,0:T(8,128)(2,1)}, u32[]{:S(2)}) copy-start(bf16[512,1024]{1,0:T(8,128)(2,1)} %get-tuple-element.94.high_ref) | copy-start | bytes 3145732
  217.0 27.5 %copy-start.2 = (bf16[512,1024]{1,0:T(8,128)(2,1)S(1)}, bf16[512,1024]{1,0:T(8,128)(2,1)}, u32[]{:S(2)}) copy-start(bf16[512,1024]{1,0:T(8,128)(2,1)} %get-tuple-element.95.low_ref) | copy-start | bytes 3145732
Sparse Core Ops, SparseCore 0:
  10.9 91.3 all-gather.2

commit v2 on v0

--- a/solution.py
+++ b/solution.py
@@ -13,6 +13,8 @@
 RING = 4
 STEPS = 4
 PERMUTED = 512
+WIDE = 256
+UNROLL = 4
 VMEM_LIMIT = 56 << 20
 F32 = jnp.float32
 BF16 = jnp.bfloat16
@@ -54,11 +56,8 @@
 
 
 def residual(kv, keep):
-    tokens, cols = kv.shape
-    grouped = kv.reshape(tokens // GROUP, GROUP, cols)
-    step = jnp.max(jnp.abs(grouped), axis=1, keepdims=True) / 7.0 + 1e-06
-    s = sine_of_cycles(grouped * (1.0 / step)) * keep[:, None, :]
-    return s.reshape(tokens, cols)
+    step = jnp.max(jnp.abs(kv), axis=0, keepdims=True) / 7.0 + 1e-06
+    return sine_of_cycles(kv * (1.0 / step)) * keep
 
 
 def accumulate_kernel(shapes, first, *refs):
@@ -128,8 +127,10 @@
     def _():
         out_ref[...] = jnp.zeros_like(out_ref)
 
-    rows = w_ref.shape[0] * w_ref.shape[2]
-    out_ref[...] += three_products(x_ref[...], w_ref[...].reshape(rows, w_ref.shape[3]))
+    batch, shards_in, quarter, cols = w_ref.shape
+    rows = batch * quarter
+    for s in range(shards_in):
+        out_ref[...] += three_products(x_ref[:, s * rows : s * rows + rows], w_ref[:, s].reshape(rows, cols))
 
 
 def accumulate_all(hidden, weight):
@@ -137,15 +138,15 @@
     batch, seq, quarter, cols = weight.shape
     return pl.pallas_call(
         accumulate_all_kernel,
-        grid=(seq,),
+        grid=(seq // 2,),
         in_specs=[
-            pl.BlockSpec((tokens, batch * quarter), lambda k: (0, k)),
-            pl.BlockSpec((batch, 1, quarter, cols), lambda k: (0, k, 0, 0)),
+            pl.BlockSpec((tokens, 2 * batch * quarter), lambda k: (0, k)),
+            pl.BlockSpec((batch, 2, quarter, cols), lambda k: (0, k, 0, 0)),
         ],
         out_specs=pl.BlockSpec((tokens, cols), lambda k: (0, 0)),
         out_shape=jax.ShapeDtypeStruct((tokens, cols), F32),
         compiler_params=pltpu.CompilerParams(vmem_limit_bytes=VMEM_LIMIT, dimension_semantics=("arbitrary",)),
-        name="cd",
+        name="rest",
         cost_estimate=pl.CostEstimate(
             flops=6 * tokens * weight.size, bytes_accessed=4 * (weight.size + hidden.size), transcendentals=0
         ),
@@ -163,23 +164,36 @@
 
     @pl.when(step == STEPS - 1)
     def _():
-        at = 0
-        for part in (ab_acc, cd_ref):
-            for p in range(part.shape[1] // 128):
-                cols = slice(at, at + 128)
-                r = residual(part[:, 128 * p : 128 * p + 128] * scale_ref[...], keep_ref[:, cols])
-                rh, rl = split(r)
-                high_ref[:, cols] = rh
-                low_ref[:, cols] = rl
+        epilogue(ab_acc, cd_ref, scale_ref, keep_ref, high_ref, low_ref, gram_ref)
+
+
+def epilogue(total_ref, rest_ref, scale_ref, keep_ref, high_ref, low_ref, gram_ref):
+    tokens = total_ref.shape[0]
+    at = 0
+    for part in (total_ref, rest_ref):
+        for first in range(0, part.shape[1], WIDE):
+            here = slice(at, at + WIDE)
+
+            @pl.loop(0, tokens // GROUP, unroll=UNROLL)
+            def _(g, part=part, first=first, here=here):
+                rows = pl.ds(pl.multiple_of(g * GROUP, GROUP), GROUP)
+                kv = part[rows, first : first + WIDE] * scale_ref[rows, :]
+                keep = keep_ref[pl.ds(pl.multiple_of(g * 8, 8), 8), here][:1]
+                rh, rl = split(residual(kv, keep))
+                high_ref[rows, here] = rh
+                low_ref[rows, here] = rl
+
+            for cols in [slice(c, c + 128) for c in range(at, at + WIDE, 128)]:
+                rh = high_ref[:, cols]
                 both = lax.dot_general(
                     rh,
-                    jnp.concatenate([rh, rl], axis=1),
+                    jnp.concatenate([rh, low_ref[:, cols]], axis=1),
                     (((0,), (0,)), ((), ())),
                     preferred_element_type=F32,
                 )
                 cross = both[:, 128:]
                 gram_ref[cols, :] = both[:, :128] + (cross + cross.T)
-                at += 128
+            at += WIDE
 
 
 def inverse_factors(grams):
@@ -286,12 +300,16 @@
         a, b = lax.optimization_barrier((a, b))
         a1, b1 = lax.optimization_barrier((send(a, "x", which), send(b, "y", which)))
         a, b = join(a, a1), join(b, b1)
-    a, b = lax.optimization_barrier((a, b))
-    a1, b1, a2, b2 = send(a, "y", 0), send(b, "x", 0), send(a, "y", 1), send(b, "x", 1)
-    total = multiply(None, [(a, b, 0)])
-    a1, b1, a2, b2, total, start = lax.optimization_barrier((a1, b1, a2, b2, total, start))
+    barrier = lax.optimization_barrier
+    a, b = barrier((a, b))
+    came = send(a, "y", 0), send(b, "x", 0)
+    total = multiply("ab0", None, (a, b, 0))
+    a1, b1, a, b, total, start = barrier((*came, a, b, total, start))
+    came = send(a, "y", 1), send(b, "x", 1)
+    total = multiply("ab1", total, (a1, b1, 1))
+    a2, b2, a1, b1, total = barrier((*came, a1, b1, total))
     a3, b3 = send(a1, "y", 1), send(b1, "x", 1)
-    total = multiply(total, [(a1, b1, 1), (a2, b2, 2)])
+    total = multiply("ab2", total, (a2, b2, 2))
     return a3, b3, total, start
 
 
@@ -322,9 +340,8 @@
             (b, jnp.stack([2 * shard(xs[k], y) + 1 for y in ys]), 1),
         ]
 
-    def multiply(total, arrivals):
-        name = "ab0" if total is None else "ab1"
-        return accumulate(name, hidden, total, [block for arrival in arrivals for block in blocks_of(*arrival)])
+    def multiply(name, total, arrival):
+        return accumulate(name, hidden, total, blocks_of(*arrival))
 
     flat = key_value_weight.reshape(rows, cols)
     quarter = rows // RING
@@ -336,7 +353,7 @@
 
     last = blocks_of(a3, b3, 3)
     specs, index = block_specs(tokens, last)
-    keep = jnp.repeat((1 - outlier).astype(F32), kv_cols, axis=1)
+    keep = jnp.repeat(jnp.repeat((1 - outlier).astype(F32), kv_cols, axis=1), 8, axis=0)
     whole = lambda *shape: pl.BlockSpec(shape, lambda j, ix: (0,) * len(shape))
     high, low, gram = pl.pallas_call(
         project_kernel,
@@ -345,7 +362,7 @@
             grid=(STEPS,),
             in_specs=specs
             + [whole(tokens, t.shape[1]) for t in (ab, cd)]
-            + [whole(tokens, 1), whole(groups, cols)],
+            + [whole(tokens, 1), whole(8 * groups, cols)],
             out_specs=[whole(tokens, cols), whole(tokens, cols), whole(128 * pairs, 128)],
             scratch_shapes=[pltpu.VMEM(ab.shape, F32)],
         ),

time: 248 us -> 246 us (level)
  waiting for transfers between devices: 97.1 us -> 94 us
    all_gather x1, waiting for transfers between devices: 16.9 us -> 0.01 us  [shards(): lax.all_gather(own, ('batch', 'seq'), axis=0)]
    ppermute x10, waiting for transfers between devices: 80.2 us -> 94 us  [send(): return lax.ppermute(v, ('head', 'seq'), plane_pairs(axis, which))]
    pallas_call x2 -> x3, Pallas kernels: 20.9 us -> 25.1 us  [accumulate(): pl.pallas_call(functools.partial(accumulate_kernel, [parts for _, _, part...]
    pallas_call x1, Pallas kernels: 23 us -> 19.2 us  [accumulate_all(): pl.pallas_call(accumulate_all_kernel, grid=(seq // 2,), in_specs=[pl.Bloc...]
  transfers between devices with their start and end apart: 11 -> 11, of which waited for: 7 -> 7; matrix products, arithmetic and copies ran while one was open for 2% -> 3% of each run, Pallas kernels for 22% -> 23%
where the time goes in v2:
time: 246 us; the launch traced here: 245 us
  waiting for transfers between devices  94 us (38%)
  Pallas kernels  81.5 us (33%)
  blocking collectives  32 us (13%)
  between operations  14.1 us (6%)
  starting transfers between devices  13.4 us (5%)
  local copies, waits for them, and re-layouts  7.47 us (3%)
  other arithmetic  2.97 us (1%)
    ppermute x10, waiting for transfers between devices, send(): return lax.ppermute(v, ('head', 'seq'), plane_pairs(axis, which))  94 us
    pallas_call x3, Pallas kernels, accumulate(): pl.pallas_call(functools.partial(accumulate_kernel, [parts for _, _, part...  25.1 us
    pallas_call x1, Pallas kernels, accumulate_all(): pl.pallas_call(accumulate_all_kernel, grid=(seq // 2,), in_specs=[pl.Bloc...  19.2 us
    all_to_all x1, blocking collectives, shards(): pieces = lax.all_to_all(gram, 'seq', 0, 0, tiled=True)  17.8 us
    all_to_all x1, blocking collectives, shards(): lax.all_to_all(jnp.broadcast_to(piece, (seq,) + piece.shape), 'seq', 0, 0)  14.1 us
    pallas_call x1, Pallas kernels, shards(): pl.pallas_call(project_kernel, grid_spec=pltpu.PrefetchScalarGridSpec(num...  13.7 us
    ppermute x10, starting transfers between devices, send(): return lax.ppermute(v, ('head', 'seq'), plane_pairs(axis, which))  13.4 us
    pallas_call x1, Pallas kernels, shards(): pl.pallas_call(functools.partial(factor_kernel, root_length), out_shape=[...  12.2 us
  transfers between devices with their start and end apart: 11, of which 7 were waited for; matrix products, arithmetic and copies ran while one was open for 3% of the time, Pallas kernels for 23%

profile of v2, /device:TPU:0, one launch (start us, length us, event | category | flops | bytes accessed | tf_op | source)
XLA Modules:
  0.0 245.5 jit_solution(11695700828889056684)
XLA Ops:
  7.2 0.0 all-gather.3.cloned.1.call-start
  7.2 2.1 copy.10
  9.3 0.1 slice.17
  9.4 0.7 constant_dynamic-slice_fusion
  10.1 0.0 all-gather.3.cloned.1.call-update
  10.1 0.1 fusion
  10.2 1.7 collective-permute-start
  11.9 1.6 collective-permute-start.1
  13.4 6.0 %collective-permute-done = f32[256,512]{1,0:T(8,128)S(1)} collective-permute-done((f32[256,512]{1,0:T(8,128)S(1)}, f32[256,512]{1,0:T(8,128)S(1)}, u32[]{:S(2)}, u32[]{:S(2)}) %collective-permute-start) | collective-permute-done | bytes 524320 | tf_op jit(solution)/shard_map/ppermute | solution.py:294
  19.5 1.6 collective-permute-done.1
  21.0 0.2 pad_maximum_fusion.2
  21.2 2.2 collective-permute-start.2
  23.4 3.0 %collective-permute-start.3 = (f32[512,512]{1,0:T(8,128)S(1)}, f32[512,512]{1,0:T(8,128)S(1)}, u32[]{:S(2)}, u32[]{:S(2)}) collective-permute-start(f32[512,512]{1,0:T(8,128)S(1)} %get-tuple-element.33), channel_id=1, source_target_pairs={{0,3},{1,2},{2,1},{3,0},{4,7},{5,6},{6,5},{7,4},{8,11},{9,10},{10,... | collective-permute-start | bytes 3145736 | tf_op jit(solution)/shard_map/ppermute | solution.py:294
  26.4 13.7 %collective-permute-done.2 = f32[512,512]{1,0:T(8,128)S(1)} collective-permute-done((f32[512,512]{1,0:T(8,128)S(1)}, f32[512,512]{1,0:T(8,128)S(1)}, u32[]{:S(2)}, u32[]{:S(2)}) %collective-permute-start.2) | collective-permute-done | bytes 1048608 | tf_op jit(solution)/shard_map/ppermute | solution.py:294
  40.1 2.1 collective-permute-done.3
  42.2 0.2 pad_maximum_fusion.1.refs_4_
  42.4 0.0 copy-start.3
  42.4 0.0 copy-start.5
  42.4 1.6 pad_maximum_fusion.refs_2_
  44.0 0.4 collective-permute-start.4
  44.3 0.6 collective-permute-start.5
  44.9 0.0 copy-done.5
  45.0 0.2 copy.8
  45.2 0.6 concatenate.32.refs_0_
  45.8 1.0 pad_maximum_fusion.4.sign_ref
  46.8 11.2 %start.1.start_ref = f32[8,128,128]{2,1,0:T(8,128)} custom-call(f32[8,128,128]{2,1,0:T(8,128)} %pad_maximum_fusion.4.sign_ref), custom_call_target="tpu_custom_call" | custom-call | flops 100000000 | bytes 1000000 | tf_op jit(solution)/shard_map/start/pallas_call | solution.py:326
  58.0 0.0 copy-done.3
  58.0 7.9 %ab0.1.refs_5_ = f32[512,512]{1,0:T(8,128)} custom-call(s32[8]{0:T(128)} %concatenate.32.refs_0_, f32[512,8192]{1,0:T(8,128)} %xb.1, f32[1024,512]{1,0:T(8,128)} %pad_maximum_fusion.refs_2_, f32[512,8192]{1,0:T(8,128)} %xb.1, f32[1024,512]{1,0:T(8,128)} %copy-done.3), custom_call_target="tpu_custom_call" | custom-call | flops 3221225472 | bytes 12582912 | tf_op jit(solution)/shard_map/ab0/pallas_call | solution.py:110
  65.9 26.4 %collective-permute-done.4.refs_2_ = f32[1024,512]{1,0:T(8,128)} collective-permute-done((f32[1024,512]{1,0:T(8,128)}, f32[1024,512]{1,0:T(8,128)}, u32[]{:S(2)}, u32[]{:S(2)}) %collective-permute-start.4) | collective-permute-done | bytes 2097184 | tf_op jit(solution)/shard_map/ppermute | solution.py:294
  92.3 0.0 collective-permute-done.5.refs_4_
  92.3 2.4 collective-permute-start.6
  94.7 0.0 collective-permute-start.7
  94.7 0.6 concatenate.34.refs_0_
  95.3 0.0 copy-start.6
  95.3 0.0 copy-start.7
  95.3 8.8 %ab1.1.refs_5_ = f32[512,512]{1,0:T(8,128)} custom-call(s32[8]{0:T(128)} %concatenate.34.refs_0_, f32[512,8192]{1,0:T(8,128)} %xb.1, f32[1024,512]{1,0:T(8,128)} %collective-permute-done.4.refs_2_, f32[512,8192]{1,0:T(8,128)} %xb.1, f32[1024,512]{1,0:T(8,128)} %collective-permute-done.5.refs_4_, f32[512,512]{1,0:T(8,128)} %ab0.1.refs_5_), custom_call_target="tpu_custom_call" | custom-call | flops 3221225472 | bytes 12582912 | tf_op jit(solution)/shard_map/ab1/pallas_call | solution.py:110
  104.1 41.9 %collective-permute-done.6.refs_2_ = f32[1024,512]{1,0:T(8,128)S(1)} collective-permute-done((f32[1024,512]{1,0:T(8,128)}, f32[1024,512]{1,0:T(8,128)S(1)}, u32[]{:S(2)}, u32[]{:S(2)}) %collective-permute-start.6) | collective-permute-done | bytes 2097184 | tf_op jit(solution)/shard_map/ppermute | solution.py:294
  146.0 0.0 copy-start.4
  146.0 2.3 collective-permute-done.7.refs_4_
  148.3 0.5 collective-permute-start.8
  148.8 1.1 collective-permute-start.9
  149.9 0.0 copy-done.6
  149.9 0.9 copy.9.scale_ref
  150.8 0.7 concatenate.35.refs_0_
  151.5 0.7 concatenate.27.index_ref
  152.2 0.0 copy-done.7
  152.2 0.1 broadcast_in_dim.13
  152.2 0.7 broadcast_bitcast_fusion.keep_ref
  153.0 0.0 copy-done.4
  153.0 8.4 %ab2.1.ab_ref = f32[512,512]{1,0:T(8,128)} custom-call(s32[8]{0:T(128)} %concatenate.35.refs_0_, f32[512,8192]{1,0:T(8,128)} %xb.1, f32[1024,512]{1,0:T(8,128)} %copy-done.4, f32[512,8192]{1,0:T(8,128)} %xb.1, f32[1024,512]{1,0:T(8,128)} %collective-permute-done.7.refs_4_, f32[512,512]{1,0:T(8,128)} %ab1.1.refs_5_), custom_call_target="tpu_custom_call" | custom-call | flops 3221225472 | bytes 12582912 | tf_op jit(solution)/shard_map/ab2/pallas_call | solution.py:110
  161.4 0.0 all-gather.3.cloned.1.call-done
  161.4 19.2 %rest.1.cd_ref = f32[512,512]{1,0:T(8,128)} custom-call(f32[512,8192]{1,0:T(8,128)} %xb.1, f32[4,16,128,512]{3,2,1,0:T(8,128)} %bitcast.50), custom_call_target="tpu_custom_call" | custom-call | flops 12884901888 | bytes 33554432 | tf_op jit(solution)/shard_map/rest/pallas_call | solution.py:139
  180.6 0.0 collective-permute-done.8.wa
  180.6 0.0 collective-permute-done.9.wb
  180.6 13.7 %project.1 = (bf16[512,1024]{1,0:T(8,128)(2,1)}, bf16[512,1024]{1,0:T(8,128)(2,1)}, f32[1024,128]{1,0:T(8,128)}) custom-call(s32[8]{0:T(128)} %concatenate.27.index_ref, f32[512,8192]{1,0:T(8,128)} %xb.1, f32[1024,512]{1,0:T(8,128)} %collective-permute-done.8.wa, f32[512,8192]{1,0:T(8,128)} %xb.1, f32[1024,512]{1,0:T(8,128)} %collective-permute-done.9.wb, ...), custom_call_target="tpu_custom_call" | custom-call | flops 3221225472 | bytes 12582912 | tf_op jit(solution)/shard_map/project/pallas_call | solution.py:358
  194.3 0.0 copy-start
  194.3 0.0 copy-start.1
  194.3 0.0 copy-start.2
  194.4 17.8 %all_to_all.14 = f32[16,64,128]{2,1,0:T(8,128)S(1)} all-to-all(f32[16,64,128]{2,1,0:T(8,128)} %bitcast.47), channel_id=1, replica_groups=mesh['batch'=4,'head'=2,'seq'=16] {'seq'}, dimensions={0} | all-to-all | bytes 1048576 | tf_op jit(solution)/shard_map/all_to_all | solution.py:379
  212.3 14.1 %all_to_all.15 = f32[16,64,128]{2,1,0:T(8,128)S(1)} all-to-all(f32[16,64,128]{2,1,0:T(8,128)S(1)} %broadcast_in_dim.15), channel_id=1, replica_groups=mesh['batch'=4,'head'=2,'seq'=16] {'seq'}, dimensions={0} | all-to-all | bytes 1048576 | tf_op jit(solution)/shard_map/all_to_all | solution.py:381
  226.4 0.0 copy-done
  226.4 0.0 copy-done.1
  226.4 0.0 copy-done.2
  226.4 12.2 %factor.1 = (bf16[4,512,128]{2,1,0:T(8,128)(2,1)}, f32[4,128,128]{2,1,0:T(8,128)}) custom-call(f32[1024,128]{1,0:T(8,128)S(1)} %bitcast.42, f32[8,128,128]{2,1,0:T(8,128)S(1)} %copy-done, bf16[512,1024]{1,0:T(8,128)(2,1)S(1)} %copy-done.1, bf16[512,1024]{1,0:T(8,128)(2,1)S(1)} %copy-done.2), custom_call_target="tpu_custom_call" | custom-call | flops 1000000000 | bytes 4194304 | tf_op jit(solution)/shard_map/factor/pallas_call | solution.py:383
  (4 shorter events, 0.1 us)
Async XLA Ops:
  7.2 154.2 %all-gather.3.cloned.1.call-start = ((), (), s32[]{:S(2)}) async-start(), calls=%async_computation.2 | async-start | bytes 17039360 | tf_op jit(solution)/shard_map/all_gather | solution.py:349
  10.2 9.3 %collective-permute-start = (f32[256,512]{1,0:T(8,128)S(1)}, f32[256,512]{1,0:T(8,128)S(1)}, u32[]{:S(2)}, u32[]{:S(2)}) collective-permute-start(f32[256,512]{1,0:T(8,128)S(1)} %get-tuple-element.28), channel_id=1, source_target_pairs={{0,4},{1,5},{2,6},{3,7},{4,0},{5,1},{6,2},{7,3},{8,12},{9,13},{10,... | collective-permute-start | bytes 1572872 | tf_op jit(solution)/shard_map/ppermute | solution.py:294
  11.9 9.2 %collective-permute-start.1 = (f32[256,512]{1,0:T(8,128)S(1)}, f32[256,512]{1,0:T(8,128)S(1)}, u32[]{:S(2)}, u32[]{:S(2)}) collective-permute-start(f32[256,512]{1,0:T(8,128)S(1)} %get-tuple-element.29), channel_id=1, source_target_pairs={{0,1},{1,0},{2,3},{3,2},{4,5},{5,4},{6,7},{7,6},{8,9},{9,8},{10,11... | collective-permute-start | bytes 1572872 | tf_op jit(solution)/shard_map/ppermute | solution.py:294
  21.2 18.9 %collective-permute-start.2 = (f32[512,512]{1,0:T(8,128)S(1)}, f32[512,512]{1,0:T(8,128)S(1)}, u32[]{:S(2)}, u32[]{:S(2)}) collective-permute-start(f32[512,512]{1,0:T(8,128)S(1)} %get-tuple-element.32), channel_id=1, source_target_pairs={{0,12},{1,13},{2,14},{3,15},{4,8},{5,9},{6,10},{7,11},{8,4},{9,5},... | collective-permute-start | bytes 3145736 | tf_op jit(solution)/shard_map/ppermute | solution.py:294
  23.4 18.8 %collective-permute-start.3 = (f32[512,512]{1,0:T(8,128)S(1)}, f32[512,512]{1,0:T(8,128)S(1)}, u32[]{:S(2)}, u32[]{:S(2)}) collective-permute-start(f32[512,512]{1,0:T(8,128)S(1)} %get-tuple-element.33), channel_id=1, source_target_pairs={{0,3},{1,2},{2,1},{3,0},{4,7},{5,6},{6,5},{7,4},{8,11},{9,10},{10,... | collective-permute-start | bytes 3145736 | tf_op jit(solution)/shard_map/ppermute | solution.py:294
  42.4 15.6 %copy-start.3 = (f32[1024,512]{1,0:T(8,128)}, f32[1024,512]{1,0:T(8,128)S(1)}, u32[]{:S(2)}) copy-start(f32[1024,512]{1,0:T(8,128)S(1)} %pad_maximum_fusion.1.refs_4_) | copy-start | bytes 6291460
  42.4 2.5 %copy-start.5 = (s32[4,2,128,64]{2,3,1,0:T(8,128)S(1)}, s32[4,2,128,64]{2,3,1,0:T(8,128)}, u32[]{:S(2)}) copy-start(s32[4,2,128,64]{2,3,1,0:T(8,128)} %param.9) | copy-start | bytes 786436
  44.0 48.3 %collective-permute-start.4 = (f32[1024,512]{1,0:T(8,128)}, f32[1024,512]{1,0:T(8,128)}, u32[]{:S(2)}, u32[]{:S(2)}) collective-permute-start(f32[1024,512]{1,0:T(8,128)} %pad_maximum_fusion.refs_2_), channel_id=1, source_target_pairs={{0,1},{1,0},{2,3},{3,2},{4,5},{5,4},{6,7},{7,6},{8,9},{9,8},{10,11... | collective-permute-start | bytes 6291464 | tf_op jit(solution)/shard_map/ppermute | solution.py:294
  44.3 48.0 %collective-permute-start.5 = (f32[1024,512]{1,0:T(8,128)S(1)}, f32[1024,512]{1,0:T(8,128)}, u32[]{:S(2)}, u32[]{:S(2)}) collective-permute-start(f32[1024,512]{1,0:T(8,128)S(1)} %pad_maximum_fusion.1.refs_4_), channel_id=1, source_target_pairs={{0,4},{1,5},{2,6},{3,7},{4,0},{5,1},{6,2},{7,3},{8,12},{9,13},{10,... | collective-permute-start | bytes 6291464 | tf_op jit(solution)/shard_map/ppermute | solution.py:294
  92.3 53.7 %collective-permute-start.6 = (f32[1024,512]{1,0:T(8,128)}, f32[1024,512]{1,0:T(8,128)S(1)}, u32[]{:S(2)}, u32[]{:S(2)}) collective-permute-start(f32[1024,512]{1,0:T(8,128)} %pad_maximum_fusion.refs_2_), channel_id=1, source_target_pairs={{0,3},{1,2},{2,1},{3,0},{4,7},{5,6},{6,5},{7,4},{8,11},{9,10},{10,... | collective-permute-start | bytes 6291464 | tf_op jit(solution)/shard_map/ppermute | solution.py:294
  94.7 53.6 %collective-permute-start.7 = (f32[1024,512]{1,0:T(8,128)}, f32[1024,512]{1,0:T(8,128)}, u32[]{:S(2)}, u32[]{:S(2)}) collective-permute-start(f32[1024,512]{1,0:T(8,128)} %copy-done.3), channel_id=1, source_target_pairs={{0,12},{1,13},{2,14},{3,15},{4,8},{5,9},{6,10},{7,11},{8,4},{9,5},... | collective-permute-start | bytes 6291464 | tf_op jit(solution)/shard_map/ppermute | solution.py:294
  95.3 54.6 %copy-start.6 = (f32[512]{0:T(512)S(1)}, f32[512]{0:T(512)}, u32[]{:S(2)}) copy-start(f32[512]{0:T(512)} %param.6) | copy-start | bytes 6148
  95.3 56.8 %copy-start.7 = (s32[8,4]{0,1:T(4,128)S(1)}, s32[8,4]{0,1:T(4,128)}, u32[]{:S(2)}) copy-start(s32[8,4]{0,1:T(4,128)} %param.8) | copy-start | bytes 388
  146.0 7.0 %copy-start.4 = (f32[1024,512]{1,0:T(8,128)}, f32[1024,512]{1,0:T(8,128)S(1)}, u32[]{:S(2)}) copy-start(f32[1024,512]{1,0:T(8,128)S(1)} %collective-permute-done.6.refs_2_) | copy-start | bytes 6291460
  148.3 32.3 %collective-permute-start.8 = (f32[1024,512]{1,0:T(8,128)}, f32[1024,512]{1,0:T(8,128)}, u32[]{:S(2)}, u32[]{:S(2)}) collective-permute-start(f32[1024,512]{1,0:T(8,128)} %collective-permute-done.4.refs_2_), channel_id=1, source_target_pairs={{0,3},{1,2},{2,1},{3,0},{4,7},{5,6},{6,5},{7,4},{8,11},{9,10},{10,... | collective-permute-start | bytes 6291464 | tf_op jit(solution)/shard_map/ppermute | solution.py:294
  148.8 31.8 %collective-permute-start.9 = (f32[1024,512]{1,0:T(8,128)}, f32[1024,512]{1,0:T(8,128)}, u32[]{:S(2)}, u32[]{:S(2)}) collective-permute-start(f32[1024,512]{1,0:T(8,128)} %collective-permute-done.5.refs_4_), channel_id=1, source_target_pairs={{0,12},{1,13},{2,14},{3,15},{4,8},{5,9},{6,10},{7,11},{8,4},{9,5},... | collective-permute-start | bytes 6291464 | tf_op jit(solution)/shard_map/ppermute | solution.py:294
  194.3 32.1 %copy-start = (f32[8,128,128]{2,1,0:T(8,128)S(1)}, f32[8,128,128]{2,1,0:T(8,128)}, u32[]{:S(2)}) copy-start(f32[8,128,128]{2,1,0:T(8,128)} %start.1.start_ref) | copy-start | bytes 1572868
  194.3 32.1 %copy-start.1 = (bf16[512,1024]{1,0:T(8,128)(2,1)S(1)}, bf16[512,1024]{1,0:T(8,128)(2,1)}, u32[]{:S(2)}) copy-start(bf16[512,1024]{1,0:T(8,128)(2,1)} %get-tuple-element.52.high_ref) | copy-start | bytes 3145732
  194.3 32.1 %copy-start.2 = (bf16[512,1024]{1,0:T(8,128)(2,1)S(1)}, bf16[512,1024]{1,0:T(8,128)(2,1)}, u32[]{:S(2)}) copy-start(bf16[512,1024]{1,0:T(8,128)(2,1)} %get-tuple-element.53.low_ref) | copy-start | bytes 3145732
Sparse Core Ops, SparseCore 0:
  11.5 132.8 all-gather.2

commit v3 on v2

--- a/solution.py
+++ b/solution.py
@@ -13,6 +13,7 @@
 RING = 4
 STEPS = 4
 PERMUTED = 512
+DEEP = 256
 WIDE = 256
 UNROLL = 4
 VMEM_LIMIT = 56 << 20
@@ -153,24 +154,27 @@
     )(hidden, weight)
 
 
-def project_kernel(index_ref, xa, wa, xb, wb, ab_ref, cd_ref, scale_ref, keep_ref, high_ref, low_ref, gram_ref, ab_acc):
+def project_kernel(index_ref, xa, wa, xb, wb, xc0, xc1, xc2, xc3, wc, ab_ref, c_ref, rest_ref, scale_ref, keep_ref,
+                   high_ref, low_ref, gram_ref, ab_acc, c_acc):
     step = pl.program_id(0)
 
     @pl.when(step == 0)
     def _():
         ab_acc[...] = ab_ref[...]
+        c_acc[...] = c_ref[...]
 
     ab_acc[...] += three_products(xa[...], wa[...]) + three_products(xb[...], wb[...])
+    c_acc[...] += three_products(jnp.concatenate([xc0[...], xc1[...], xc2[...], xc3[...]], axis=1), wc[...])
 
     @pl.when(step == STEPS - 1)
     def _():
-        epilogue(ab_acc, cd_ref, scale_ref, keep_ref, high_ref, low_ref, gram_ref)
-
-
-def epilogue(total_ref, rest_ref, scale_ref, keep_ref, high_ref, low_ref, gram_ref):
-    tokens = total_ref.shape[0]
+        epilogue((ab_acc, c_acc, rest_ref), scale_ref, keep_ref, high_ref, low_ref, gram_ref)
+
+
+def epilogue(parts, scale_ref, keep_ref, high_ref, low_ref, gram_ref):
+    tokens = scale_ref.shape[0]
     at = 0
-    for part in (total_ref, rest_ref):
+    for part in parts:
         for first in range(0, part.shape[1], WIDE):
             here = slice(at, at + WIDE)
 
@@ -289,28 +293,37 @@
     return pairs
 
 
-def gather_blocks(weight, multiply, start):
-    def send(v, axis, which):
-        return lax.ppermute(v, ("head", "seq"), plane_pairs(axis, which))
-
+def depth_pairs(which):
+    return [(z * 2 + h, flat_partner(z, h, which) * 2 + h) for z in range(RING) for h in range(2)]
+
+
+def send(v, axis, which):
+    if axis == "z":
+        return lax.ppermute(v, ("batch", "head"), depth_pairs(which))
+    return lax.ppermute(v, ("head", "seq"), plane_pairs(axis, which))
+
+
+def gather_blocks(weight, deep, multiply, start):
+    barrier = lax.optimization_barrier
     join = lambda a, b: jnp.concatenate([a, b], axis=0)
     half = weight.shape[0] // 2
     a, b = weight[:half], weight[half:]
     for which in range(2):
-        a, b = lax.optimization_barrier((a, b))
-        a1, b1 = lax.optimization_barrier((send(a, "x", which), send(b, "y", which)))
+        a, b = barrier((a, b))
+        a1, b1 = barrier((send(a, "x", which), send(b, "y", which)))
         a, b = join(a, a1), join(b, b1)
-    barrier = lax.optimization_barrier
-    a, b = barrier((a, b))
-    came = send(a, "y", 0), send(b, "x", 0)
-    total = multiply("ab0", None, (a, b, 0))
-    a1, b1, a, b, total, start = barrier((*came, a, b, total, start))
-    came = send(a, "y", 1), send(b, "x", 1)
-    total = multiply("ab1", total, (a1, b1, 1))
-    a2, b2, a1, b1, total = barrier((*came, a1, b1, total))
-    a3, b3 = send(a1, "y", 1), send(b1, "x", 1)
-    total = multiply("ab2", total, (a2, b2, 2))
-    return a3, b3, total, start
+    a, b, c = own = barrier((a, b, deep))
+    came = send(a, "y", 0), send(b, "x", 0), send(c, "z", 0)
+    totals = multiply("0", None, own, 0)
+    came, own, totals, start = barrier((came, own, totals, start))
+    a, b, c = own
+    later = send(a, "y", 1), send(b, "x", 1), send(c, "z", 1)
+    totals = multiply("1", totals, came, 1)
+    later, came, totals = barrier((later, came, totals))
+    a, b, c = came
+    last = send(a, "y", 1), send(b, "x", 1), send(c, "z", 1)
+    totals = multiply("2", totals, later, 2)
+    return last, totals, start
 
 
 def shards(hidden, row_scale, key_value_weight, outlier, sketch_sign_flags):
@@ -331,27 +344,38 @@
     )(jnp.concatenate([signs, signs], axis=2))
 
     head, place, plane = lax.axis_index("head"), lax.axis_index("seq"), lax.axis_index("batch")
-    xs, ys = around(place // RING, head), around(place % RING, head)
+    xs, ys, zs = around(place // RING, head), around(place % RING, head), around(plane, head)
     shard = lambda x, y: x * RING + y
 
-    def blocks_of(a, b, k):
+    def plane_blocks(a, b, k):
         return [
             (a, jnp.stack([2 * shard(x, ys[k]) for x in xs]), 1),
             (b, jnp.stack([2 * shard(xs[k], y) + 1 for y in ys]), 1),
         ]
 
-    def multiply(name, total, arrival):
-        return accumulate(name, hidden, total, blocks_of(*arrival))
+    def deep_block(c, k):
+        return (c, jnp.arange(seq, dtype=jnp.int32) * RING + zs[k], RING)
+
+    def multiply(name, totals, arrival, k):
+        a, b, c = arrival
+        ab_total, c_total = totals or (None, None)
+        return (
+            accumulate("ab" + name, hidden, ab_total, plane_blocks(a, b, k)),
+            accumulate("c" + name, hidden, c_total, [deep_block(c, k)]),
+        )
 
     flat = key_value_weight.reshape(rows, cols)
     quarter = rows // RING
+    rest_at = PERMUTED + DEEP
     own = lax.dynamic_slice_in_dim(flat[:, PERMUTED:], plane * quarter, quarter, 0)
-    rest = lax.all_gather(own, ("batch", "seq"), axis=0).reshape(RING, seq, quarter, cols - PERMUTED)
-    a3, b3, ab, start = gather_blocks(flat[:, :PERMUTED], multiply, start)
-    rest, ab = lax.optimization_barrier((rest, ab))
+    deep = lax.all_gather(own[:, :DEEP], "seq", axis=0, tiled=True)
+    own, _ = lax.optimization_barrier((own[:, DEEP:], own))
+    rest = lax.all_gather(own, ("batch", "seq"), axis=0).reshape(RING, seq, quarter, cols - rest_at)
+    (a3, b3, c3), (ab, c), start = gather_blocks(flat[:, :PERMUTED], deep, multiply, start)
+    rest, ab, c = lax.optimization_barrier((rest, ab, c))
     cd = accumulate_all(hidden, rest)
 
-    last = blocks_of(a3, b3, 3)
+    last = plane_blocks(a3, b3, 3) + [deep_block(c3, 3)]
     specs, index = block_specs(tokens, last)
     keep = jnp.repeat(jnp.repeat((1 - outlier).astype(F32), kv_cols, axis=1), 8, axis=0)
     whole = lambda *shape: pl.BlockSpec(shape, lambda j, ix: (0,) * len(shape))
@@ -361,10 +385,10 @@
             num_scalar_prefetch=1,
             grid=(STEPS,),
             in_specs=specs
-            + [whole(tokens, t.shape[1]) for t in (ab, cd)]
+            + [whole(tokens, t.shape[1]) for t in (ab, c, cd)]
             + [whole(tokens, 1), whole(8 * groups, cols)],
             out_specs=[whole(tokens, cols), whole(tokens, cols), whole(128 * pairs, 128)],
-            scratch_shapes=[pltpu.VMEM(ab.shape, F32)],
+            scratch_shapes=[pltpu.VMEM(ab.shape, F32), pltpu.VMEM(c.shape, F32)],
         ),
         out_shape=[
             jax.ShapeDtypeStruct((tokens, cols), BF16),
@@ -374,7 +398,7 @@
         compiler_params=pltpu.CompilerParams(vmem_limit_bytes=VMEM_LIMIT, dimension_semantics=("arbitrary",)),
         name="project",
         cost_estimate=cost(tokens, last),
-    )(index, *block_operands(hidden, last), ab, cd, row_scale[:, None], keep)
+    )(index, *block_operands(hidden, last), ab, c, cd, row_scale[:, None], keep)
 
     pieces = lax.all_to_all(gram, "seq", 0, 0, tiled=True)
     piece = jnp.sum(pieces.reshape(seq, 128 * pairs // seq, 128), axis=0)

time: 246 us -> 247 us (level)
  waiting for transfers between devices: 94 us -> 66 us
  Pallas kernels: 81.5 us -> 97.8 us
  starting transfers between devices: 13.4 us -> 21.2 us
    ppermute x10, waiting for transfers between devices: 94 us -> 44 us  [send(): return lax.ppermute(v, ('head', 'seq'), plane_pairs(axis, which))]
    pallas_call x3 -> x6, Pallas kernels: 25.1 us -> 44.4 us  [accumulate(): pl.pallas_call(functools.partial(accumulate_kernel, [parts for _, _, part...]
    all_gather x0 -> x1, waiting for transfers between devices: none -> 15.1 us  [shards(): deep = lax.all_gather(own[:, :DEEP], 'seq', axis=0, tiled=True)]
    ppermute x0 -> x3, starting transfers between devices: none -> 7.4 us  [send(): return lax.ppermute(v, ('batch', 'head'), depth_pairs(which))]
    ppermute x0 -> x3, waiting for transfers between devices: none -> 6.09 us  [send(): return lax.ppermute(v, ('batch', 'head'), depth_pairs(which))]
    pallas_call x1, Pallas kernels: 19.2 us -> 13.8 us  [accumulate_all(): pl.pallas_call(accumulate_all_kernel, grid=(seq // 2,), in_specs=[pl.Bloc...]
    all_to_all x1, blocking collectives: 17.8 us -> 20.3 us  [shards(): pieces = lax.all_to_all(gram, 'seq', 0, 0, tiled=True)]
    pallas_call x1, Pallas kernels: 13.7 us -> 16.2 us  [shards(): pl.pallas_call(project_kernel, grid_spec=pltpu.PrefetchScalarGridSpec(num...]
  transfers between devices with their start and end apart: 11 -> 15, of which waited for: 7 -> 8; matrix products, arithmetic and copies ran while one was open for 3% -> 4% of each run, Pallas kernels for 23% -> 28%
where the time goes in v3:
time: 247 us; the launch traced here: 246 us
  Pallas kernels  97.8 us (40%)
  waiting for transfers between devices  66 us (27%)
  blocking collectives  33.8 us (14%)
  starting transfers between devices  21.2 us (9%)
  between operations  14.2 us (6%)
  local copies, waits for them, and re-layouts  8.79 us (4%)
  other arithmetic  4.63 us (2%)
    pallas_call x6, Pallas kernels, accumulate(): pl.pallas_call(functools.partial(accumulate_kernel, [parts for _, _, part...  44.4 us
    ppermute x10, waiting for transfers between devices, send(): return lax.ppermute(v, ('head', 'seq'), plane_pairs(axis, which))  44 us
    all_to_all x1, blocking collectives, shards(): pieces = lax.all_to_all(gram, 'seq', 0, 0, tiled=True)  20.3 us
    pallas_call x1, Pallas kernels, shards(): pl.pallas_call(project_kernel, grid_spec=pltpu.PrefetchScalarGridSpec(num...  16.2 us
    all_gather x1, waiting for transfers between devices, shards(): deep = lax.all_gather(own[:, :DEEP], 'seq', axis=0, tiled=True)  15.1 us
    pallas_call x1, Pallas kernels, accumulate_all(): pl.pallas_call(accumulate_all_kernel, grid=(seq // 2,), in_specs=[pl.Bloc...  13.8 us
    ppermute x10, starting transfers between devices, send(): return lax.ppermute(v, ('head', 'seq'), plane_pairs(axis, which))  13.7 us
    all_to_all x1, blocking collectives, shards(): lax.all_to_all(jnp.broadcast_to(piece, (seq,) + piece.shape), 'seq', 0, 0)  13.4 us
  transfers between devices with their start and end apart: 15, of which 8 were waited for; matrix products, arithmetic and copies ran while one was open for 4% of the time, Pallas kernels for 28%

profile of v3, /device:TPU:0, one launch (start us, length us, event | category | flops | bytes accessed | tf_op | source)
XLA Modules:
  0.0 246.4 jit_solution(5677052397635547724)
XLA Ops:
  7.2 0.0 all-gather.4.cloned.1.call-start
  7.2 2.1 copy.10
  9.3 0.1 slice.25
  9.4 0.7 fusion.5
  10.1 0.0 all-gather.4.cloned.1.call-update
  10.1 0.0 all-gather.6.cloned.1.call-start
  10.2 0.7 all-gather.6.cloned.1.call-update
  10.9 0.1 fusion.4
  11.0 1.7 collective-permute-start
  12.6 1.6 collective-permute-start.1
  14.2 6.0 %collective-permute-done = f32[256,512]{1,0:T(8,128)S(1)} collective-permute-done((f32[256,512]{1,0:T(8,128)S(1)}, f32[256,512]{1,0:T(8,128)S(1)}, u32[]{:S(2)}, u32[]{:S(2)}) %collective-permute-start) | collective-permute-done | bytes 524320 | tf_op jit(solution)/shard_map/ppermute | solution.py:303
  20.2 1.6 collective-permute-done.1
  21.8 0.2 pad_maximum_fusion.2
  22.0 2.2 collective-permute-start.2
  24.1 3.0 %collective-permute-start.3 = (f32[512,512]{1,0:T(8,128)S(1)}, f32[512,512]{1,0:T(8,128)S(1)}, u32[]{:S(2)}, u32[]{:S(2)}) collective-permute-start(f32[512,512]{1,0:T(8,128)S(1)} %get-tuple-element.42), channel_id=1, source_target_pairs={{0,3},{1,2},{2,1},{3,0},{4,7},{5,6},{6,5},{7,4},{8,11},{9,10},{10,... | collective-permute-start | bytes 3145736 | tf_op jit(solution)/shard_map/ppermute | solution.py:303
  27.2 13.0 %collective-permute-done.2 = f32[512,512]{1,0:T(8,128)S(1)} collective-permute-done((f32[512,512]{1,0:T(8,128)S(1)}, f32[512,512]{1,0:T(8,128)S(1)}, u32[]{:S(2)}, u32[]{:S(2)}) %collective-permute-start.2) | collective-permute-done | bytes 1048608 | tf_op jit(solution)/shard_map/ppermute | solution.py:303
  40.2 1.4 collective-permute-done.3
  41.6 0.2 pad_maximum_fusion.1.refs_4_
  41.7 0.0 copy-start.6
  41.8 1.6 pad_maximum_fusion.refs_2_
  43.3 15.1 %all-gather.4.cloned.1.call-done.refs_5_ = f32[2048,256]{1,0:T(8,128)} async-done(((f32[128,256]{1,0:T(8,128)}), f32[2048,256]{1,0:T(8,128)}) %all-gather.4.cloned.1.call-update) | async-done | bytes 2097168 | tf_op jit(solution)/shard_map/all_gather | solution.py:371
  58.4 1.2 collective-permute-start.4
  59.6 0.3 collective-permute-start.5
  59.9 1.6 collective-permute-start.6
  61.4 0.2 copy.8
  61.7 0.6 concatenate.32.refs_0_
  62.3 1.0 pad_maximum_fusion.4.sign_ref
  63.3 11.2 %start.1.start_ref = f32[8,128,128]{2,1,0:T(8,128)} custom-call(f32[8,128,128]{2,1,0:T(8,128)} %pad_maximum_fusion.4.sign_ref), custom_call_target="tpu_custom_call" | custom-call | flops 100000000 | bytes 1000000 | tf_op jit(solution)/shard_map/start/pallas_call | solution.py:339
  74.5 0.6 fusion.2.refs_0_
  75.1 6.2 %c0.1.refs_6_ = f32[512,256]{1,0:T(8,128)} custom-call(s32[16]{0:T(128)} %fusion.2.refs_0_, f32[512,8192]{1,0:T(8,128)} %xc3.1, f32[512,8192]{1,0:T(8,128)} %xc3.1, f32[512,8192]{1,0:T(8,128)} %xc3.1, f32[512,8192]{1,0:T(8,128)} %xc3.1, f32[2048,256]{1,0:T(8,128)} %all-gather.4.cloned.1.call-done.refs_5_), custom_call_target="tpu_custom_call" | custom-call | flops 1610612736 | bytes 10485760 | tf_op jit(solution)/shard_map/c0/pallas_call | solution.py:111
  81.3 7.9 %ab0.1.refs_5_ = f32[512,512]{1,0:T(8,128)} custom-call(s32[8]{0:T(128)} %concatenate.32.refs_0_, f32[512,8192]{1,0:T(8,128)} %xc3.1, f32[1024,512]{1,0:T(8,128)} %pad_maximum_fusion.refs_2_, f32[512,8192]{1,0:T(8,128)} %xc3.1, f32[1024,512]{1,0:T(8,128)} %copy-done.3), custom_call_target="tpu_custom_call" | custom-call | flops 3221225472 | bytes 12582912 | tf_op jit(solution)/shard_map/ab0/pallas_call | solution.py:111
  89.3 0.0 collective-permute-done.4.refs_2_
  89.3 0.0 collective-permute-done.5.refs_4_
  89.3 0.0 collective-permute-done.6.refs_5_
  89.3 1.9 collective-permute-start.7
  91.2 2.0 collective-permute-start.8
  93.2 2.2 collective-permute-start.9
  95.3 0.7 concatenate.34.refs_0_
  96.0 0.5 fusion.1.refs_0_
  96.5 6.6 %c1.1.refs_6_ = f32[512,256]{1,0:T(8,128)} custom-call(s32[16]{0:T(128)} %fusion.1.refs_0_, f32[512,8192]{1,0:T(8,128)} %xc3.1, f32[512,8192]{1,0:T(8,128)} %xc3.1, f32[512,8192]{1,0:T(8,128)} %xc3.1, f32[512,8192]{1,0:T(8,128)} %xc3.1, f32[2048,256]{1,0:T(8,128)} %collective-permute-done.6.refs_5_, f32[512,256]{1,0:T(8,128)} %c0.1.refs_6_), custom_call_target="tpu_custom_call" | custom-call | flops 1610612736 | bytes 10485760 | tf_op jit(solution)/shard_map/c1/pallas_call | solution.py:111
  103.1 8.6 %ab1.1.refs_5_ = f32[512,512]{1,0:T(8,128)} custom-call(s32[8]{0:T(128)} %concatenate.34.refs_0_, f32[512,8192]{1,0:T(8,128)} %xc3.1, f32[1024,512]{1,0:T(8,128)} %collective-permute-done.4.refs_2_, f32[512,8192]{1,0:T(8,128)} %xc3.1, f32[1024,512]{1,0:T(8,128)} %collective-permute-done.5.refs_4_, f32[512,512]{1,0:T(8,128)} %ab0.1.refs_5_), custom_call_target="tpu_custom_call" | custom-call | flops 3221225472 | bytes 12582912 | tf_op jit(solution)/shard_map/ab1/pallas_call | solution.py:111
  111.8 20.2 %collective-permute-done.7.refs_2_ = f32[1024,512]{1,0:T(8,128)S(1)} collective-permute-done((f32[1024,512]{1,0:T(8,128)}, f32[1024,512]{1,0:T(8,128)S(1)}, u32[]{:S(2)}, u32[]{:S(2)}) %collective-permute-start.7) | collective-permute-done | bytes 2097184 | tf_op jit(solution)/shard_map/ppermute | solution.py:303
  132.0 1.8 collective-permute-done.8.refs_4_
  133.8 6.1 %collective-permute-done.9.refs_5_ = f32[2048,256]{1,0:T(8,128)} collective-permute-done((f32[2048,256]{1,0:T(8,128)}, f32[2048,256]{1,0:T(8,128)}, u32[]{:S(2)}, u32[]{:S(2)}) %collective-permute-start.9) | collective-permute-done | bytes 2097184 | tf_op jit(solution)/shard_map/ppermute | solution.py:302
  139.9 0.0 collective-permute-start.10
  139.9 0.0 collective-permute-start.11
  139.9 3.7 %collective-permute-start.12 = (f32[2048,256]{1,0:T(8,128)}, f32[2048,256]{1,0:T(8,128)}, u32[]{:S(2)}, u32[]{:S(2)}) collective-permute-start(f32[2048,256]{1,0:T(8,128)} %collective-permute-done.6.refs_5_), channel_id=1, source_target_pairs={{0,96},{16,48},{32,64},{48,16},{64,32},{80,112},{96,0},{112,80},{1... | collective-permute-start | bytes 6291464 | tf_op jit(solution)/shard_map/ppermute | solution.py:302
  143.6 0.9 copy.9.scale_ref
  144.4 0.7 concatenate.35.refs_0_
  145.1 0.6 concatenate.27.index_ref
  145.8 0.6 fusion.refs_0_
  146.3 0.1 broadcast_in_dim.13
  146.4 0.7 broadcast_bitcast_fusion.keep_ref
  147.1 6.6 %c2.1.c_ref = f32[512,256]{1,0:T(8,128)} custom-call(s32[16]{0:T(128)} %fusion.refs_0_, f32[512,8192]{1,0:T(8,128)} %xc3.1, f32[512,8192]{1,0:T(8,128)} %xc3.1, f32[512,8192]{1,0:T(8,128)} %xc3.1, f32[512,8192]{1,0:T(8,128)} %xc3.1, f32[2048,256]{1,0:T(8,128)} %collective-permute-done.9.refs_5_, f32[512,256]{1,0:T(8,128)} %c1.1.refs_6_), custom_call_target="tpu_custom_call" | custom-call | flops 1610612736 | bytes 10485760 | tf_op jit(solution)/shard_map/c2/pallas_call | solution.py:111
  153.7 8.4 %ab2.1.ab_ref = f32[512,512]{1,0:T(8,128)} custom-call(s32[8]{0:T(128)} %concatenate.35.refs_0_, f32[512,8192]{1,0:T(8,128)} %xc3.1, f32[1024,512]{1,0:T(8,128)} %copy-done.5, f32[512,8192]{1,0:T(8,128)} %xc3.1, f32[1024,512]{1,0:T(8,128)} %collective-permute-done.8.refs_4_, f32[512,512]{1,0:T(8,128)} %ab1.1.refs_5_), custom_call_target="tpu_custom_call" | custom-call | flops 3221225472 | bytes 12582912 | tf_op jit(solution)/shard_map/ab2/pallas_call | solution.py:111
  162.1 13.8 %rest.1.rest_ref = f32[512,256]{1,0:T(8,128)} custom-call(f32[512,8192]{1,0:T(8,128)} %xc3.1, f32[4,16,128,256]{3,2,1,0:T(8,128)} %bitcast.43), custom_call_target="tpu_custom_call" | custom-call | flops 6442450944 | bytes 25165824 | tf_op jit(solution)/shard_map/rest/pallas_call | solution.py:140
  176.0 0.0 collective-permute-done.10.wa
  176.0 0.0 collective-permute-done.11.wb
  176.0 0.0 collective-permute-done.12.wc
  176.0 1.3 copy-done.4
  177.3 16.2 %project.1 = (bf16[512,1024]{1,0:T(8,128)(2,1)}, bf16[512,1024]{1,0:T(8,128)(2,1)}, f32[1024,128]{1,0:T(8,128)}) custom-call(s32[24]{0:T(128)} %concatenate.27.index_ref, f32[512,8192]{1,0:T(8,128)} %xc3.1, f32[1024,512]{1,0:T(8,128)} %copy-done.4, f32[512,8192]{1,0:T(8,128)} %xc3.1, f32[1024,512]{1,0:T(8,128)} %collective-permute-done.11.wb, ...), custom_call_target="tpu_custom_call" | custom-call | flops 4831838208 | bytes 14680064 | tf_op jit(solution)/shard_map/project/pallas_call | solution.py:382
  193.5 20.3 %all_to_all.14 = f32[16,64,128]{2,1,0:T(8,128)S(1)} all-to-all(f32[16,64,128]{2,1,0:T(8,128)} %bitcast.48), channel_id=1, replica_groups=mesh['batch'=4,'head'=2,'seq'=16] {'seq'}, dimensions={0} | all-to-all | bytes 1048576 | tf_op jit(solution)/shard_map/all_to_all | solution.py:403
  213.9 13.4 %all_to_all.15 = f32[16,64,128]{2,1,0:T(8,128)S(1)} all-to-all(f32[16,64,128]{2,1,0:T(8,128)S(1)} %broadcast_in_dim.15), channel_id=1, replica_groups=mesh['batch'=4,'head'=2,'seq'=16] {'seq'}, dimensions={0} | all-to-all | bytes 1048576 | tf_op jit(solution)/shard_map/all_to_all | solution.py:405
  227.4 12.2 %factor.1 = (bf16[4,512,128]{2,1,0:T(8,128)(2,1)}, f32[4,128,128]{2,1,0:T(8,128)}) custom-call(f32[1024,128]{1,0:T(8,128)S(1)} %bitcast.42, f32[8,128,128]{2,1,0:T(8,128)S(1)} %copy-done, bf16[512,1024]{1,0:T(8,128)(2,1)S(1)} %copy-done.1, bf16[512,1024]{1,0:T(8,128)(2,1)S(1)} %copy-done.2), custom_call_target="tpu_custom_call" | custom-call | flops 1000000000 | bytes 4194304 | tf_op jit(solution)/shard_map/factor/pallas_call | solution.py:407
  (22 shorter events, 0.1 us)
Async XLA Ops:
  7.2 51.3 %all-gather.4.cloned.1.call-start = ((), (), s32[]{:S(2)}) async-start(), calls=%async_computation.2 | async-start | bytes 2228224 | tf_op jit(solution)/shard_map/all_gather | solution.py:371
  10.1 152.0 %all-gather.6.cloned.1.call-start = ((), (), s32[]{:S(2)}) async-start(), calls=%async_computation.3 | async-start | bytes 8519680 | tf_op jit(solution)/shard_map/all_gather | solution.py:373
  11.0 9.3 %collective-permute-start = (f32[256,512]{1,0:T(8,128)S(1)}, f32[256,512]{1,0:T(8,128)S(1)}, u32[]{:S(2)}, u32[]{:S(2)}) collective-permute-start(f32[256,512]{1,0:T(8,128)S(1)} %get-tuple-element.37), channel_id=1, source_target_pairs={{0,4},{1,5},{2,6},{3,7},{4,0},{5,1},{6,2},{7,3},{8,12},{9,13},{10,... | collective-permute-start | bytes 1572872 | tf_op jit(solution)/shard_map/ppermute | solution.py:303
  12.6 9.2 %collective-permute-start.1 = (f32[256,512]{1,0:T(8,128)S(1)}, f32[256,512]{1,0:T(8,128)S(1)}, u32[]{:S(2)}, u32[]{:S(2)}) collective-permute-start(f32[256,512]{1,0:T(8,128)S(1)} %get-tuple-element.38), channel_id=1, source_target_pairs={{0,1},{1,0},{2,3},{3,2},{4,5},{5,4},{6,7},{7,6},{8,9},{9,8},{10,11... | collective-permute-start | bytes 1572872 | tf_op jit(solution)/shard_map/ppermute | solution.py:303
  22.0 18.2 %collective-permute-start.2 = (f32[512,512]{1,0:T(8,128)S(1)}, f32[512,512]{1,0:T(8,128)S(1)}, u32[]{:S(2)}, u32[]{:S(2)}) collective-permute-start(f32[512,512]{1,0:T(8,128)S(1)} %get-tuple-element.41), channel_id=1, source_target_pairs={{0,12},{1,13},{2,14},{3,15},{4,8},{5,9},{6,10},{7,11},{8,4},{9,5},... | collective-permute-start | bytes 3145736 | tf_op jit(solution)/shard_map/ppermute | solution.py:303
  24.1 17.4 %collective-permute-start.3 = (f32[512,512]{1,0:T(8,128)S(1)}, f32[512,512]{1,0:T(8,128)S(1)}, u32[]{:S(2)}, u32[]{:S(2)}) collective-permute-start(f32[512,512]{1,0:T(8,128)S(1)} %get-tuple-element.42), channel_id=1, source_target_pairs={{0,3},{1,2},{2,1},{3,0},{4,7},{5,6},{6,5},{7,4},{8,11},{9,10},{10,... | collective-permute-start | bytes 3145736 | tf_op jit(solution)/shard_map/ppermute | solution.py:303
  41.7 39.6 %copy-start.3 = (f32[1024,512]{1,0:T(8,128)}, f32[1024,512]{1,0:T(8,128)S(1)}, u32[]{:S(2)}) copy-start(f32[1024,512]{1,0:T(8,128)S(1)} %pad_maximum_fusion.1.refs_4_) | copy-start | bytes 6291460
  41.7 19.7 %copy-start.6 = (s32[4,2,128,64]{2,3,1,0:T(8,128)S(1)}, s32[4,2,128,64]{2,3,1,0:T(8,128)}, u32[]{:S(2)}) copy-start(s32[4,2,128,64]{2,3,1,0:T(8,128)} %param.9) | copy-start | bytes 786436
  58.4 30.8 %collective-permute-start.4 = (f32[1024,512]{1,0:T(8,128)}, f32[1024,512]{1,0:T(8,128)}, u32[]{:S(2)}, u32[]{:S(2)}) collective-permute-start(f32[1024,512]{1,0:T(8,128)} %pad_maximum_fusion.refs_2_), channel_id=1, source_target_pairs={{0,1},{1,0},{2,3},{3,2},{4,5},{5,4},{6,7},{7,6},{8,9},{9,8},{10,11... | collective-permute-start | bytes 6291464 | tf_op jit(solution)/shard_map/ppermute | solution.py:303
  59.6 29.7 %collective-permute-start.5 = (f32[1024,512]{1,0:T(8,128)S(1)}, f32[1024,512]{1,0:T(8,128)}, u32[]{:S(2)}, u32[]{:S(2)}) collective-permute-start(f32[1024,512]{1,0:T(8,128)S(1)} %pad_maximum_fusion.1.refs_4_), channel_id=1, source_target_pairs={{0,4},{1,5},{2,6},{3,7},{4,0},{5,1},{6,2},{7,3},{8,12},{9,13},{10,... | collective-permute-start | bytes 6291464 | tf_op jit(solution)/shard_map/ppermute | solution.py:303
  59.9 29.4 %collective-permute-start.6 = (f32[2048,256]{1,0:T(8,128)}, f32[2048,256]{1,0:T(8,128)}, u32[]{:S(2)}, u32[]{:S(2)}) collective-permute-start(f32[2048,256]{1,0:T(8,128)} %all-gather.4.cloned.1.call-done.refs_5_), channel_id=1, source_target_pairs={{0,32},{16,112},{32,0},{48,80},{64,96},{80,48},{96,64},{112,16},{1... | collective-permute-start | bytes 6291464 | tf_op jit(solution)/shard_map/ppermute | solution.py:302
  89.3 42.7 %collective-permute-start.7 = (f32[1024,512]{1,0:T(8,128)}, f32[1024,512]{1,0:T(8,128)S(1)}, u32[]{:S(2)}, u32[]{:S(2)}) collective-permute-start(f32[1024,512]{1,0:T(8,128)} %pad_maximum_fusion.refs_2_), channel_id=1, source_target_pairs={{0,3},{1,2},{2,1},{3,0},{4,7},{5,6},{6,5},{7,4},{8,11},{9,10},{10,... | collective-permute-start | bytes 6291464 | tf_op jit(solution)/shard_map/ppermute | solution.py:303
  91.2 42.6 %collective-permute-start.8 = (f32[1024,512]{1,0:T(8,128)}, f32[1024,512]{1,0:T(8,128)}, u32[]{:S(2)}, u32[]{:S(2)}) collective-permute-start(f32[1024,512]{1,0:T(8,128)} %copy-done.3), channel_id=1, source_target_pairs={{0,12},{1,13},{2,14},{3,15},{4,8},{5,9},{6,10},{7,11},{8,4},{9,5},... | collective-permute-start | bytes 6291464 | tf_op jit(solution)/shard_map/ppermute | solution.py:303
  93.2 46.7 %collective-permute-start.9 = (f32[2048,256]{1,0:T(8,128)}, f32[2048,256]{1,0:T(8,128)}, u32[]{:S(2)}, u32[]{:S(2)}) collective-permute-start(f32[2048,256]{1,0:T(8,128)} %all-gather.4.cloned.1.call-done.refs_5_), channel_id=1, source_target_pairs={{0,96},{16,48},{32,64},{48,16},{64,32},{80,112},{96,0},{112,80},{1... | collective-permute-start | bytes 6291464 | tf_op jit(solution)/shard_map/ppermute | solution.py:302
  103.1 40.5 %copy-start.7 = (f32[512]{0:T(512)S(1)}, f32[512]{0:T(512)}, u32[]{:S(2)}) copy-start(f32[512]{0:T(512)} %param.6) | copy-start | bytes 6148
  103.1 43.2 %copy-start.8 = (s32[8,4]{0,1:T(4,128)S(1)}, s32[8,4]{0,1:T(4,128)}, u32[]{:S(2)}) copy-start(s32[8,4]{0,1:T(4,128)} %param.8) | copy-start | bytes 388
  132.0 1.8 copy-start.5
  139.9 36.1 %collective-permute-start.10 = (f32[1024,512]{1,0:T(8,128)}, f32[1024,512]{1,0:T(8,128)S(1)}, u32[]{:S(2)}, u32[]{:S(2)}) collective-permute-start(f32[1024,512]{1,0:T(8,128)} %collective-permute-done.4.refs_2_), channel_id=1, source_target_pairs={{0,3},{1,2},{2,1},{3,0},{4,7},{5,6},{6,5},{7,4},{8,11},{9,10},{10,... | collective-permute-start | bytes 6291464 | tf_op jit(solution)/shard_map/ppermute | solution.py:303
  139.9 36.1 %collective-permute-start.11 = (f32[1024,512]{1,0:T(8,128)}, f32[1024,512]{1,0:T(8,128)}, u32[]{:S(2)}, u32[]{:S(2)}) collective-permute-start(f32[1024,512]{1,0:T(8,128)} %collective-permute-done.5.refs_4_), channel_id=1, source_target_pairs={{0,12},{1,13},{2,14},{3,15},{4,8},{5,9},{6,10},{7,11},{8,4},{9,5},... | collective-permute-start | bytes 6291464 | tf_op jit(solution)/shard_map/ppermute | solution.py:303
  139.9 36.1 %collective-permute-start.12 = (f32[2048,256]{1,0:T(8,128)}, f32[2048,256]{1,0:T(8,128)}, u32[]{:S(2)}, u32[]{:S(2)}) collective-permute-start(f32[2048,256]{1,0:T(8,128)} %collective-permute-done.6.refs_5_), channel_id=1, source_target_pairs={{0,96},{16,48},{32,64},{48,16},{64,32},{80,112},{96,0},{112,80},{1... | collective-permute-start | bytes 6291464 | tf_op jit(solution)/shard_map/ppermute | solution.py:302
  176.0 1.3 copy-start.4
  193.5 33.9 %copy-start = (f32[8,128,128]{2,1,0:T(8,128)S(1)}, f32[8,128,128]{2,1,0:T(8,128)}, u32[]{:S(2)}) copy-start(f32[8,128,128]{2,1,0:T(8,128)} %start.1.start_ref) | copy-start | bytes 1572868
  193.5 33.9 %copy-start.1 = (bf16[512,1024]{1,0:T(8,128)(2,1)S(1)}, bf16[512,1024]{1,0:T(8,128)(2,1)}, u32[]{:S(2)}) copy-start(bf16[512,1024]{1,0:T(8,128)(2,1)} %get-tuple-element.70.high_ref) | copy-start | bytes 3145732
  193.5 33.9 %copy-start.2 = (bf16[512,1024]{1,0:T(8,128)(2,1)S(1)}, bf16[512,1024]{1,0:T(8,128)(2,1)}, u32[]{:S(2)}) copy-start(bf16[512,1024]{1,0:T(8,128)(2,1)} %get-tuple-element.71.low_ref) | copy-start | bytes 3145732
Sparse Core Ops, SparseCore 0:
  10.7 47.6 all-gather.3
  61.3 87.3 all-gather.5

commit v4 on v3

--- a/solution.py
+++ b/solution.py
@@ -83,7 +83,7 @@
 
 def block_specs(tokens, blocks):
     specs, at = [], 0
-    for w, index, parts in blocks:
+    for w, parts in blocks:
         rows = w.shape[0] // STEPS
         for i in range(parts):
             specs.append(
@@ -91,29 +91,30 @@
             )
         specs.append(pl.BlockSpec((rows, w.shape[1]), lambda j, ix: (j, 0)))
         at += STEPS * parts
-    return specs, jnp.concatenate([index for _, index, _ in blocks])
+    return specs
 
 
 def block_operands(hidden, blocks):
-    return [x for w, _, parts in blocks for x in [hidden] * parts + [w]]
+    return [x for w, parts in blocks for x in [hidden] * parts + [w]]
 
 
 def cost(tokens, blocks):
-    macs = sum(w.size for w, _, _ in blocks) * tokens
-    return pl.CostEstimate(flops=6 * macs, bytes_accessed=sum(4 * w.size for w, _, _ in blocks) + 4 * tokens * 4096, transcendentals=0)
-
-
-def accumulate(name, hidden, total, blocks):
+    macs = sum(w.size for w, _ in blocks) * tokens
+    return pl.CostEstimate(
+        flops=6 * macs, bytes_accessed=sum(4 * w.size + 4 * tokens * w.shape[0] for w, _ in blocks), transcendentals=0
+    )
+
+
+def accumulate(name, hidden, total, index, blocks):
     tokens = hidden.shape[0]
     cols = blocks[0][0].shape[1]
-    specs, index = block_specs(tokens, blocks)
     whole = pl.BlockSpec((tokens, cols), lambda j, ix: (0, 0))
     return pl.pallas_call(
-        functools.partial(accumulate_kernel, [parts for _, _, parts in blocks], total is None),
+        functools.partial(accumulate_kernel, [parts for _, parts in blocks], total is None),
         grid_spec=pltpu.PrefetchScalarGridSpec(
             num_scalar_prefetch=1,
             grid=(STEPS,),
-            in_specs=specs + ([] if total is None else [whole]),
+            in_specs=block_specs(tokens, blocks) + ([] if total is None else [whole]),
             out_specs=whole,
         ),
         out_shape=jax.ShapeDtypeStruct((tokens, cols), F32),
@@ -303,27 +304,39 @@
     return lax.ppermute(v, ("head", "seq"), plane_pairs(axis, which))
 
 
-def gather_blocks(weight, deep, multiply, start):
+def gather_blocks(weight, deep, multiply, early):
     barrier = lax.optimization_barrier
     join = lambda a, b: jnp.concatenate([a, b], axis=0)
     half = weight.shape[0] // 2
     a, b = weight[:half], weight[half:]
     for which in range(2):
         a, b = barrier((a, b))
-        a1, b1 = barrier((send(a, "x", which), send(b, "y", which)))
-        a, b = join(a, a1), join(b, b1)
-    a, b, c = own = barrier((a, b, deep))
-    came = send(a, "y", 0), send(b, "x", 0), send(c, "z", 0)
-    totals = multiply("0", None, own, 0)
-    came, own, totals, start = barrier((came, own, totals, start))
-    a, b, c = own
-    later = send(a, "y", 1), send(b, "x", 1), send(c, "z", 1)
-    totals = multiply("1", totals, came, 1)
-    later, came, totals = barrier((later, came, totals))
-    a, b, c = came
-    last = send(a, "y", 1), send(b, "x", 1), send(c, "z", 1)
-    totals = multiply("2", totals, later, 2)
-    return last, totals, start
+        came = send(a, "x", which), send(b, "y", which)
+        if which:
+            came, early = barrier((came, early))
+        else:
+            came = barrier(came)
+        a, b = join(a, came[0]), join(b, came[1])
+    plane0 = barrier((a, b))
+    to_y_x = lambda blocks, which: (send(blocks[0], "y", which), send(blocks[1], "x", which))
+    plane1 = to_y_x(plane0, 0)
+    plane = multiply(None, plane0, 0)
+    deep0, plane0, plane = barrier((deep, plane0, plane))
+    deep1 = send(deep0, "z", 0)
+    depth = multiply(None, (deep0,), 0)
+    plane1, plane0, plane, depth = barrier((plane1, plane0, plane, depth))
+    plane2 = to_y_x(plane0, 1)
+    plane = multiply(plane, plane1, 1)
+    deep1, deep0, plane = barrier((deep1, deep0, plane))
+    deep2 = send(deep0, "z", 1)
+    depth = multiply(depth, (deep1,), 1)
+    plane2, plane1, depth = barrier((plane2, plane1, depth))
+    plane3 = to_y_x(plane1, 1)
+    plane = multiply(plane, plane2, 2)
+    deep2, deep1, plane = barrier((deep2, deep1, plane))
+    deep3 = send(deep1, "z", 1)
+    depth = multiply(depth, (deep2,), 2)
+    return (*plane3, deep3), (plane, depth), early
 
 
 def shards(hidden, row_scale, key_value_weight, outlier, sketch_sign_flags):
@@ -346,23 +359,21 @@
     head, place, plane = lax.axis_index("head"), lax.axis_index("seq"), lax.axis_index("batch")
     xs, ys, zs = around(place // RING, head), around(place % RING, head), around(plane, head)
     shard = lambda x, y: x * RING + y
-
-    def plane_blocks(a, b, k):
-        return [
-            (a, jnp.stack([2 * shard(x, ys[k]) for x in xs]), 1),
-            (b, jnp.stack([2 * shard(xs[k], y) + 1 for y in ys]), 1),
-        ]
-
-    def deep_block(c, k):
-        return (c, jnp.arange(seq, dtype=jnp.int32) * RING + zs[k], RING)
-
-    def multiply(name, totals, arrival, k):
-        a, b, c = arrival
-        ab_total, c_total = totals or (None, None)
-        return (
-            accumulate("ab" + name, hidden, ab_total, plane_blocks(a, b, k)),
-            accumulate("c" + name, hidden, c_total, [deep_block(c, k)]),
-        )
+    plane_index = [
+        (jnp.stack([2 * shard(x, ys[k]) for x in xs]), jnp.stack([2 * shard(xs[k], y) + 1 for y in ys]))
+        for k in range(RING)
+    ]
+    deep_index = [(jnp.arange(seq, dtype=jnp.int32) * RING + zs[k],) for k in range(RING)]
+    joined = lambda *lists: jnp.concatenate([i for indices in lists for i in indices])
+    plane_at = [joined(i) for i in plane_index]
+    deep_at = [joined(i) for i in deep_index]
+    last_at = joined(plane_index[3], deep_index[3])
+    scale = row_scale[:, None]
+    keep = jnp.repeat(jnp.repeat((1 - outlier).astype(F32), kv_cols, axis=1), 8, axis=0)
+
+    def multiply(total, blocks, k):
+        kind, parts, at = ("plane", 1, plane_at) if len(blocks) == 2 else ("deep", RING, deep_at)
+        return accumulate(kind + str(k), hidden, total, at[k], [(w, parts) for w in blocks])
 
     flat = key_value_weight.reshape(rows, cols)
     quarter = rows // RING
@@ -371,13 +382,13 @@
     deep = lax.all_gather(own[:, :DEEP], "seq", axis=0, tiled=True)
     own, _ = lax.optimization_barrier((own[:, DEEP:], own))
     rest = lax.all_gather(own, ("batch", "seq"), axis=0).reshape(RING, seq, quarter, cols - rest_at)
-    (a3, b3, c3), (ab, c), start = gather_blocks(flat[:, :PERMUTED], deep, multiply, start)
+    early = (start, scale, keep, last_at)
+    (a3, b3, c3), (ab, c), (start, scale, keep, last_at) = gather_blocks(flat[:, :PERMUTED], deep, multiply, early)
     rest, ab, c = lax.optimization_barrier((rest, ab, c))
     cd = accumulate_all(hidden, rest)
 
-    last = plane_blocks(a3, b3, 3) + [deep_block(c3, 3)]
-    specs, index = block_specs(tokens, last)
-    keep = jnp.repeat(jnp.repeat((1 - outlier).astype(F32), kv_cols, axis=1), 8, axis=0)
+    last = [(a3, 1), (b3, 1), (c3, RING)]
+    specs = block_specs(tokens, last)
     whole = lambda *shape: pl.BlockSpec(shape, lambda j, ix: (0,) * len(shape))
     high, low, gram = pl.pallas_call(
         project_kernel,
@@ -398,7 +409,7 @@
         compiler_params=pltpu.CompilerParams(vmem_limit_bytes=VMEM_LIMIT, dimension_semantics=("arbitrary",)),
         name="project",
         cost_estimate=cost(tokens, last),
-    )(index, *block_operands(hidden, last), ab, c, cd, row_scale[:, None], keep)
+    )(last_at, *block_operands(hidden, last), ab, c, cd, scale, keep)
 
     pieces = lax.all_to_all(gram, "seq", 0, 0, tiled=True)
     piece = jnp.sum(pieces.reshape(seq, 128 * pairs // seq, 128), axis=0)

time: 247 us -> 237 us (0.960)
  waiting for transfers between devices: 66 us -> 53.6 us
  other arithmetic: 4.63 us -> 8.27 us
  blocking collectives: 33.8 us -> 30.4 us
    ppermute x10, waiting for transfers between devices: 44 us -> 28.4 us  [send(): return lax.ppermute(v, ('head', 'seq'), plane_pairs(axis, which))]
    all_gather x1, waiting for transfers between devices: 15.1 us -> 4.58 us  [shards(): deep = lax.all_gather(own[:, :DEEP], 'seq', axis=0, tiled=True)]
    all_gather x1, waiting for transfers between devices: 0.01 us -> 9.59 us  [shards(): lax.all_gather(own, ('batch', 'seq'), axis=0)]
    ppermute x3, waiting for transfers between devices: 6.09 us -> 10.3 us  [send(): return lax.ppermute(v, ('batch', 'head'), depth_pairs(which))]
    all_to_all x1, blocking collectives: 20.3 us -> 16.6 us  [shards(): pieces = lax.all_to_all(gram, 'seq', 0, 0, tiled=True)]
    concatenate x3, other arithmetic: 1.91 us -> 5.59 us  [gather_blocks(): join = lambda a, b: jnp.concatenate([a, b], axis=0)]
  transfers between devices with their start and end apart: 15 -> 15, of which waited for: 8 -> 10; matrix products, arithmetic and copies ran while one was open for 4% -> 5% of each run, Pallas kernels for 28% -> 29%
where the time goes in v4:
time: 237 us; the launch traced here: 236 us
  Pallas kernels  97.9 us (41%)
  waiting for transfers between devices  53.6 us (23%)
  blocking collectives  30.4 us (13%)
  starting transfers between devices  22.8 us (10%)
  between operations  14.2 us (6%)
  local copies, waits for them, and re-layouts  8.79 us (4%)
  other arithmetic  8.27 us (3%)
    pallas_call x6, Pallas kernels, accumulate(): pl.pallas_call(functools.partial(accumulate_kernel, [parts for _, parts i...  44.3 us
    ppermute x10, waiting for transfers between devices, send(): return lax.ppermute(v, ('head', 'seq'), plane_pairs(axis, which))  28.4 us
    all_to_all x1, blocking collectives, shards(): pieces = lax.all_to_all(gram, 'seq', 0, 0, tiled=True)  16.6 us
    pallas_call x1, Pallas kernels, shards(): pl.pallas_call(project_kernel, grid_spec=pltpu.PrefetchScalarGridSpec(num...  16.3 us
    ppermute x10, starting transfers between devices, send(): return lax.ppermute(v, ('head', 'seq'), plane_pairs(axis, which))  16.1 us
    pallas_call x1, Pallas kernels, accumulate_all(): pl.pallas_call(accumulate_all_kernel, grid=(seq // 2,), in_specs=[pl.Bloc...  13.8 us
    all_to_all x1, blocking collectives, shards(): lax.all_to_all(jnp.broadcast_to(piece, (seq,) + piece.shape), 'seq', 0, 0)  13.8 us
    pallas_call x1, Pallas kernels, shards(): pl.pallas_call(functools.partial(factor_kernel, root_length), out_shape=[...  12.2 us
  transfers between devices with their start and end apart: 15, of which 10 were waited for; matrix products, arithmetic and copies ran while one was open for 5% of the time, Pallas kernels for 29%

profile of v4, /device:TPU:0, one launch (start us, length us, event | category | flops | bytes accessed | tf_op | source)
XLA Modules:
  0.0 235.9 jit_solution(10011569178266170148)
XLA Ops:
  7.2 0.0 all-gather.4.cloned.1.call-start
  7.2 2.1 copy.10
  9.3 0.1 slice.25
  9.4 0.7 fusion.5
  10.1 0.0 all-gather.4.cloned.1.call-update
  10.1 0.0 all-gather.6.cloned.1.call-start
  10.2 0.7 all-gather.6.cloned.1.call-update
  10.9 0.1 fusion.4
  11.0 0.0 copy-start.5
  11.0 1.7 collective-permute-start
  12.6 1.6 collective-permute-start.1
  14.2 6.0 %collective-permute-done = f32[256,512]{1,0:T(8,128)S(1)} collective-permute-done((f32[256,512]{1,0:T(8,128)S(1)}, f32[256,512]{1,0:T(8,128)S(1)}, u32[]{:S(2)}, u32[]{:S(2)}) %collective-permute-start) | collective-permute-done | bytes 524320 | tf_op jit(solution)/shard_map/ppermute | solution.py:304
  20.2 1.6 collective-permute-done.1
  21.8 0.2 pad_maximum_fusion.2
  22.0 0.0 copy-start.7
  22.0 2.2 collective-permute-start.2
  24.2 3.0 %collective-permute-start.3 = (f32[512,512]{1,0:T(8,128)S(1)}, f32[512,512]{1,0:T(8,128)}, u32[]{:S(2)}, u32[]{:S(2)}) collective-permute-start(f32[512,512]{1,0:T(8,128)S(1)} %get-tuple-element.49), channel_id=1, source_target_pairs={{0,3},{1,2},{2,1},{3,0},{4,7},{5,6},{6,5},{7,4},{8,11},{9,10},{10,... | collective-permute-start | bytes 3145736 | tf_op jit(solution)/shard_map/ppermute | solution.py:304
  27.2 0.2 copy.8
  27.4 0.7 concatenate.30.index_ref
  28.1 1.0 pad_maximum_fusion.4.sign_ref
  29.1 11.2 %start.1.start_ref = f32[8,128,128]{2,1,0:T(8,128)} custom-call(f32[8,128,128]{2,1,0:T(8,128)} %pad_maximum_fusion.4.sign_ref), custom_call_target="tpu_custom_call" | custom-call | flops 100000000 | bytes 1000000 | tf_op jit(solution)/shard_map/start/pallas_call | solution.py:352
  40.3 0.1 broadcast_in_dim.13
  40.4 0.7 broadcast_bitcast_fusion.keep_ref
  41.1 0.0 collective-permute-done.2
  41.1 0.6 collective-permute-done.3
  41.7 2.7 %pad_maximum_fusion.1.refs_4_ = f32[1024,512]{1,0:T(8,128)} fusion(f32[512,512]{1,0:T(8,128)} %collective-permute-done.3, f32[512,512]{1,0:T(8,128)S(1)} %get-tuple-element.49), kind=kLoop, calls=%fused_computation.1 | loop fusion | flops 524288 | bytes 4194304 | tf_op jit(solution)/shard_map/concatenate | solution.py:309
  44.4 2.7 %pad_maximum_fusion.refs_2_ = f32[1024,512]{1,0:T(8,128)} fusion(f32[512,512]{1,0:T(8,128)} %collective-permute-done.2, f32[512,512]{1,0:T(8,128)S(1)} %get-tuple-element.48), kind=kLoop, calls=%fused_computation | loop fusion | flops 524288 | bytes 4194304 | tf_op jit(solution)/shard_map/concatenate | solution.py:309
  47.1 0.5 collective-permute-start.4
  47.6 0.5 collective-permute-start.5
  48.1 0.7 concatenate.33.refs_0_
  48.7 7.9 %plane0.1.refs_5_ = f32[512,512]{1,0:T(8,128)} custom-call(s32[8]{0:T(128)} %concatenate.33.refs_0_, f32[512,8192]{1,0:T(8,128)} %xc3.1, f32[1024,512]{1,0:T(8,128)} %pad_maximum_fusion.refs_2_, f32[512,8192]{1,0:T(8,128)} %xc3.1, f32[1024,512]{1,0:T(8,128)} %pad_maximum_fusion.1.refs_4_), custom_call_target="tpu_custom_call" | custom-call | flops 3221225472 | bytes 8388608 | tf_op jit(solution)/shard_map/plane0/pallas_call | solution.py:112
  56.6 4.6 %all-gather.4.cloned.1.call-done.refs_5_ = f32[2048,256]{1,0:T(8,128)} async-done(((f32[128,256]{1,0:T(8,128)}), f32[2048,256]{1,0:T(8,128)}) %all-gather.4.cloned.1.call-update) | async-done | bytes 2097168 | tf_op jit(solution)/shard_map/all_gather | solution.py:382
  61.2 1.7 collective-permute-start.8
  62.9 0.6 fusion.2.refs_0_
  63.5 6.2 %deep0.1.refs_6_ = f32[512,256]{1,0:T(8,128)} custom-call(s32[16]{0:T(128)} %fusion.2.refs_0_, f32[512,8192]{1,0:T(8,128)} %xc3.1, f32[512,8192]{1,0:T(8,128)} %xc3.1, f32[512,8192]{1,0:T(8,128)} %xc3.1, f32[512,8192]{1,0:T(8,128)} %xc3.1, f32[2048,256]{1,0:T(8,128)} %all-gather.4.cloned.1.call-done.refs_5_), custom_call_target="tpu_custom_call" | custom-call | flops 1610612736 | bytes 6291456 | tf_op jit(solution)/shard_map/deep0/pallas_call | solution.py:112
  69.7 8.7 %collective-permute-done.4.refs_2_ = f32[1024,512]{1,0:T(8,128)} collective-permute-done((f32[1024,512]{1,0:T(8,128)}, f32[1024,512]{1,0:T(8,128)}, u32[]{:S(2)}, u32[]{:S(2)}) %collective-permute-start.4) | collective-permute-done | bytes 2097184 | tf_op jit(solution)/shard_map/ppermute | solution.py:304
  78.5 0.8 collective-permute-done.5.refs_4_
  79.3 1.4 collective-permute-start.6
  80.7 1.8 collective-permute-start.7
  82.5 0.7 concatenate.34.refs_0_
  83.2 8.5 %plane1.1.refs_5_ = f32[512,512]{1,0:T(8,128)} custom-call(s32[8]{0:T(128)} %concatenate.34.refs_0_, f32[512,8192]{1,0:T(8,128)} %xc3.1, f32[1024,512]{1,0:T(8,128)} %collective-permute-done.4.refs_2_, f32[512,8192]{1,0:T(8,128)} %xc3.1, f32[1024,512]{1,0:T(8,128)} %collective-permute-done.5.refs_4_, f32[512,512]{1,0:T(8,128)} %plane0.1.refs_5_), custom_call_target="tpu_custom_call" | custom-call | flops 3221225472 | bytes 8388608 | tf_op jit(solution)/shard_map/plane1/pallas_call | solution.py:112
  91.7 0.0 collective-permute-done.8.refs_5_
  91.7 2.7 %collective-permute-start.11 = (f32[2048,256]{1,0:T(8,128)}, f32[2048,256]{1,0:T(8,128)}, u32[]{:S(2)}, u32[]{:S(2)}) collective-permute-start(f32[2048,256]{1,0:T(8,128)} %all-gather.4.cloned.1.call-done.refs_5_), channel_id=1, source_target_pairs={{0,96},{16,48},{32,64},{48,16},{64,32},{80,112},{96,0},{112,80},{1... | collective-permute-start | bytes 6291464 | tf_op jit(solution)/shard_map/ppermute | solution.py:303
  94.4 0.6 concatenate.35.refs_0_
  95.0 0.5 fusion.1.refs_0_
  95.5 6.6 %deep1.1.refs_6_ = f32[512,256]{1,0:T(8,128)} custom-call(s32[16]{0:T(128)} %fusion.1.refs_0_, f32[512,8192]{1,0:T(8,128)} %xc3.1, f32[512,8192]{1,0:T(8,128)} %xc3.1, f32[512,8192]{1,0:T(8,128)} %xc3.1, f32[512,8192]{1,0:T(8,128)} %xc3.1, f32[2048,256]{1,0:T(8,128)} %collective-permute-done.8.refs_5_, f32[512,256]{1,0:T(8,128)} %deep0.1.refs_6_), custom_call_target="tpu_custom_call" | custom-call | flops 1610612736 | bytes 6291456 | tf_op jit(solution)/shard_map/deep1/pallas_call | solution.py:112
  102.1 10.7 %collective-permute-done.6.refs_2_ = f32[1024,512]{1,0:T(8,128)S(1)} collective-permute-done((f32[1024,512]{1,0:T(8,128)}, f32[1024,512]{1,0:T(8,128)S(1)}, u32[]{:S(2)}, u32[]{:S(2)}) %collective-permute-start.6) | collective-permute-done | bytes 2097184 | tf_op jit(solution)/shard_map/ppermute | solution.py:304
  112.8 1.3 copy-done.4
  114.1 1.9 collective-permute-start.10
  116.0 1.7 collective-permute-start.9
  117.7 8.4 %plane2.1.ab_ref = f32[512,512]{1,0:T(8,128)} custom-call(s32[8]{0:T(128)} %concatenate.35.refs_0_, f32[512,8192]{1,0:T(8,128)} %xc3.1, f32[1024,512]{1,0:T(8,128)} %copy-done.4, f32[512,8192]{1,0:T(8,128)} %xc3.1, f32[1024,512]{1,0:T(8,128)} %collective-permute-done.7.refs_4_, f32[512,512]{1,0:T(8,128)} %plane1.1.refs_5_), custom_call_target="tpu_custom_call" | custom-call | flops 3221225472 | bytes 8388608 | tf_op jit(solution)/shard_map/plane2/pallas_call | solution.py:112
  126.1 8.4 %collective-permute-done.11.refs_5_ = f32[2048,256]{1,0:T(8,128)} collective-permute-done((f32[2048,256]{1,0:T(8,128)}, f32[2048,256]{1,0:T(8,128)}, u32[]{:S(2)}, u32[]{:S(2)}) %collective-permute-start.11) | collective-permute-done | bytes 2097184 | tf_op jit(solution)/shard_map/ppermute | solution.py:303
  134.5 2.2 collective-permute-start.12
  136.7 0.5 fusion.refs_0_
  137.2 0.9 copy.9.scale_ref
  138.1 6.6 %deep2.1.c_ref = f32[512,256]{1,0:T(8,128)} custom-call(s32[16]{0:T(128)} %fusion.refs_0_, f32[512,8192]{1,0:T(8,128)} %xc3.1, f32[512,8192]{1,0:T(8,128)} %xc3.1, f32[512,8192]{1,0:T(8,128)} %xc3.1, f32[512,8192]{1,0:T(8,128)} %xc3.1, f32[2048,256]{1,0:T(8,128)} %collective-permute-done.11.refs_5_, f32[512,256]{1,0:T(8,128)} %deep1.1.refs_6_), custom_call_target="tpu_custom_call" | custom-call | flops 1610612736 | bytes 6291456 | tf_op jit(solution)/shard_map/deep2/pallas_call | solution.py:112
  144.7 9.6 %all-gather.6.cloned.1.call-done = f32[8192,256]{1,0:T(8,128)} async-done(((f32[128,256]{1,0:T(8,128)}), f32[8192,256]{1,0:T(8,128)}) %all-gather.6.cloned.1.call-update) | async-done | bytes 8388624 | tf_op jit(solution)/shard_map/all_gather | solution.py:384
  154.3 13.8 %rest.1.rest_ref = f32[512,256]{1,0:T(8,128)} custom-call(f32[512,8192]{1,0:T(8,128)} %xc3.1, f32[4,16,128,256]{3,2,1,0:T(8,128)} %bitcast.43), custom_call_target="tpu_custom_call" | custom-call | flops 6442450944 | bytes 25165824 | tf_op jit(solution)/shard_map/rest/pallas_call | solution.py:141
  168.1 0.0 collective-permute-done.10.wb
  168.1 1.9 collective-permute-done.12.wc
  170.0 16.3 %project.1 = (bf16[512,1024]{1,0:T(8,128)(2,1)}, bf16[512,1024]{1,0:T(8,128)(2,1)}, f32[1024,128]{1,0:T(8,128)}) custom-call(s32[24]{0:T(128)} %concatenate.30.index_ref, f32[512,8192]{1,0:T(8,128)} %xc3.1, f32[1024,512]{1,0:T(8,128)} %collective-permute-done.9.wa, f32[512,8192]{1,0:T(8,128)} %xc3.1, f32[1024,512]{1,0:T(8,128)} %copy-done.3, ...), custom_call_target="tpu_custom_call" | custom-call | flops 4831838208 | bytes 14680064 | tf_op jit(solution)/shard_map/project/pallas_call | solution.py:393
  186.4 16.6 %all_to_all.14 = f32[16,64,128]{2,1,0:T(8,128)S(1)} all-to-all(f32[16,64,128]{2,1,0:T(8,128)} %bitcast.48), channel_id=1, replica_groups=mesh['batch'=4,'head'=2,'seq'=16] {'seq'}, dimensions={0} | all-to-all | bytes 1048576 | tf_op jit(solution)/shard_map/all_to_all | solution.py:414
  203.1 13.8 %all_to_all.15 = f32[16,64,128]{2,1,0:T(8,128)S(1)} all-to-all(f32[16,64,128]{2,1,0:T(8,128)S(1)} %broadcast_in_dim.15), channel_id=1, replica_groups=mesh['batch'=4,'head'=2,'seq'=16] {'seq'}, dimensions={0} | all-to-all | bytes 1048576 | tf_op jit(solution)/shard_map/all_to_all | solution.py:416
  216.9 12.2 %factor.1 = (bf16[4,512,128]{2,1,0:T(8,128)(2,1)}, f32[4,128,128]{2,1,0:T(8,128)}) custom-call(f32[1024,128]{1,0:T(8,128)S(1)} %bitcast.42, f32[8,128,128]{2,1,0:T(8,128)S(1)} %copy-done, bf16[512,1024]{1,0:T(8,128)(2,1)S(1)} %copy-done.1, bf16[512,1024]{1,0:T(8,128)(2,1)S(1)} %copy-done.2), custom_call_target="tpu_custom_call" | custom-call | flops 1000000000 | bytes 4194304 | tf_op jit(solution)/shard_map/factor/pallas_call | solution.py:418
  (20 shorter events, 0.1 us)
Async XLA Ops:
  7.2 54.1 %all-gather.4.cloned.1.call-start = ((), (), s32[]{:S(2)}) async-start(), calls=%async_computation.2 | async-start | bytes 2228224 | tf_op jit(solution)/shard_map/all_gather | solution.py:382
  10.1 144.2 %all-gather.6.cloned.1.call-start = ((), (), s32[]{:S(2)}) async-start(), calls=%async_computation.3 | async-start | bytes 8519680 | tf_op jit(solution)/shard_map/all_gather | solution.py:384
  11.0 16.2 %copy-start.5 = (s32[4,2,128,64]{2,3,1,0:T(8,128)S(1)}, s32[4,2,128,64]{2,3,1,0:T(8,128)}, u32[]{:S(2)}) copy-start(s32[4,2,128,64]{2,3,1,0:T(8,128)} %param.9) | copy-start | bytes 786436
  11.0 9.3 %collective-permute-start = (f32[256,512]{1,0:T(8,128)S(1)}, f32[256,512]{1,0:T(8,128)S(1)}, u32[]{:S(2)}, u32[]{:S(2)}) collective-permute-start(f32[256,512]{1,0:T(8,128)S(1)} %get-tuple-element.44), channel_id=1, source_target_pairs={{0,4},{1,5},{2,6},{3,7},{4,0},{5,1},{6,2},{7,3},{8,12},{9,13},{10,... | collective-permute-start | bytes 1572872 | tf_op jit(solution)/shard_map/ppermute | solution.py:304
  12.6 9.2 %collective-permute-start.1 = (f32[256,512]{1,0:T(8,128)S(1)}, f32[256,512]{1,0:T(8,128)S(1)}, u32[]{:S(2)}, u32[]{:S(2)}) collective-permute-start(f32[256,512]{1,0:T(8,128)S(1)} %get-tuple-element.45), channel_id=1, source_target_pairs={{0,1},{1,0},{2,3},{3,2},{4,5},{5,4},{6,7},{7,6},{8,9},{9,8},{10,11... | collective-permute-start | bytes 1572872 | tf_op jit(solution)/shard_map/ppermute | solution.py:304
  22.0 18.4 %copy-start.7 = (s32[8,4]{0,1:T(4,128)S(1)}, s32[8,4]{0,1:T(4,128)}, u32[]{:S(2)}) copy-start(s32[8,4]{0,1:T(4,128)} %param.8) | copy-start | bytes 388
  22.0 19.1 %collective-permute-start.2 = (f32[512,512]{1,0:T(8,128)S(1)}, f32[512,512]{1,0:T(8,128)}, u32[]{:S(2)}, u32[]{:S(2)}) collective-permute-start(f32[512,512]{1,0:T(8,128)S(1)} %get-tuple-element.48), channel_id=1, source_target_pairs={{0,12},{1,13},{2,14},{3,15},{4,8},{5,9},{6,10},{7,11},{8,4},{9,5},... | collective-permute-start | bytes 3145736 | tf_op jit(solution)/shard_map/ppermute | solution.py:304
  24.2 17.5 %collective-permute-start.3 = (f32[512,512]{1,0:T(8,128)S(1)}, f32[512,512]{1,0:T(8,128)}, u32[]{:S(2)}, u32[]{:S(2)}) collective-permute-start(f32[512,512]{1,0:T(8,128)S(1)} %get-tuple-element.49), channel_id=1, source_target_pairs={{0,3},{1,2},{2,1},{3,0},{4,7},{5,6},{6,5},{7,4},{8,11},{9,10},{10,... | collective-permute-start | bytes 3145736 | tf_op jit(solution)/shard_map/ppermute | solution.py:304
  47.1 31.4 %collective-permute-start.4 = (f32[1024,512]{1,0:T(8,128)}, f32[1024,512]{1,0:T(8,128)}, u32[]{:S(2)}, u32[]{:S(2)}) collective-permute-start(f32[1024,512]{1,0:T(8,128)} %pad_maximum_fusion.refs_2_), channel_id=1, source_target_pairs={{0,1},{1,0},{2,3},{3,2},{4,5},{5,4},{6,7},{7,6},{8,9},{9,8},{10,11... | collective-permute-start | bytes 6291464 | tf_op jit(solution)/shard_map/ppermute | solution.py:304
  47.6 31.7 %collective-permute-start.5 = (f32[1024,512]{1,0:T(8,128)}, f32[1024,512]{1,0:T(8,128)}, u32[]{:S(2)}, u32[]{:S(2)}) collective-permute-start(f32[1024,512]{1,0:T(8,128)} %pad_maximum_fusion.1.refs_4_), channel_id=1, source_target_pairs={{0,4},{1,5},{2,6},{3,7},{4,0},{5,1},{6,2},{7,3},{8,12},{9,13},{10,... | collective-permute-start | bytes 6291464 | tf_op jit(solution)/shard_map/ppermute | solution.py:304
  61.2 30.4 %collective-permute-start.8 = (f32[2048,256]{1,0:T(8,128)}, f32[2048,256]{1,0:T(8,128)}, u32[]{:S(2)}, u32[]{:S(2)}) collective-permute-start(f32[2048,256]{1,0:T(8,128)} %all-gather.4.cloned.1.call-done.refs_5_), channel_id=1, source_target_pairs={{0,32},{16,112},{32,0},{48,80},{64,96},{80,48},{96,64},{112,16},{1... | collective-permute-start | bytes 6291464 | tf_op jit(solution)/shard_map/ppermute | solution.py:303
  79.3 33.5 %collective-permute-start.6 = (f32[1024,512]{1,0:T(8,128)}, f32[1024,512]{1,0:T(8,128)S(1)}, u32[]{:S(2)}, u32[]{:S(2)}) collective-permute-start(f32[1024,512]{1,0:T(8,128)} %pad_maximum_fusion.refs_2_), channel_id=1, source_target_pairs={{0,3},{1,2},{2,1},{3,0},{4,7},{5,6},{6,5},{7,4},{8,11},{9,10},{10,... | collective-permute-start | bytes 6291464 | tf_op jit(solution)/shard_map/ppermute | solution.py:304
  80.7 33.5 %collective-permute-start.7 = (f32[1024,512]{1,0:T(8,128)}, f32[1024,512]{1,0:T(8,128)}, u32[]{:S(2)}, u32[]{:S(2)}) collective-permute-start(f32[1024,512]{1,0:T(8,128)} %pad_maximum_fusion.1.refs_4_), channel_id=1, source_target_pairs={{0,12},{1,13},{2,14},{3,15},{4,8},{5,9},{6,10},{7,11},{8,4},{9,5},... | collective-permute-start | bytes 6291464 | tf_op jit(solution)/shard_map/ppermute | solution.py:304
  91.7 42.8 %collective-permute-start.11 = (f32[2048,256]{1,0:T(8,128)}, f32[2048,256]{1,0:T(8,128)}, u32[]{:S(2)}, u32[]{:S(2)}) collective-permute-start(f32[2048,256]{1,0:T(8,128)} %all-gather.4.cloned.1.call-done.refs_5_), channel_id=1, source_target_pairs={{0,96},{16,48},{32,64},{48,16},{64,32},{80,112},{96,0},{112,80},{1... | collective-permute-start | bytes 6291464 | tf_op jit(solution)/shard_map/ppermute | solution.py:303
  102.1 35.1 %copy-start.6 = (f32[512]{0:T(512)S(1)}, f32[512]{0:T(512)}, u32[]{:S(2)}) copy-start(f32[512]{0:T(512)} %param.6) | copy-start | bytes 6148
  112.8 1.3 copy-start.4
  114.1 54.0 %collective-permute-start.10 = (f32[1024,512]{1,0:T(8,128)}, f32[1024,512]{1,0:T(8,128)S(1)}, u32[]{:S(2)}, u32[]{:S(2)}) collective-permute-start(f32[1024,512]{1,0:T(8,128)} %collective-permute-done.5.refs_4_), channel_id=1, source_target_pairs={{0,12},{1,13},{2,14},{3,15},{4,8},{5,9},{6,10},{7,11},{8,4},{9,5},... | collective-permute-start | bytes 6291464 | tf_op jit(solution)/shard_map/ppermute | solution.py:304
  116.0 52.1 %collective-permute-start.9 = (f32[1024,512]{1,0:T(8,128)}, f32[1024,512]{1,0:T(8,128)}, u32[]{:S(2)}, u32[]{:S(2)}) collective-permute-start(f32[1024,512]{1,0:T(8,128)} %collective-permute-done.4.refs_2_), channel_id=1, source_target_pairs={{0,3},{1,2},{2,1},{3,0},{4,7},{5,6},{6,5},{7,4},{8,11},{9,10},{10,... | collective-permute-start | bytes 6291464 | tf_op jit(solution)/shard_map/ppermute | solution.py:304
  134.5 35.5 %collective-permute-start.12 = (f32[2048,256]{1,0:T(8,128)}, f32[2048,256]{1,0:T(8,128)}, u32[]{:S(2)}, u32[]{:S(2)}) collective-permute-start(f32[2048,256]{1,0:T(8,128)} %collective-permute-done.8.refs_5_), channel_id=1, source_target_pairs={{0,96},{16,48},{32,64},{48,16},{64,32},{80,112},{96,0},{112,80},{1... | collective-permute-start | bytes 6291464 | tf_op jit(solution)/shard_map/ppermute | solution.py:303
  168.1 1.9 copy-start.3
  186.4 30.5 %copy-start = (f32[8,128,128]{2,1,0:T(8,128)S(1)}, f32[8,128,128]{2,1,0:T(8,128)}, u32[]{:S(2)}) copy-start(f32[8,128,128]{2,1,0:T(8,128)} %start.1.start_ref) | copy-start | bytes 1572868
  186.4 30.5 %copy-start.1 = (bf16[512,1024]{1,0:T(8,128)(2,1)S(1)}, bf16[512,1024]{1,0:T(8,128)(2,1)}, u32[]{:S(2)}) copy-start(bf16[512,1024]{1,0:T(8,128)(2,1)} %get-tuple-element.84.high_ref) | copy-start | bytes 3145732
  186.4 30.5 %copy-start.2 = (bf16[512,1024]{1,0:T(8,128)(2,1)S(1)}, bf16[512,1024]{1,0:T(8,128)(2,1)}, u32[]{:S(2)}) copy-start(bf16[512,1024]{1,0:T(8,128)(2,1)} %get-tuple-element.85.low_ref) | copy-start | bytes 3145732
Sparse Core Ops, SparseCore 0:
  10.7 50.4 all-gather.3
  64.1 90.1 all-gather.5

commit v5 on v4

--- a/solution.py
+++ b/solution.py
@@ -12,7 +12,7 @@
 RANK = 64
 RING = 4
 STEPS = 4
-PERMUTED = 512
+PERMUTED = 640
 DEEP = 256
 WIDE = 256
 UNROLL = 4
@@ -155,21 +155,19 @@
     )(hidden, weight)
 
 
-def project_kernel(index_ref, xa, wa, xb, wb, xc0, xc1, xc2, xc3, wc, ab_ref, c_ref, rest_ref, scale_ref, keep_ref,
-                   high_ref, low_ref, gram_ref, ab_acc, c_acc):
+def project_kernel(index_ref, x0, x1, x2, x3, w, plane_ref, depth_ref, rest_ref, scale_ref, keep_ref,
+                   high_ref, low_ref, gram_ref, depth_acc):
     step = pl.program_id(0)
 
     @pl.when(step == 0)
     def _():
-        ab_acc[...] = ab_ref[...]
-        c_acc[...] = c_ref[...]
-
-    ab_acc[...] += three_products(xa[...], wa[...]) + three_products(xb[...], wb[...])
-    c_acc[...] += three_products(jnp.concatenate([xc0[...], xc1[...], xc2[...], xc3[...]], axis=1), wc[...])
+        depth_acc[...] = depth_ref[...]
+
+    depth_acc[...] += three_products(jnp.concatenate([x0[...], x1[...], x2[...], x3[...]], axis=1), w[...])
 
     @pl.when(step == STEPS - 1)
     def _():
-        epilogue((ab_acc, c_acc, rest_ref), scale_ref, keep_ref, high_ref, low_ref, gram_ref)
+        epilogue((plane_ref, depth_acc, rest_ref), scale_ref, keep_ref, high_ref, low_ref, gram_ref)
 
 
 def epilogue(parts, scale_ref, keep_ref, high_ref, low_ref, gram_ref):
@@ -177,18 +175,19 @@
     at = 0
     for part in parts:
         for first in range(0, part.shape[1], WIDE):
-            here = slice(at, at + WIDE)
+            wide = min(WIDE, part.shape[1] - first)
+            here = slice(at, at + wide)
 
             @pl.loop(0, tokens // GROUP, unroll=UNROLL)
-            def _(g, part=part, first=first, here=here):
+            def _(g, part=part, first=first, wide=wide, here=here):
                 rows = pl.ds(pl.multiple_of(g * GROUP, GROUP), GROUP)
-                kv = part[rows, first : first + WIDE] * scale_ref[rows, :]
+                kv = part[rows, first : first + wide] * scale_ref[rows, :]
                 keep = keep_ref[pl.ds(pl.multiple_of(g * 8, 8), 8), here][:1]
                 rh, rl = split(residual(kv, keep))
                 high_ref[rows, here] = rh
                 low_ref[rows, here] = rl
 
-            for cols in [slice(c, c + 128) for c in range(at, at + WIDE, 128)]:
+            for cols in [slice(c, c + 128) for c in range(at, at + wide, 128)]:
                 rh = high_ref[:, cols]
                 both = lax.dot_general(
                     rh,
@@ -198,7 +197,7 @@
                 )
                 cross = both[:, 128:]
                 gram_ref[cols, :] = both[:, :128] + (cross + cross.T)
-            at += WIDE
+            at += wide
 
 
 def inverse_factors(grams):
@@ -336,7 +335,7 @@
     deep2, deep1, plane = barrier((deep2, deep1, plane))
     deep3 = send(deep1, "z", 1)
     depth = multiply(depth, (deep2,), 2)
-    return (*plane3, deep3), (plane, depth), early
+    return plane3, deep3, plane, depth, early
 
 
 def shards(hidden, row_scale, key_value_weight, outlier, sketch_sign_flags):
@@ -367,7 +366,6 @@
     joined = lambda *lists: jnp.concatenate([i for indices in lists for i in indices])
     plane_at = [joined(i) for i in plane_index]
     deep_at = [joined(i) for i in deep_index]
-    last_at = joined(plane_index[3], deep_index[3])
     scale = row_scale[:, None]
     keep = jnp.repeat(jnp.repeat((1 - outlier).astype(F32), kv_cols, axis=1), 8, axis=0)
 
@@ -382,12 +380,15 @@
     deep = lax.all_gather(own[:, :DEEP], "seq", axis=0, tiled=True)
     own, _ = lax.optimization_barrier((own[:, DEEP:], own))
     rest = lax.all_gather(own, ("batch", "seq"), axis=0).reshape(RING, seq, quarter, cols - rest_at)
-    early = (start, scale, keep, last_at)
-    (a3, b3, c3), (ab, c), (start, scale, keep, last_at) = gather_blocks(flat[:, :PERMUTED], deep, multiply, early)
+    early = (start, scale, keep)
+    plane3, deep3, ab, c, (start, scale, keep) = gather_blocks(flat[:, :PERMUTED], deep, multiply, early)
     rest, ab, c = lax.optimization_barrier((rest, ab, c))
     cd = accumulate_all(hidden, rest)
-
-    last = [(a3, 1), (b3, 1), (c3, RING)]
+    plane3, ab, cd = lax.optimization_barrier((plane3, ab, cd))
+    ab = multiply(ab, plane3, 3)
+    deep3, ab, c = lax.optimization_barrier((deep3, ab, c))
+
+    last = [(deep3, RING)]
     specs = block_specs(tokens, last)
     whole = lambda *shape: pl.BlockSpec(shape, lambda j, ix: (0,) * len(shape))
     high, low, gram = pl.pallas_call(
@@ -399,7 +400,7 @@
             + [whole(tokens, t.shape[1]) for t in (ab, c, cd)]
             + [whole(tokens, 1), whole(8 * groups, cols)],
             out_specs=[whole(tokens, cols), whole(tokens, cols), whole(128 * pairs, 128)],
-            scratch_shapes=[pltpu.VMEM(ab.shape, F32), pltpu.VMEM(c.shape, F32)],
+            scratch_shapes=[pltpu.VMEM(c.shape, F32)],
         ),
         out_shape=[
             jax.ShapeDtypeStruct((tokens, cols), BF16),
@@ -409,7 +410,7 @@
         compiler_params=pltpu.CompilerParams(vmem_limit_bytes=VMEM_LIMIT, dimension_semantics=("arbitrary",)),
         name="project",
         cost_estimate=cost(tokens, last),
-    )(last_at, *block_operands(hidden, last), ab, c, cd, scale, keep)
+    )(deep_at[3], *block_operands(hidden, last), ab, c, cd, scale, keep)
 
     pieces = lax.all_to_all(gram, "seq", 0, 0, tiled=True)
     piece = jnp.sum(pieces.reshape(seq, 128 * pairs // seq, 128), axis=0)

time: 237 us -> 248 us (1.046)
  Pallas kernels: 97.9 us -> 108 us
  waiting for transfers between devices: 53.6 us -> 50.8 us
    ppermute x10, waiting for transfers between devices: 28.4 us -> 50.7 us  [send(): return lax.ppermute(v, ('head', 'seq'), plane_pairs(axis, which))]
    pallas_call x6 -> x7, Pallas kernels: 44.3 us -> 59.1 us  [accumulate(): pl.pallas_call(functools.partial(accumulate_kernel, [parts for _, parts i...]
    ppermute x3, waiting for transfers between devices: 10.3 us -> 0.01 us  [send(): return lax.ppermute(v, ('batch', 'head'), depth_pairs(which))]
    all_gather x1, waiting for transfers between devices: 9.59 us -> 0.01 us  [shards(): lax.all_gather(own, ('batch', 'seq'), axis=0)]
    all_gather x1, waiting for transfers between devices: 4.58 us -> 0.01 us  [shards(): deep = lax.all_gather(own[:, :DEEP], 'seq', axis=0, tiled=True)]
    pallas_call x1, Pallas kernels: 16.3 us -> 12.8 us  [shards(): pl.pallas_call(project_kernel, grid_spec=pltpu.PrefetchScalarGridSpec(num...]
  transfers between devices with their start and end apart: 15 -> 15, of which waited for: 10 -> 8; matrix products, arithmetic and copies ran while one was open for 5% -> 6% of each run, Pallas kernels for 29% -> 34%
where the time goes in v5:
time: 248 us; the launch traced here: 247 us
  Pallas kernels  108 us (44%)
  waiting for transfers between devices  50.8 us (20%)
  blocking collectives  31.9 us (13%)
  starting transfers between devices  23.8 us (10%)
  between operations  14.2 us (6%)
  other arithmetic  10.3 us (4%)
  local copies, waits for them, and re-layouts  8.08 us (3%)
    pallas_call x7, Pallas kernels, accumulate(): pl.pallas_call(functools.partial(accumulate_kernel, [parts for _, parts i...  59.1 us
    ppermute x10, waiting for transfers between devices, send(): return lax.ppermute(v, ('head', 'seq'), plane_pairs(axis, which))  50.7 us
    all_to_all x1, blocking collectives, shards(): pieces = lax.all_to_all(gram, 'seq', 0, 0, tiled=True)  17.7 us
    ppermute x10, starting transfers between devices, send(): return lax.ppermute(v, ('head', 'seq'), plane_pairs(axis, which))  15.9 us
    all_to_all x1, blocking collectives, shards(): lax.all_to_all(jnp.broadcast_to(piece, (seq,) + piece.shape), 'seq', 0, 0)  14.2 us
    pallas_call x1, Pallas kernels, accumulate_all(): pl.pallas_call(accumulate_all_kernel, grid=(seq // 2,), in_specs=[pl.Bloc...  12.9 us
    pallas_call x1, Pallas kernels, shards(): pl.pallas_call(project_kernel, grid_spec=pltpu.PrefetchScalarGridSpec(num...  12.8 us
    pallas_call x1, Pallas kernels, shards(): pl.pallas_call(functools.partial(factor_kernel, root_length), out_shape=[...  12.2 us
  transfers between devices with their start and end apart: 15, of which 8 were waited for; matrix products, arithmetic and copies ran while one was open for 6% of the time, Pallas kernels for 34%

profile of v5, /device:TPU:0, one launch (start us, length us, event | category | flops | bytes accessed | tf_op | source)
XLA Modules:
  0.0 247.3 jit_solution(11902822101525053812)
XLA Ops:
  7.2 0.0 all-gather.4.cloned.1.call-start
  7.2 2.1 copy.10
  9.3 0.1 slice.23
  9.4 0.7 constant_dynamic-slice_fusion
  10.0 0.0 all-gather.4.cloned.1.call-update
  10.1 0.0 all-gather.6.cloned.1.call-start
  10.1 0.1 fusion.4
  10.2 0.0 copy-start.6
  10.2 1.7 collective-permute-start
  11.9 1.6 collective-permute-start.1
  13.5 7.4 %collective-permute-done = f32[256,640]{1,0:T(8,128)S(1)} collective-permute-done((f32[256,640]{1,0:T(8,128)S(1)}, f32[256,640]{1,0:T(8,128)S(1)}, u32[]{:S(2)}, u32[]{:S(2)}) %collective-permute-start) | collective-permute-done | bytes 655392 | tf_op jit(solution)/shard_map/ppermute | solution.py:303
  20.9 1.6 collective-permute-done.1
  22.5 0.2 pad_maximum_fusion.2
  22.7 2.2 collective-permute-start.2
  24.8 3.0 %collective-permute-start.3 = (f32[512,640]{1,0:T(8,128)S(1)}, f32[512,640]{1,0:T(8,128)}, u32[]{:S(2)}, u32[]{:S(2)}) collective-permute-start(f32[512,640]{1,0:T(8,128)S(1)} %get-tuple-element.55), channel_id=1, source_target_pairs={{0,3},{1,2},{2,1},{3,0},{4,7},{5,6},{6,5},{7,4},{8,11},{9,10},{10,... | collective-permute-start | bytes 3932168 | tf_op jit(solution)/shard_map/ppermute | solution.py:303
  27.8 0.7 dynamic-slice.1
  28.5 0.0 all-gather.6.cloned.1.call-update
  28.5 1.0 add_convert_fusion
  29.5 0.2 copy.8
  29.7 1.0 pad_maximum_fusion.4.sign_ref
  30.7 11.2 %start.1.start_ref = f32[8,128,128]{2,1,0:T(8,128)} custom-call(f32[8,128,128]{2,1,0:T(8,128)} %pad_maximum_fusion.4.sign_ref), custom_call_target="tpu_custom_call" | custom-call | flops 100000000 | bytes 1000000 | tf_op jit(solution)/shard_map/start/pallas_call | solution.py:351
  41.9 0.1 broadcast_in_dim.13
  42.0 0.7 broadcast_bitcast_fusion.keep_ref
  42.7 0.5 collective-permute-done.2
  43.3 1.9 collective-permute-done.3
  45.2 3.1 %pad_maximum_fusion.refs_2_ = f32[1024,640]{1,0:T(8,128)} fusion(f32[512,640]{1,0:T(8,128)} %collective-permute-done.2, f32[512,640]{1,0:T(8,128)S(1)} %get-tuple-element.54), kind=kLoop, calls=%fused_computation | loop fusion | flops 655360 | bytes 5242880 | tf_op jit(solution)/shard_map/concatenate | solution.py:308
  48.2 3.0 %pad_maximum_fusion.1.refs_4_ = f32[1024,640]{1,0:T(8,128)} fusion(f32[512,640]{1,0:T(8,128)} %collective-permute-done.3, f32[512,640]{1,0:T(8,128)S(1)} %get-tuple-element.55), kind=kLoop, calls=%fused_computation.1 | loop fusion | flops 655360 | bytes 5242880 | tf_op jit(solution)/shard_map/concatenate | solution.py:308
  51.2 0.3 collective-permute-start.5
  51.5 0.7 collective-permute-start.6
  52.3 0.7 concatenate.32.refs_0_
  52.9 9.5 %plane0.1.refs_5_ = f32[512,640]{1,0:T(8,128)} custom-call(s32[8]{0:T(128)} %concatenate.32.refs_0_, f32[512,8192]{1,0:T(8,128)} %x3.1, f32[1024,640]{1,0:T(8,128)} %pad_maximum_fusion.refs_2_, f32[512,8192]{1,0:T(8,128)} %x3.1, f32[1024,640]{1,0:T(8,128)} %pad_maximum_fusion.1.refs_4_), custom_call_target="tpu_custom_call" | custom-call | flops 4026531840 | bytes 9437184 | tf_op jit(solution)/shard_map/plane0/pallas_call | solution.py:112
  62.4 1.8 collective-permute-start.4
  64.2 0.5 fusion.2.refs_0_
  64.7 6.2 %deep0.1.refs_6_ = f32[512,256]{1,0:T(8,128)} custom-call(s32[16]{0:T(128)} %fusion.2.refs_0_, f32[512,8192]{1,0:T(8,128)} %x3.1, f32[512,8192]{1,0:T(8,128)} %x3.1, f32[512,8192]{1,0:T(8,128)} %x3.1, f32[512,8192]{1,0:T(8,128)} %x3.1, f32[2048,256]{1,0:T(8,128)} %all-gather.4.cloned.1.call-done.refs_5_), custom_call_target="tpu_custom_call" | custom-call | flops 1610612736 | bytes 6291456 | tf_op jit(solution)/shard_map/deep0/pallas_call | solution.py:112
  70.9 14.3 %collective-permute-done.5.refs_2_ = f32[1024,640]{1,0:T(8,128)S(1)} collective-permute-done((f32[1024,640]{1,0:T(8,128)}, f32[1024,640]{1,0:T(8,128)S(1)}, u32[]{:S(2)}, u32[]{:S(2)}) %collective-permute-start.5) | collective-permute-done | bytes 2621472 | tf_op jit(solution)/shard_map/ppermute | solution.py:303
  85.2 0.8 collective-permute-done.6.refs_4_
  85.9 2.0 collective-permute-start.8
  88.0 1.8 collective-permute-start.9
  89.7 0.7 concatenate.33.refs_0_
  90.4 10.1 %plane1.1.refs_5_ = f32[512,640]{1,0:T(8,128)} custom-call(s32[8]{0:T(128)} %concatenate.33.refs_0_, f32[512,8192]{1,0:T(8,128)} %x3.1, f32[1024,640]{1,0:T(8,128)} %copy-done.3, f32[512,8192]{1,0:T(8,128)} %x3.1, f32[1024,640]{1,0:T(8,128)} %collective-permute-done.6.refs_4_, f32[512,640]{1,0:T(8,128)} %plane0.1.refs_5_), custom_call_target="tpu_custom_call" | custom-call | flops 4026531840 | bytes 9437184 | tf_op jit(solution)/shard_map/plane1/pallas_call | solution.py:112
  100.5 0.0 collective-permute-done.4.refs_5_
  100.5 3.0 %collective-permute-start.7 = (f32[2048,256]{1,0:T(8,128)}, f32[2048,256]{1,0:T(8,128)}, u32[]{:S(2)}, u32[]{:S(2)}) collective-permute-start(f32[2048,256]{1,0:T(8,128)} %all-gather.4.cloned.1.call-done.refs_5_), channel_id=1, source_target_pairs={{0,96},{16,48},{32,64},{48,16},{64,32},{80,112},{96,0},{112,80},{1... | collective-permute-start | bytes 6291464 | tf_op jit(solution)/shard_map/ppermute | solution.py:302
  103.4 0.6 fusion.1.refs_0_
  104.0 6.7 %deep1.1.refs_6_ = f32[512,256]{1,0:T(8,128)} custom-call(s32[16]{0:T(128)} %fusion.1.refs_0_, f32[512,8192]{1,0:T(8,128)} %x3.1, f32[512,8192]{1,0:T(8,128)} %x3.1, f32[512,8192]{1,0:T(8,128)} %x3.1, f32[512,8192]{1,0:T(8,128)} %x3.1, f32[2048,256]{1,0:T(8,128)} %collective-permute-done.4.refs_5_, f32[512,256]{1,0:T(8,128)} %deep0.1.refs_6_), custom_call_target="tpu_custom_call" | custom-call | flops 1610612736 | bytes 6291456 | tf_op jit(solution)/shard_map/deep1/pallas_call | solution.py:112
  110.7 20.7 %collective-permute-done.8.refs_2_ = f32[1024,640]{1,0:T(8,128)} collective-permute-done((f32[1024,640]{1,0:T(8,128)}, f32[1024,640]{1,0:T(8,128)}, u32[]{:S(2)}, u32[]{:S(2)}) %collective-permute-start.8) | collective-permute-done | bytes 2621472 | tf_op jit(solution)/shard_map/ppermute | solution.py:303
  131.4 3.6 %collective-permute-done.9.refs_4_ = f32[1024,640]{1,0:T(8,128)} collective-permute-done((f32[1024,640]{1,0:T(8,128)}, f32[1024,640]{1,0:T(8,128)}, u32[]{:S(2)}, u32[]{:S(2)}) %collective-permute-start.9) | collective-permute-done | bytes 2621472 | tf_op jit(solution)/shard_map/ppermute | solution.py:303
  135.0 0.5 collective-permute-start.11
  135.4 2.1 collective-permute-start.12
  137.5 0.6 concatenate.34.refs_0_
  138.2 10.1 %plane2.1.refs_5_ = f32[512,640]{1,0:T(8,128)} custom-call(s32[8]{0:T(128)} %concatenate.34.refs_0_, f32[512,8192]{1,0:T(8,128)} %x3.1, f32[1024,640]{1,0:T(8,128)} %collective-permute-done.8.refs_2_, f32[512,8192]{1,0:T(8,128)} %x3.1, f32[1024,640]{1,0:T(8,128)} %collective-permute-done.9.refs_4_, f32[512,640]{1,0:T(8,128)} %plane1.1.refs_5_), custom_call_target="tpu_custom_call" | custom-call | flops 4026531840 | bytes 9437184 | tf_op jit(solution)/shard_map/plane2/pallas_call | solution.py:112
  148.3 0.0 collective-permute-done.7.refs_5_
  148.3 3.1 %collective-permute-start.10 = (f32[2048,256]{1,0:T(8,128)}, f32[2048,256]{1,0:T(8,128)}, u32[]{:S(2)}, u32[]{:S(2)}) collective-permute-start(f32[2048,256]{1,0:T(8,128)} %collective-permute-done.4.refs_5_), channel_id=1, source_target_pairs={{0,96},{16,48},{32,64},{48,16},{64,32},{80,112},{96,0},{112,80},{1... | collective-permute-start | bytes 6291464 | tf_op jit(solution)/shard_map/ppermute | solution.py:302
  151.4 0.6 concatenate.35.refs_0_
  152.1 0.5 fusion.refs_0_
  152.6 0.5 fusion.3.index_ref
  153.1 0.9 copy.9.scale_ref
  154.0 6.6 %deep2.1.depth_ref = f32[512,256]{1,0:T(8,128)} custom-call(s32[16]{0:T(128)} %fusion.refs_0_, f32[512,8192]{1,0:T(8,128)} %x3.1, f32[512,8192]{1,0:T(8,128)} %x3.1, f32[512,8192]{1,0:T(8,128)} %x3.1, f32[512,8192]{1,0:T(8,128)} %x3.1, f32[2048,256]{1,0:T(8,128)} %collective-permute-done.7.refs_5_, f32[512,256]{1,0:T(8,128)} %deep1.1.refs_6_), custom_call_target="tpu_custom_call" | custom-call | flops 1610612736 | bytes 6291456 | tf_op jit(solution)/shard_map/deep2/pallas_call | solution.py:112
  160.5 12.9 %rest.1.rest_ref = f32[512,128]{1,0:T(8,128)} custom-call(f32[512,8192]{1,0:T(8,128)} %x3.1, f32[4,16,128,128]{3,2,1,0:T(8,128)} %bitcast.45), custom_call_target="tpu_custom_call" | custom-call | flops 3221225472 | bytes 20971520 | tf_op jit(solution)/shard_map/rest/pallas_call | solution.py:141
  173.4 0.0 collective-permute-done.11.refs_2_
  173.4 10.0 %plane3.1.plane_ref = f32[512,640]{1,0:T(8,128)} custom-call(s32[8]{0:T(128)} %concatenate.35.refs_0_, f32[512,8192]{1,0:T(8,128)} %x3.1, f32[1024,640]{1,0:T(8,128)} %collective-permute-done.11.refs_2_, f32[512,8192]{1,0:T(8,128)} %x3.1, f32[1024,640]{1,0:T(8,128)} %collective-permute-done.12.refs_4_, f32[512,640]{1,0:T(8,128)} %plane2.1.refs_5_), custom_call_target="tpu_custom_call" | custom-call | flops 4026531840 | bytes 9437184 | tf_op jit(solution)/shard_map/plane3/pallas_call | solution.py:112
  183.4 12.8 %project.1 = (bf16[512,1024]{1,0:T(8,128)(2,1)}, bf16[512,1024]{1,0:T(8,128)(2,1)}, f32[1024,128]{1,0:T(8,128)}) custom-call(s32[16]{0:T(128)} %fusion.3.index_ref, f32[512,8192]{1,0:T(8,128)} %x3.1, f32[512,8192]{1,0:T(8,128)} %x3.1, f32[512,8192]{1,0:T(8,128)} %x3.1, f32[512,8192]{1,0:T(8,128)} %x3.1, f32[2048,256]{1,0:T(8,128)} %collective-permute-done.10.w, ...), custom_call_target="tpu_custom_call" | custom-call | flops 1610612736 | bytes 6291456 | tf_op jit(solution)/shard_map/project/pallas_call | solution.py:394
  196.2 17.7 %all_to_all.14 = f32[16,64,128]{2,1,0:T(8,128)S(1)} all-to-all(f32[16,64,128]{2,1,0:T(8,128)} %bitcast.48), channel_id=1, replica_groups=mesh['batch'=4,'head'=2,'seq'=16] {'seq'}, dimensions={0} | all-to-all | bytes 1048576 | tf_op jit(solution)/shard_map/all_to_all | solution.py:415
  214.0 14.2 %all_to_all.15 = f32[16,64,128]{2,1,0:T(8,128)S(1)} all-to-all(f32[16,64,128]{2,1,0:T(8,128)S(1)} %broadcast_in_dim.15), channel_id=1, replica_groups=mesh['batch'=4,'head'=2,'seq'=16] {'seq'}, dimensions={0} | all-to-all | bytes 1048576 | tf_op jit(solution)/shard_map/all_to_all | solution.py:417
  228.2 12.2 %factor.1 = (bf16[4,512,128]{2,1,0:T(8,128)(2,1)}, f32[4,128,128]{2,1,0:T(8,128)}) custom-call(f32[1024,128]{1,0:T(8,128)S(1)} %bitcast.42, f32[8,128,128]{2,1,0:T(8,128)S(1)} %copy-done, bf16[512,1024]{1,0:T(8,128)(2,1)S(1)} %copy-done.1, bf16[512,1024]{1,0:T(8,128)(2,1)S(1)} %copy-done.2), custom_call_target="tpu_custom_call" | custom-call | flops 1000000000 | bytes 4194304 | tf_op jit(solution)/shard_map/factor/pallas_call | solution.py:419
  (20 shorter events, 0.1 us)
Async XLA Ops:
  7.2 55.2 %all-gather.4.cloned.1.call-start = ((), (), s32[]{:S(2)}) async-start(), calls=%async_computation.2 | async-start | bytes 2228224 | tf_op jit(solution)/shard_map/all_gather | solution.py:380
  10.1 150.5 %all-gather.6.cloned.1.call-start = ((), (), s32[]{:S(2)}) async-start(), calls=%async_computation.3 | async-start | bytes 4259840 | tf_op jit(solution)/shard_map/all_gather | solution.py:382
  10.2 19.5 %copy-start.6 = (s32[8,4]{0,1:T(4,128)S(1)}, s32[8,4]{0,1:T(4,128)}, u32[]{:S(2)}) copy-start(s32[8,4]{0,1:T(4,128)} %param.8) | copy-start | bytes 388
  10.2 10.7 %collective-permute-start = (f32[256,640]{1,0:T(8,128)S(1)}, f32[256,640]{1,0:T(8,128)S(1)}, u32[]{:S(2)}, u32[]{:S(2)}) collective-permute-start(f32[256,640]{1,0:T(8,128)S(1)} %get-tuple-element.50), channel_id=1, source_target_pairs={{0,4},{1,5},{2,6},{3,7},{4,0},{5,1},{6,2},{7,3},{8,12},{9,13},{10,... | collective-permute-start | bytes 1966088 | tf_op jit(solution)/shard_map/ppermute | solution.py:303
  11.9 10.6 %collective-permute-start.1 = (f32[256,640]{1,0:T(8,128)S(1)}, f32[256,640]{1,0:T(8,128)S(1)}, u32[]{:S(2)}, u32[]{:S(2)}) collective-permute-start(f32[256,640]{1,0:T(8,128)S(1)} %get-tuple-element.51), channel_id=1, source_target_pairs={{0,1},{1,0},{2,3},{3,2},{4,5},{5,4},{6,7},{7,6},{8,9},{9,8},{10,11... | collective-permute-start | bytes 1966088 | tf_op jit(solution)/shard_map/ppermute | solution.py:303
  22.7 20.6 %collective-permute-start.2 = (f32[512,640]{1,0:T(8,128)S(1)}, f32[512,640]{1,0:T(8,128)}, u32[]{:S(2)}, u32[]{:S(2)}) collective-permute-start(f32[512,640]{1,0:T(8,128)S(1)} %get-tuple-element.54), channel_id=1, source_target_pairs={{0,12},{1,13},{2,14},{3,15},{4,8},{5,9},{6,10},{7,11},{8,4},{9,5},... | collective-permute-start | bytes 3932168 | tf_op jit(solution)/shard_map/ppermute | solution.py:303
  24.8 20.3 %collective-permute-start.3 = (f32[512,640]{1,0:T(8,128)S(1)}, f32[512,640]{1,0:T(8,128)}, u32[]{:S(2)}, u32[]{:S(2)}) collective-permute-start(f32[512,640]{1,0:T(8,128)S(1)} %get-tuple-element.55), channel_id=1, source_target_pairs={{0,3},{1,2},{2,1},{3,0},{4,7},{5,6},{6,5},{7,4},{8,11},{9,10},{10,... | collective-permute-start | bytes 3932168 | tf_op jit(solution)/shard_map/ppermute | solution.py:303
  51.2 34.0 %collective-permute-start.5 = (f32[1024,640]{1,0:T(8,128)}, f32[1024,640]{1,0:T(8,128)S(1)}, u32[]{:S(2)}, u32[]{:S(2)}) collective-permute-start(f32[1024,640]{1,0:T(8,128)} %pad_maximum_fusion.refs_2_), channel_id=1, source_target_pairs={{0,1},{1,0},{2,3},{3,2},{4,5},{5,4},{6,7},{7,6},{8,9},{9,8},{10,11... | collective-permute-start | bytes 7864328 | tf_op jit(solution)/shard_map/ppermute | solution.py:303
  51.5 34.4 %collective-permute-start.6 = (f32[1024,640]{1,0:T(8,128)}, f32[1024,640]{1,0:T(8,128)}, u32[]{:S(2)}, u32[]{:S(2)}) collective-permute-start(f32[1024,640]{1,0:T(8,128)} %pad_maximum_fusion.1.refs_4_), channel_id=1, source_target_pairs={{0,4},{1,5},{2,6},{3,7},{4,0},{5,1},{6,2},{7,3},{8,12},{9,13},{10,... | collective-permute-start | bytes 7864328 | tf_op jit(solution)/shard_map/ppermute | solution.py:303
  62.4 38.1 %collective-permute-start.4 = (f32[2048,256]{1,0:T(8,128)}, f32[2048,256]{1,0:T(8,128)}, u32[]{:S(2)}, u32[]{:S(2)}) collective-permute-start(f32[2048,256]{1,0:T(8,128)} %all-gather.4.cloned.1.call-done.refs_5_), channel_id=1, source_target_pairs={{0,32},{16,112},{32,0},{48,80},{64,96},{80,48},{96,64},{112,16},{1... | collective-permute-start | bytes 6291464 | tf_op jit(solution)/shard_map/ppermute | solution.py:302
  85.2 5.3 %copy-start.3 = (f32[1024,640]{1,0:T(8,128)}, f32[1024,640]{1,0:T(8,128)S(1)}, u32[]{:S(2)}) copy-start(f32[1024,640]{1,0:T(8,128)S(1)} %collective-permute-done.5.refs_2_) | copy-start | bytes 7864324
  85.9 45.5 %collective-permute-start.8 = (f32[1024,640]{1,0:T(8,128)}, f32[1024,640]{1,0:T(8,128)}, u32[]{:S(2)}, u32[]{:S(2)}) collective-permute-start(f32[1024,640]{1,0:T(8,128)} %pad_maximum_fusion.refs_2_), channel_id=1, source_target_pairs={{0,3},{1,2},{2,1},{3,0},{4,7},{5,6},{6,5},{7,4},{8,11},{9,10},{10,... | collective-permute-start | bytes 7864328 | tf_op jit(solution)/shard_map/ppermute | solution.py:303
  88.0 47.0 %collective-permute-start.9 = (f32[1024,640]{1,0:T(8,128)}, f32[1024,640]{1,0:T(8,128)}, u32[]{:S(2)}, u32[]{:S(2)}) collective-permute-start(f32[1024,640]{1,0:T(8,128)} %pad_maximum_fusion.1.refs_4_), channel_id=1, source_target_pairs={{0,12},{1,13},{2,14},{3,15},{4,8},{5,9},{6,10},{7,11},{8,4},{9,5},... | collective-permute-start | bytes 7864328 | tf_op jit(solution)/shard_map/ppermute | solution.py:303
  100.5 47.8 %collective-permute-start.7 = (f32[2048,256]{1,0:T(8,128)}, f32[2048,256]{1,0:T(8,128)}, u32[]{:S(2)}, u32[]{:S(2)}) collective-permute-start(f32[2048,256]{1,0:T(8,128)} %all-gather.4.cloned.1.call-done.refs_5_), channel_id=1, source_target_pairs={{0,96},{16,48},{32,64},{48,16},{64,32},{80,112},{96,0},{112,80},{1... | collective-permute-start | bytes 6291464 | tf_op jit(solution)/shard_map/ppermute | solution.py:302
  104.0 31.0 %copy-start.4 = (f32[1024,640]{1,0:T(8,128)S(1)}, f32[1024,640]{1,0:T(8,128)}, u32[]{:S(2)}) copy-start(f32[1024,640]{1,0:T(8,128)} %copy-done.3) | copy-start | bytes 7864324
  135.0 38.4 %collective-permute-start.11 = (f32[1024,640]{1,0:T(8,128)S(1)}, f32[1024,640]{1,0:T(8,128)}, u32[]{:S(2)}, u32[]{:S(2)}) collective-permute-start(f32[1024,640]{1,0:T(8,128)S(1)} %copy-done.4), channel_id=1, source_target_pairs={{0,3},{1,2},{2,1},{3,0},{4,7},{5,6},{6,5},{7,4},{8,11},{9,10},{10,... | collective-permute-start | bytes 7864328 | tf_op jit(solution)/shard_map/ppermute | solution.py:303
  135.4 37.9 %collective-permute-start.12 = (f32[1024,640]{1,0:T(8,128)}, f32[1024,640]{1,0:T(8,128)}, u32[]{:S(2)}, u32[]{:S(2)}) collective-permute-start(f32[1024,640]{1,0:T(8,128)} %collective-permute-done.6.refs_4_), channel_id=1, source_target_pairs={{0,12},{1,13},{2,14},{3,15},{4,8},{5,9},{6,10},{7,11},{8,4},{9,5},... | collective-permute-start | bytes 7864328 | tf_op jit(solution)/shard_map/ppermute | solution.py:303
  138.2 14.9 %copy-start.5 = (f32[512]{0:T(512)S(1)}, f32[512]{0:T(512)}, u32[]{:S(2)}) copy-start(f32[512]{0:T(512)} %param.6) | copy-start | bytes 6148
  148.3 35.1 %collective-permute-start.10 = (f32[2048,256]{1,0:T(8,128)}, f32[2048,256]{1,0:T(8,128)}, u32[]{:S(2)}, u32[]{:S(2)}) collective-permute-start(f32[2048,256]{1,0:T(8,128)} %collective-permute-done.4.refs_5_), channel_id=1, source_target_pairs={{0,96},{16,48},{32,64},{48,16},{64,32},{80,112},{96,0},{112,80},{1... | collective-permute-start | bytes 6291464 | tf_op jit(solution)/shard_map/ppermute | solution.py:302
  196.2 32.0 %copy-start = (f32[8,128,128]{2,1,0:T(8,128)S(1)}, f32[8,128,128]{2,1,0:T(8,128)}, u32[]{:S(2)}) copy-start(f32[8,128,128]{2,1,0:T(8,128)} %start.1.start_ref) | copy-start | bytes 1572868
  196.2 32.0 %copy-start.1 = (bf16[512,1024]{1,0:T(8,128)(2,1)S(1)}, bf16[512,1024]{1,0:T(8,128)(2,1)}, u32[]{:S(2)}) copy-start(bf16[512,1024]{1,0:T(8,128)(2,1)} %get-tuple-element.96.high_ref) | copy-start | bytes 3145732
  196.2 32.0 %copy-start.2 = (bf16[512,1024]{1,0:T(8,128)(2,1)S(1)}, bf16[512,1024]{1,0:T(8,128)(2,1)}, u32[]{:S(2)}) copy-start(bf16[512,1024]{1,0:T(8,128)(2,1)} %get-tuple-element.97.low_ref) | copy-start | bytes 3145732
Sparse Core Ops, SparseCore 0:
  10.7 49.1 all-gather.3
  62.8 71.9 all-gather.5

commit v6 on v4

--- a/solution.py
+++ b/solution.py
@@ -379,9 +379,9 @@
     quarter = rows // RING
     rest_at = PERMUTED + DEEP
     own = lax.dynamic_slice_in_dim(flat[:, PERMUTED:], plane * quarter, quarter, 0)
-    deep = lax.all_gather(own[:, :DEEP], "seq", axis=0, tiled=True)
-    own, _ = lax.optimization_barrier((own[:, DEEP:], own))
-    rest = lax.all_gather(own, ("batch", "seq"), axis=0).reshape(RING, seq, quarter, cols - rest_at)
+    deep = jnp.broadcast_to(own[:, :DEEP], (seq, quarter, DEEP))
+    deep = lax.all_to_all(deep, "seq", 0, 0).reshape(seq * quarter, DEEP)
+    rest = lax.all_gather(own[:, DEEP:], ("batch", "seq"), axis=0).reshape(RING, seq, quarter, cols - rest_at)
     early = (start, scale, keep, last_at)
     (a3, b3, c3), (ab, c), (start, scale, keep, last_at) = gather_blocks(flat[:, :PERMUTED], deep, multiply, early)
     rest, ab, c = lax.optimization_barrier((rest, ab, c))

time: 237 us -> 251 us (1.059)
  starting transfers between devices: 22.8 us -> 30.4 us
  waiting for transfers between devices: 53.6 us -> 58.1 us
    ppermute x10, waiting for transfers between devices: 28.4 us -> 55.1 us  [send(): return lax.ppermute(v, ('head', 'seq'), plane_pairs(axis, which))]
    all_gather x2 -> x1, waiting for transfers between devices: 14.2 us -> 0.01 us  [shards(): lax.all_gather(own[:, DEEP:], ('batch', 'seq'), axis=0)]
    ppermute x3, waiting for transfers between devices: 10.3 us -> 2.9 us  [send(): return lax.ppermute(v, ('batch', 'head'), depth_pairs(which))]
    all_to_all x0 -> x1, starting transfers between devices: none -> 6.5 us  [shards(): deep = lax.all_to_all(deep, 'seq', 0, 0).reshape(seq * quarter, DEEP)]
  transfers between devices with their start and end apart: 15 -> 15, of which waited for: 10 -> 6; matrix products, arithmetic and copies ran while one was open for 5% -> 6% of each run, Pallas kernels for 29% -> 28%
where the time goes in v6:
time: 251 us
  Pallas kernels  98 us (39%)
  waiting for transfers between devices  58.1 us (23%)
  starting transfers between devices  30.4 us (12%)
  blocking collectives  29.3 us (12%)
  between operations  14.2 us (6%)
  local copies, waits for them, and re-layouts  11 us (4%)
  other arithmetic  9.49 us (4%)
    ppermute x10, waiting for transfers between devices, send(): return lax.ppermute(v, ('head', 'seq'), plane_pairs(axis, which))  55.1 us
    pallas_call x6, Pallas kernels, accumulate(): pl.pallas_call(functools.partial(accumulate_kernel, [parts for _, parts i...  44.4 us
    pallas_call x1, Pallas kernels, shards(): pl.pallas_call(project_kernel, grid_spec=pltpu.PrefetchScalarGridSpec(num...  16.3 us
    all_to_all x1, blocking collectives, shards(): pieces = lax.all_to_all(gram, 'seq', 0, 0, tiled=True)  16 us
    ppermute x10, starting transfers between devices, send(): return lax.ppermute(v, ('head', 'seq'), plane_pairs(axis, which))  15.7 us
    pallas_call x1, Pallas kernels, accumulate_all(): pl.pallas_call(accumulate_all_kernel, grid=(seq // 2,), in_specs=[pl.Bloc...  13.8 us
    all_to_all x1, blocking collectives, shards(): lax.all_to_all(jnp.broadcast_to(piece, (seq,) + piece.shape), 'seq', 0, 0)  13.3 us
    pallas_call x1, Pallas kernels, shards(): pl.pallas_call(functools.partial(factor_kernel, root_length), out_shape=[...  12.2 us
  transfers between devices with their start and end apart: 15, of which 6 were waited for; matrix products, arithmetic and copies ran while one was open for 6% of the time, Pallas kernels for 28%

profile of v6, /device:TPU:0, one launch (start us, length us, event | category | flops | bytes accessed | tf_op | source)
XLA Modules:
  0.0 250.5 jit_solution(12839767792690043469)
XLA Ops:
  7.2 0.0 all-gather.3.cloned.1.call-start
  7.2 2.1 copy.10
  9.3 0.1 slice.25
  9.4 0.7 fusion.5
  10.1 0.0 all-gather.3.cloned.1.call-update
  10.1 0.1 fusion.4
  10.2 1.7 collective-permute-start
  11.8 1.6 collective-permute-start.1
  13.4 1.5 broadcast_in_dim.18
  15.0 6.5 %all-to-all-start = ((f32[16,128,256]{2,1,0:T(8,128)}), f32[16,128,256]{2,1,0:T(8,128)}, u32[]{:S(2)}, u32[]{:S(2)}) async-start(f32[16,128,256]{2,1,0:T(8,128)} %broadcast_in_dim.18), calls=%async_computation | async-start | bytes 4194304 | tf_op jit(solution)/shard_map/all_to_all | solution.py:383
  21.5 0.0 copy-start.6
  21.5 0.0 collective-permute-done
  21.5 0.0 copy-start.5
  21.5 0.8 copy-done.5
  22.3 0.0 collective-permute-done.1
  22.3 1.4 pad_maximum_fusion.2
  23.7 0.0 copy-start.8
  23.7 3.2 %collective-permute-start.2 = (f32[512,512]{1,0:T(8,128)S(1)}, f32[512,512]{1,0:T(8,128)}, u32[]{:S(2)}, u32[]{:S(2)}) collective-permute-start(f32[512,512]{1,0:T(8,128)S(1)} %get-tuple-element.47), channel_id=1, source_target_pairs={{0,12},{1,13},{2,14},{3,15},{4,8},{5,9},{6,10},{7,11},{8,4},{9,5},... | collective-permute-start | bytes 3145736 | tf_op jit(solution)/shard_map/ppermute | solution.py:304
  26.9 2.7 %collective-permute-start.3 = (f32[512,512]{1,0:T(8,128)S(1)}, f32[512,512]{1,0:T(8,128)}, u32[]{:S(2)}, u32[]{:S(2)}) collective-permute-start(f32[512,512]{1,0:T(8,128)S(1)} %get-tuple-element.48), channel_id=1, source_target_pairs={{0,3},{1,2},{2,1},{3,0},{4,7},{5,6},{6,5},{7,4},{8,11},{9,10},{10,... | collective-permute-start | bytes 3145736 | tf_op jit(solution)/shard_map/ppermute | solution.py:304
  29.6 0.2 copy.8
  29.8 0.7 concatenate.30.index_ref
  30.5 1.0 pad_maximum_fusion.4.sign_ref
  31.5 11.2 %start.1.start_ref = f32[8,128,128]{2,1,0:T(8,128)} custom-call(f32[8,128,128]{2,1,0:T(8,128)} %pad_maximum_fusion.4.sign_ref), custom_call_target="tpu_custom_call" | custom-call | flops 100000000 | bytes 1000000 | tf_op jit(solution)/shard_map/start/pallas_call | solution.py:352
  42.7 0.1 broadcast_in_dim.16
  42.8 0.7 broadcast_bitcast_fusion.keep_ref
  43.5 17.1 %collective-permute-done.2 = f32[512,512]{1,0:T(8,128)} collective-permute-done((f32[512,512]{1,0:T(8,128)S(1)}, f32[512,512]{1,0:T(8,128)}, u32[]{:S(2)}, u32[]{:S(2)}) %collective-permute-start.2) | collective-permute-done | bytes 1048608 | tf_op jit(solution)/shard_map/ppermute | solution.py:304
  60.6 0.0 collective-permute-done.3
  60.6 2.7 %pad_maximum_fusion.1.refs_4_ = f32[1024,512]{1,0:T(8,128)} fusion(f32[512,512]{1,0:T(8,128)} %collective-permute-done.3, f32[512,512]{1,0:T(8,128)S(1)} %get-tuple-element.48), kind=kLoop, calls=%fused_computation.1 | loop fusion | flops 524288 | bytes 4194304 | tf_op jit(solution)/shard_map/concatenate | solution.py:309
  63.3 2.7 %pad_maximum_fusion.refs_2_ = f32[1024,512]{1,0:T(8,128)} fusion(f32[512,512]{1,0:T(8,128)} %collective-permute-done.2, f32[512,512]{1,0:T(8,128)S(1)} %get-tuple-element.47), kind=kLoop, calls=%fused_computation | loop fusion | flops 524288 | bytes 4194304 | tf_op jit(solution)/shard_map/concatenate | solution.py:309
  66.0 1.5 collective-permute-start.4
  67.6 1.1 collective-permute-start.5
  68.6 0.6 concatenate.33.refs_0_
  69.2 8.0 %plane0.1.refs_5_ = f32[512,512]{1,0:T(8,128)} custom-call(s32[8]{0:T(128)} %concatenate.33.refs_0_, f32[512,8192]{1,0:T(8,128)} %xc3.1, f32[1024,512]{1,0:T(8,128)} %pad_maximum_fusion.refs_2_, f32[512,8192]{1,0:T(8,128)} %xc3.1, f32[1024,512]{1,0:T(8,128)} %pad_maximum_fusion.1.refs_4_), custom_call_target="tpu_custom_call" | custom-call | flops 3221225472 | bytes 8388608 | tf_op jit(solution)/shard_map/plane0/pallas_call | solution.py:112
  77.2 0.0 all-to-all-done
  77.2 2.1 collective-permute-start.8
  79.3 0.6 fusion.2.refs_0_
  79.8 6.4 %deep0.1.refs_6_ = f32[512,256]{1,0:T(8,128)} custom-call(s32[16]{0:T(128)} %fusion.2.refs_0_, f32[512,8192]{1,0:T(8,128)} %xc3.1, f32[512,8192]{1,0:T(8,128)} %xc3.1, f32[512,8192]{1,0:T(8,128)} %xc3.1, f32[512,8192]{1,0:T(8,128)} %xc3.1, f32[2048,256]{1,0:T(8,128)} %bitcast.12.refs_5_), custom_call_target="tpu_custom_call" | custom-call | flops 1610612736 | bytes 6291456 | tf_op jit(solution)/shard_map/deep0/pallas_call | solution.py:112
  86.2 28.6 %collective-permute-done.4.refs_2_ = f32[1024,512]{1,0:T(8,128)} collective-permute-done((f32[1024,512]{1,0:T(8,128)}, f32[1024,512]{1,0:T(8,128)}, u32[]{:S(2)}, u32[]{:S(2)}) %collective-permute-start.4) | collective-permute-done | bytes 2097184 | tf_op jit(solution)/shard_map/ppermute | solution.py:304
  114.9 3.2 %collective-permute-done.5.refs_4_ = f32[1024,512]{1,0:T(8,128)} collective-permute-done((f32[1024,512]{1,0:T(8,128)}, f32[1024,512]{1,0:T(8,128)}, u32[]{:S(2)}, u32[]{:S(2)}) %collective-permute-start.5) | collective-permute-done | bytes 2097184 | tf_op jit(solution)/shard_map/ppermute | solution.py:304
  118.1 2.4 collective-permute-start.6
  120.5 0.0 collective-permute-start.7
  120.5 0.7 concatenate.34.refs_0_
  121.2 8.5 %plane1.1.refs_5_ = f32[512,512]{1,0:T(8,128)} custom-call(s32[8]{0:T(128)} %concatenate.34.refs_0_, f32[512,8192]{1,0:T(8,128)} %xc3.1, f32[1024,512]{1,0:T(8,128)} %collective-permute-done.4.refs_2_, f32[512,8192]{1,0:T(8,128)} %xc3.1, f32[1024,512]{1,0:T(8,128)} %collective-permute-done.5.refs_4_, f32[512,512]{1,0:T(8,128)} %plane0.1.refs_5_), custom_call_target="tpu_custom_call" | custom-call | flops 3221225472 | bytes 8388608 | tf_op jit(solution)/shard_map/plane1/pallas_call | solution.py:112
  129.7 3.3 %collective-permute-start.11 = (f32[2048,256]{1,0:T(8,128)}, f32[2048,256]{1,0:T(8,128)}, u32[]{:S(2)}, u32[]{:S(2)}) collective-permute-start(f32[2048,256]{1,0:T(8,128)} %bitcast.12.refs_5_), channel_id=1, source_target_pairs={{0,96},{16,48},{32,64},{48,16},{64,32},{80,112},{96,0},{112,80},{1... | collective-permute-start | bytes 6291464 | tf_op jit(solution)/shard_map/ppermute | solution.py:303
  132.9 0.6 concatenate.35.refs_0_
  133.5 0.5 fusion.1.refs_0_
  134.1 6.5 %deep1.1.refs_6_ = f32[512,256]{1,0:T(8,128)} custom-call(s32[16]{0:T(128)} %fusion.1.refs_0_, f32[512,8192]{1,0:T(8,128)} %xc3.1, f32[512,8192]{1,0:T(8,128)} %xc3.1, f32[512,8192]{1,0:T(8,128)} %xc3.1, f32[512,8192]{1,0:T(8,128)} %xc3.1, f32[2048,256]{1,0:T(8,128)} %collective-permute-done.8.refs_5_, f32[512,256]{1,0:T(8,128)} %deep0.1.refs_6_), custom_call_target="tpu_custom_call" | custom-call | flops 1610612736 | bytes 6291456 | tf_op jit(solution)/shard_map/deep1/pallas_call | solution.py:112
  140.6 4.9 %collective-permute-done.6.refs_2_ = f32[1024,512]{1,0:T(8,128)S(1)} collective-permute-done((f32[1024,512]{1,0:T(8,128)}, f32[1024,512]{1,0:T(8,128)S(1)}, u32[]{:S(2)}, u32[]{:S(2)}) %collective-permute-start.6) | collective-permute-done | bytes 2097184 | tf_op jit(solution)/shard_map/ppermute | solution.py:304
  145.6 1.3 copy-done.4
  146.9 1.2 collective-permute-done.7.refs_4_
  148.1 0.0 collective-permute-start.10
  148.1 1.6 collective-permute-start.9
  149.7 8.4 %plane2.1.ab_ref = f32[512,512]{1,0:T(8,128)} custom-call(s32[8]{0:T(128)} %concatenate.35.refs_0_, f32[512,8192]{1,0:T(8,128)} %xc3.1, f32[1024,512]{1,0:T(8,128)} %copy-done.4, f32[512,8192]{1,0:T(8,128)} %xc3.1, f32[1024,512]{1,0:T(8,128)} %collective-permute-done.7.refs_4_, f32[512,512]{1,0:T(8,128)} %plane1.1.refs_5_), custom_call_target="tpu_custom_call" | custom-call | flops 3221225472 | bytes 8388608 | tf_op jit(solution)/shard_map/plane2/pallas_call | solution.py:112
  158.1 0.0 collective-permute-done.11.refs_5_
  158.1 2.9 %collective-permute-start.12 = (f32[2048,256]{1,0:T(8,128)}, f32[2048,256]{1,0:T(8,128)}, u32[]{:S(2)}, u32[]{:S(2)}) collective-permute-start(f32[2048,256]{1,0:T(8,128)} %collective-permute-done.8.refs_5_), channel_id=1, source_target_pairs={{0,96},{16,48},{32,64},{48,16},{64,32},{80,112},{96,0},{112,80},{1... | collective-permute-start | bytes 6291464 | tf_op jit(solution)/shard_map/ppermute | solution.py:303
  161.0 0.5 fusion.refs_0_
  161.5 0.9 copy.9.scale_ref
  162.4 6.6 %deep2.1.c_ref = f32[512,256]{1,0:T(8,128)} custom-call(s32[16]{0:T(128)} %fusion.refs_0_, f32[512,8192]{1,0:T(8,128)} %xc3.1, f32[512,8192]{1,0:T(8,128)} %xc3.1, f32[512,8192]{1,0:T(8,128)} %xc3.1, f32[512,8192]{1,0:T(8,128)} %xc3.1, f32[2048,256]{1,0:T(8,128)} %collective-permute-done.11.refs_5_, f32[512,256]{1,0:T(8,128)} %deep1.1.refs_6_), custom_call_target="tpu_custom_call" | custom-call | flops 1610612736 | bytes 6291456 | tf_op jit(solution)/shard_map/deep2/pallas_call | solution.py:112
  168.9 13.8 %rest.1.rest_ref = f32[512,256]{1,0:T(8,128)} custom-call(f32[512,8192]{1,0:T(8,128)} %xc3.1, f32[4,16,128,256]{3,2,1,0:T(8,128)} %bitcast.44), custom_call_target="tpu_custom_call" | custom-call | flops 6442450944 | bytes 25165824 | tf_op jit(solution)/shard_map/rest/pallas_call | solution.py:141
  182.8 2.9 %collective-permute-done.12.wc = f32[2048,256]{1,0:T(8,128)} collective-permute-done((f32[2048,256]{1,0:T(8,128)}, f32[2048,256]{1,0:T(8,128)}, u32[]{:S(2)}, u32[]{:S(2)}) %collective-permute-start.12) | collective-permute-done | bytes 2097184 | tf_op jit(solution)/shard_map/ppermute | solution.py:303
  185.7 16.3 %project.1 = (bf16[512,1024]{1,0:T(8,128)(2,1)}, bf16[512,1024]{1,0:T(8,128)(2,1)}, f32[1024,128]{1,0:T(8,128)}) custom-call(s32[24]{0:T(128)} %concatenate.30.index_ref, f32[512,8192]{1,0:T(8,128)} %xc3.1, f32[1024,512]{1,0:T(8,128)} %collective-permute-done.9.wa, f32[512,8192]{1,0:T(8,128)} %xc3.1, f32[1024,512]{1,0:T(8,128)} %copy-done.3, ...), custom_call_target="tpu_custom_call" | custom-call | flops 4831838208 | bytes 14680064 | tf_op jit(solution)/shard_map/project/pallas_call | solution.py:393
  202.0 16.0 %all_to_all.19 = f32[16,64,128]{2,1,0:T(8,128)S(1)} all-to-all(f32[16,64,128]{2,1,0:T(8,128)} %bitcast.49), channel_id=1, replica_groups=mesh['batch'=4,'head'=2,'seq'=16] {'seq'}, dimensions={0} | all-to-all | bytes 1048576 | tf_op jit(solution)/shard_map/all_to_all | solution.py:414
  218.1 13.3 %all_to_all.20 = f32[16,64,128]{2,1,0:T(8,128)S(1)} all-to-all(f32[16,64,128]{2,1,0:T(8,128)S(1)} %broadcast_in_dim.19), channel_id=1, replica_groups=mesh['batch'=4,'head'=2,'seq'=16] {'seq'}, dimensions={0} | all-to-all | bytes 1048576 | tf_op jit(solution)/shard_map/all_to_all | solution.py:416
  231.5 12.2 %factor.1 = (bf16[4,512,128]{2,1,0:T(8,128)(2,1)}, f32[4,128,128]{2,1,0:T(8,128)}) custom-call(f32[1024,128]{1,0:T(8,128)S(1)} %bitcast.43, f32[8,128,128]{2,1,0:T(8,128)S(1)} %copy-done, bf16[512,1024]{1,0:T(8,128)(2,1)S(1)} %copy-done.1, bf16[512,1024]{1,0:T(8,128)(2,1)S(1)} %copy-done.2), custom_call_target="tpu_custom_call" | custom-call | flops 1000000000 | bytes 4194304 | tf_op jit(solution)/shard_map/factor/pallas_call | solution.py:418
  (22 shorter events, 0.2 us)
Async XLA Ops:
  7.2 161.8 %all-gather.3.cloned.1.call-start = ((), (), s32[]{:S(2)}) async-start(), calls=%async_computation.3 | async-start | bytes 8519680 | tf_op jit(solution)/shard_map/all_gather | solution.py:384
  10.2 11.3 %collective-permute-start = (f32[256,512]{1,0:T(8,128)S(1)}, f32[256,512]{1,0:T(8,128)S(1)}, u32[]{:S(2)}, u32[]{:S(2)}) collective-permute-start(f32[256,512]{1,0:T(8,128)S(1)} %get-tuple-element.43), channel_id=1, source_target_pairs={{0,4},{1,5},{2,6},{3,7},{4,0},{5,1},{6,2},{7,3},{8,12},{9,13},{10,... | collective-permute-start | bytes 1572872 | tf_op jit(solution)/shard_map/ppermute | solution.py:304
  11.8 10.4 %collective-permute-start.1 = (f32[256,512]{1,0:T(8,128)S(1)}, f32[256,512]{1,0:T(8,128)}, u32[]{:S(2)}, u32[]{:S(2)}) collective-permute-start(f32[256,512]{1,0:T(8,128)S(1)} %get-tuple-element.44), channel_id=1, source_target_pairs={{0,1},{1,0},{2,3},{3,2},{4,5},{5,4},{6,7},{7,6},{8,9},{9,8},{10,11... | collective-permute-start | bytes 1572872 | tf_op jit(solution)/shard_map/ppermute | solution.py:304
  15.0 62.2 %all-to-all-start = ((f32[16,128,256]{2,1,0:T(8,128)}), f32[16,128,256]{2,1,0:T(8,128)}, u32[]{:S(2)}, u32[]{:S(2)}) async-start(f32[16,128,256]{2,1,0:T(8,128)} %broadcast_in_dim.18), calls=%async_computation | async-start | bytes 4194304 | tf_op jit(solution)/shard_map/all_to_all | solution.py:383
  21.5 8.1 %copy-start.6 = (s32[4,2,128,64]{2,3,1,0:T(8,128)S(1)}, s32[4,2,128,64]{2,3,1,0:T(8,128)}, u32[]{:S(2)}) copy-start(s32[4,2,128,64]{2,3,1,0:T(8,128)} %param.9) | copy-start | bytes 786436
  21.5 0.8 copy-start.5
  23.7 19.0 %copy-start.8 = (s32[8,4]{0,1:T(4,128)S(1)}, s32[8,4]{0,1:T(4,128)}, u32[]{:S(2)}) copy-start(s32[8,4]{0,1:T(4,128)} %param.8) | copy-start | bytes 388
  23.7 36.9 %collective-permute-start.2 = (f32[512,512]{1,0:T(8,128)S(1)}, f32[512,512]{1,0:T(8,128)}, u32[]{:S(2)}, u32[]{:S(2)}) collective-permute-start(f32[512,512]{1,0:T(8,128)S(1)} %get-tuple-element.47), channel_id=1, source_target_pairs={{0,12},{1,13},{2,14},{3,15},{4,8},{5,9},{6,10},{7,11},{8,4},{9,5},... | collective-permute-start | bytes 3145736 | tf_op jit(solution)/shard_map/ppermute | solution.py:304
  26.9 33.7 %collective-permute-start.3 = (f32[512,512]{1,0:T(8,128)S(1)}, f32[512,512]{1,0:T(8,128)}, u32[]{:S(2)}, u32[]{:S(2)}) collective-permute-start(f32[512,512]{1,0:T(8,128)S(1)} %get-tuple-element.48), channel_id=1, source_target_pairs={{0,3},{1,2},{2,1},{3,0},{4,7},{5,6},{6,5},{7,4},{8,11},{9,10},{10,... | collective-permute-start | bytes 3145736 | tf_op jit(solution)/shard_map/ppermute | solution.py:304
  66.0 48.9 %collective-permute-start.4 = (f32[1024,512]{1,0:T(8,128)}, f32[1024,512]{1,0:T(8,128)}, u32[]{:S(2)}, u32[]{:S(2)}) collective-permute-start(f32[1024,512]{1,0:T(8,128)} %pad_maximum_fusion.refs_2_), channel_id=1, source_target_pairs={{0,1},{1,0},{2,3},{3,2},{4,5},{5,4},{6,7},{7,6},{8,9},{9,8},{10,11... | collective-permute-start | bytes 6291464 | tf_op jit(solution)/shard_map/ppermute | solution.py:304
  67.6 50.5 %collective-permute-start.5 = (f32[1024,512]{1,0:T(8,128)}, f32[1024,512]{1,0:T(8,128)}, u32[]{:S(2)}, u32[]{:S(2)}) collective-permute-start(f32[1024,512]{1,0:T(8,128)} %pad_maximum_fusion.1.refs_4_), channel_id=1, source_target_pairs={{0,4},{1,5},{2,6},{3,7},{4,0},{5,1},{6,2},{7,3},{8,12},{9,13},{10,... | collective-permute-start | bytes 6291464 | tf_op jit(solution)/shard_map/ppermute | solution.py:304
  77.2 52.5 %collective-permute-start.8 = (f32[2048,256]{1,0:T(8,128)}, f32[2048,256]{1,0:T(8,128)}, u32[]{:S(2)}, u32[]{:S(2)}) collective-permute-start(f32[2048,256]{1,0:T(8,128)} %bitcast.12.refs_5_), channel_id=1, source_target_pairs={{0,32},{16,112},{32,0},{48,80},{64,96},{80,48},{96,64},{112,16},{1... | collective-permute-start | bytes 6291464 | tf_op jit(solution)/shard_map/ppermute | solution.py:303
  118.1 27.5 %collective-permute-start.6 = (f32[1024,512]{1,0:T(8,128)}, f32[1024,512]{1,0:T(8,128)S(1)}, u32[]{:S(2)}, u32[]{:S(2)}) collective-permute-start(f32[1024,512]{1,0:T(8,128)} %pad_maximum_fusion.refs_2_), channel_id=1, source_target_pairs={{0,3},{1,2},{2,1},{3,0},{4,7},{5,6},{6,5},{7,4},{8,11},{9,10},{10,... | collective-permute-start | bytes 6291464 | tf_op jit(solution)/shard_map/ppermute | solution.py:304
  120.5 27.6 %collective-permute-start.7 = (f32[1024,512]{1,0:T(8,128)}, f32[1024,512]{1,0:T(8,128)}, u32[]{:S(2)}, u32[]{:S(2)}) collective-permute-start(f32[1024,512]{1,0:T(8,128)} %pad_maximum_fusion.1.refs_4_), channel_id=1, source_target_pairs={{0,12},{1,13},{2,14},{3,15},{4,8},{5,9},{6,10},{7,11},{8,4},{9,5},... | collective-permute-start | bytes 6291464 | tf_op jit(solution)/shard_map/ppermute | solution.py:304
  129.7 28.4 %collective-permute-start.11 = (f32[2048,256]{1,0:T(8,128)}, f32[2048,256]{1,0:T(8,128)}, u32[]{:S(2)}, u32[]{:S(2)}) collective-permute-start(f32[2048,256]{1,0:T(8,128)} %bitcast.12.refs_5_), channel_id=1, source_target_pairs={{0,96},{16,48},{32,64},{48,16},{64,32},{80,112},{96,0},{112,80},{1... | collective-permute-start | bytes 6291464 | tf_op jit(solution)/shard_map/ppermute | solution.py:303
  140.6 20.9 %copy-start.7 = (f32[512]{0:T(512)S(1)}, f32[512]{0:T(512)}, u32[]{:S(2)}) copy-start(f32[512]{0:T(512)} %param.6) | copy-start | bytes 6148
  145.6 1.3 copy-start.4
  148.1 34.7 %collective-permute-start.10 = (f32[1024,512]{1,0:T(8,128)}, f32[1024,512]{1,0:T(8,128)S(1)}, u32[]{:S(2)}, u32[]{:S(2)}) collective-permute-start(f32[1024,512]{1,0:T(8,128)} %collective-permute-done.5.refs_4_), channel_id=1, source_target_pairs={{0,12},{1,13},{2,14},{3,15},{4,8},{5,9},{6,10},{7,11},{8,4},{9,5},... | collective-permute-start | bytes 6291464 | tf_op jit(solution)/shard_map/ppermute | solution.py:304
  148.1 34.7 %collective-permute-start.9 = (f32[1024,512]{1,0:T(8,128)}, f32[1024,512]{1,0:T(8,128)}, u32[]{:S(2)}, u32[]{:S(2)}) collective-permute-start(f32[1024,512]{1,0:T(8,128)} %collective-permute-done.4.refs_2_), channel_id=1, source_target_pairs={{0,3},{1,2},{2,1},{3,0},{4,7},{5,6},{6,5},{7,4},{8,11},{9,10},{10,... | collective-permute-start | bytes 6291464 | tf_op jit(solution)/shard_map/ppermute | solution.py:304
  158.1 27.6 %collective-permute-start.12 = (f32[2048,256]{1,0:T(8,128)}, f32[2048,256]{1,0:T(8,128)}, u32[]{:S(2)}, u32[]{:S(2)}) collective-permute-start(f32[2048,256]{1,0:T(8,128)} %collective-permute-done.8.refs_5_), channel_id=1, source_target_pairs={{0,96},{16,48},{32,64},{48,16},{64,32},{80,112},{96,0},{112,80},{1... | collective-permute-start | bytes 6291464 | tf_op jit(solution)/shard_map/ppermute | solution.py:303
  182.8 2.9 %copy-start.3 = (f32[1024,512]{1,0:T(8,128)}, f32[1024,512]{1,0:T(8,128)S(1)}, u32[]{:S(2)}) copy-start(f32[1024,512]{1,0:T(8,128)S(1)} %collective-permute-done.10.wb) | copy-start | bytes 6291460
  202.0 29.4 %copy-start = (f32[8,128,128]{2,1,0:T(8,128)S(1)}, f32[8,128,128]{2,1,0:T(8,128)}, u32[]{:S(2)}) copy-start(f32[8,128,128]{2,1,0:T(8,128)} %start.1.start_ref) | copy-start | bytes 1572868
  202.0 29.4 %copy-start.1 = (bf16[512,1024]{1,0:T(8,128)(2,1)S(1)}, bf16[512,1024]{1,0:T(8,128)(2,1)}, u32[]{:S(2)}) copy-start(bf16[512,1024]{1,0:T(8,128)(2,1)} %get-tuple-element.82.high_ref) | copy-start | bytes 3145732
  202.0 29.4 %copy-start.2 = (bf16[512,1024]{1,0:T(8,128)(2,1)S(1)}, bf16[512,1024]{1,0:T(8,128)(2,1)}, u32[]{:S(2)}) copy-start(bf16[512,1024]{1,0:T(8,128)(2,1)} %get-tuple-element.83.low_ref) | copy-start | bytes 3145732
Sparse Core Ops, SparseCore 0:
  10.9 108.9 all-gather.2

commit v7 on v5

--- a/solution.py
+++ b/solution.py
@@ -12,7 +12,7 @@
 RANK = 64
 RING = 4
 STEPS = 4
-PERMUTED = 640
+PERMUTED = 512
 DEEP = 256
 WIDE = 256
 UNROLL = 4
@@ -175,19 +175,18 @@
     at = 0
     for part in parts:
         for first in range(0, part.shape[1], WIDE):
-            wide = min(WIDE, part.shape[1] - first)
-            here = slice(at, at + wide)
+            here = slice(at, at + WIDE)
 
             @pl.loop(0, tokens // GROUP, unroll=UNROLL)
-            def _(g, part=part, first=first, wide=wide, here=here):
+            def _(g, part=part, first=first, here=here):
                 rows = pl.ds(pl.multiple_of(g * GROUP, GROUP), GROUP)
-                kv = part[rows, first : first + wide] * scale_ref[rows, :]
+                kv = part[rows, first : first + WIDE] * scale_ref[rows, :]
                 keep = keep_ref[pl.ds(pl.multiple_of(g * 8, 8), 8), here][:1]
                 rh, rl = split(residual(kv, keep))
                 high_ref[rows, here] = rh
                 low_ref[rows, here] = rl
 
-            for cols in [slice(c, c + 128) for c in range(at, at + wide, 128)]:
+            for cols in [slice(c, c + 128) for c in range(at, at + WIDE, 128)]:
                 rh = high_ref[:, cols]
                 both = lax.dot_general(
                     rh,
@@ -197,7 +196,7 @@
                 )
                 cross = both[:, 128:]
                 gram_ref[cols, :] = both[:, :128] + (cross + cross.T)
-            at += wide
+            at += WIDE
 
 
 def inverse_factors(grams):
@@ -335,7 +334,9 @@
     deep2, deep1, plane = barrier((deep2, deep1, plane))
     deep3 = send(deep1, "z", 1)
     depth = multiply(depth, (deep2,), 2)
-    return plane3, deep3, plane, depth, early
+    plane3, plane, depth = barrier((plane3, plane, depth))
+    plane = multiply(plane, plane3, 3)
+    return deep3, plane, depth, early
 
 
 def shards(hidden, row_scale, key_value_weight, outlier, sketch_sign_flags):
@@ -381,12 +382,9 @@
     own, _ = lax.optimization_barrier((own[:, DEEP:], own))
     rest = lax.all_gather(own, ("batch", "seq"), axis=0).reshape(RING, seq, quarter, cols - rest_at)
     early = (start, scale, keep)
-    plane3, deep3, ab, c, (start, scale, keep) = gather_blocks(flat[:, :PERMUTED], deep, multiply, early)
+    deep3, ab, c, (start, scale, keep) = gather_blocks(flat[:, :PERMUTED], deep, multiply, early)
     rest, ab, c = lax.optimization_barrier((rest, ab, c))
     cd = accumulate_all(hidden, rest)
-    plane3, ab, cd = lax.optimization_barrier((plane3, ab, cd))
-    ab = multiply(ab, plane3, 3)
-    deep3, ab, c = lax.optimization_barrier((deep3, ab, c))
 
     last = [(deep3, RING)]
     specs = block_specs(tokens, last)

time: 248 us -> 249 us (level)
  waiting for transfers between devices: 50.8 us -> 62.2 us
  Pallas kernels: 108 us -> 103 us
  blocking collectives: 31.9 us -> 28 us
    ppermute x3, waiting for transfers between devices: 0.01 us -> 7.05 us  [send(): return lax.ppermute(v, ('batch', 'head'), depth_pairs(which))]
    pallas_call x7, Pallas kernels: 59.1 us -> 53.1 us  [accumulate(): pl.pallas_call(functools.partial(accumulate_kernel, [parts for _, parts i...]
    all_gather x1, waiting for transfers between devices: 0.01 us -> 4.53 us  [shards(): deep = lax.all_gather(own[:, :DEEP], 'seq', axis=0, tiled=True)]
    all_to_all x1, blocking collectives: 17.7 us -> 14.6 us  [shards(): pieces = lax.all_to_all(gram, 'seq', 0, 0, tiled=True)]
  transfers between devices with their start and end apart: 15 -> 15, of which waited for: 8 -> 11; matrix products, arithmetic and copies ran while one was open for 6% -> 5% of each run, Pallas kernels for 34% -> 32%
where the time goes in v7:
time: 249 us; the launch traced here: 248 us
  Pallas kernels  103 us (41%)
  waiting for transfers between devices  62.2 us (25%)
  blocking collectives  28 us (11%)
  starting transfers between devices  23.4 us (9%)
  between operations  14.2 us (6%)
  other arithmetic  8.82 us (4%)
  local copies, waits for them, and re-layouts  8.73 us (4%)
    pallas_call x7, Pallas kernels, accumulate(): pl.pallas_call(functools.partial(accumulate_kernel, [parts for _, parts i...  53.1 us
    ppermute x10, waiting for transfers between devices, send(): return lax.ppermute(v, ('head', 'seq'), plane_pairs(axis, which))  49.9 us
    ppermute x10, starting transfers between devices, send(): return lax.ppermute(v, ('head', 'seq'), plane_pairs(axis, which))  16.3 us
    all_to_all x1, blocking collectives, shards(): pieces = lax.all_to_all(gram, 'seq', 0, 0, tiled=True)  14.6 us
    pallas_call x1, Pallas kernels, accumulate_all(): pl.pallas_call(accumulate_all_kernel, grid=(seq // 2,), in_specs=[pl.Bloc...  13.9 us
    all_to_all x1, blocking collectives, shards(): lax.all_to_all(jnp.broadcast_to(piece, (seq,) + piece.shape), 'seq', 0, 0)  13.3 us
    pallas_call x1, Pallas kernels, shards(): pl.pallas_call(project_kernel, grid_spec=pltpu.PrefetchScalarGridSpec(num...  12.3 us
    pallas_call x1, Pallas kernels, shards(): pl.pallas_call(functools.partial(factor_kernel, root_length), out_shape=[...  12.2 us
  transfers between devices with their start and end apart: 15, of which 11 were waited for; matrix products, arithmetic and copies ran while one was open for 5% of the time, Pallas kernels for 32%

profile of v7, /device:TPU:0, one launch (start us, length us, event | category | flops | bytes accessed | tf_op | source)
XLA Modules:
  0.0 247.9 jit_solution(888452455867720648)
XLA Ops:
  7.2 0.0 all-gather.4.cloned.1.call-start
  7.2 2.1 copy.10
  9.3 0.1 slice.23
  9.4 0.7 fusion.5
  10.1 0.0 all-gather.4.cloned.1.call-update
  10.1 0.0 all-gather.6.cloned.1.call-start
  10.2 0.7 all-gather.6.cloned.1.call-update
  10.9 0.1 fusion.4
  11.0 0.0 copy-start.5
  11.0 1.7 collective-permute-start
  12.6 1.6 collective-permute-start.1
  14.2 6.0 %collective-permute-done = f32[256,512]{1,0:T(8,128)S(1)} collective-permute-done((f32[256,512]{1,0:T(8,128)S(1)}, f32[256,512]{1,0:T(8,128)S(1)}, u32[]{:S(2)}, u32[]{:S(2)}) %collective-permute-start) | collective-permute-done | bytes 524320 | tf_op jit(solution)/shard_map/ppermute | solution.py:302
  20.2 1.6 collective-permute-done.1
  21.8 0.2 pad_maximum_fusion.2
  22.0 0.0 copy-start.7
  22.0 2.2 collective-permute-start.2
  24.2 3.0 %collective-permute-start.3 = (f32[512,512]{1,0:T(8,128)S(1)}, f32[512,512]{1,0:T(8,128)}, u32[]{:S(2)}, u32[]{:S(2)}) collective-permute-start(f32[512,512]{1,0:T(8,128)S(1)} %get-tuple-element.52), channel_id=1, source_target_pairs={{0,3},{1,2},{2,1},{3,0},{4,7},{5,6},{6,5},{7,4},{8,11},{9,10},{10,... | collective-permute-start | bytes 3145736 | tf_op jit(solution)/shard_map/ppermute | solution.py:302
  27.2 0.2 copy.8
  27.4 1.0 pad_maximum_fusion.4.sign_ref
  28.4 11.3 %start.1.start_ref = f32[8,128,128]{2,1,0:T(8,128)} custom-call(f32[8,128,128]{2,1,0:T(8,128)} %pad_maximum_fusion.4.sign_ref), custom_call_target="tpu_custom_call" | custom-call | flops 100000000 | bytes 1000000 | tf_op jit(solution)/shard_map/start/pallas_call | solution.py:352
  39.7 0.1 broadcast_in_dim.13
  39.8 0.7 broadcast_bitcast_fusion.keep_ref
  40.5 1.2 collective-permute-done.3
  41.7 2.7 %pad_maximum_fusion.1.refs_4_ = f32[1024,512]{1,0:T(8,128)} fusion(f32[512,512]{1,0:T(8,128)} %collective-permute-done.3, f32[512,512]{1,0:T(8,128)S(1)} %get-tuple-element.52), kind=kLoop, calls=%fused_computation.1 | loop fusion | flops 524288 | bytes 4194304 | tf_op jit(solution)/shard_map/concatenate | solution.py:307
  44.4 2.7 %pad_maximum_fusion.refs_2_ = f32[1024,512]{1,0:T(8,128)} fusion(f32[512,512]{1,0:T(8,128)} %collective-permute-done.2, f32[512,512]{1,0:T(8,128)S(1)} %get-tuple-element.51), kind=kLoop, calls=%fused_computation | loop fusion | flops 524288 | bytes 4194304 | tf_op jit(solution)/shard_map/concatenate | solution.py:307
  47.2 0.5 collective-permute-start.5
  47.6 0.5 collective-permute-start.6
  48.1 0.6 concatenate.32.refs_0_
  48.8 7.9 %plane0.1.refs_5_ = f32[512,512]{1,0:T(8,128)} custom-call(s32[8]{0:T(128)} %concatenate.32.refs_0_, f32[512,8192]{1,0:T(8,128)} %x3.1, f32[1024,512]{1,0:T(8,128)} %pad_maximum_fusion.refs_2_, f32[512,8192]{1,0:T(8,128)} %x3.1, f32[1024,512]{1,0:T(8,128)} %pad_maximum_fusion.1.refs_4_), custom_call_target="tpu_custom_call" | custom-call | flops 3221225472 | bytes 8388608 | tf_op jit(solution)/shard_map/plane0/pallas_call | solution.py:112
  56.7 4.5 %all-gather.4.cloned.1.call-done.refs_5_ = f32[2048,256]{1,0:T(8,128)} async-done(((f32[128,256]{1,0:T(8,128)}), f32[2048,256]{1,0:T(8,128)}) %all-gather.4.cloned.1.call-update) | async-done | bytes 2097168 | tf_op jit(solution)/shard_map/all_gather | solution.py:381
  61.2 1.7 collective-permute-start.4
  62.9 0.5 fusion.2.refs_0_
  63.4 6.2 %deep0.1.refs_6_ = f32[512,256]{1,0:T(8,128)} custom-call(s32[16]{0:T(128)} %fusion.2.refs_0_, f32[512,8192]{1,0:T(8,128)} %x3.1, f32[512,8192]{1,0:T(8,128)} %x3.1, f32[512,8192]{1,0:T(8,128)} %x3.1, f32[512,8192]{1,0:T(8,128)} %x3.1, f32[2048,256]{1,0:T(8,128)} %all-gather.4.cloned.1.call-done.refs_5_), custom_call_target="tpu_custom_call" | custom-call | flops 1610612736 | bytes 6291456 | tf_op jit(solution)/shard_map/deep0/pallas_call | solution.py:112
  69.7 8.8 %collective-permute-done.5.refs_2_ = f32[1024,512]{1,0:T(8,128)} collective-permute-done((f32[1024,512]{1,0:T(8,128)}, f32[1024,512]{1,0:T(8,128)}, u32[]{:S(2)}, u32[]{:S(2)}) %collective-permute-start.5) | collective-permute-done | bytes 2097184 | tf_op jit(solution)/shard_map/ppermute | solution.py:302
  78.5 0.8 collective-permute-done.6.refs_4_
  79.3 1.4 collective-permute-start.8
  80.7 1.8 collective-permute-start.9
  82.5 0.6 concatenate.33.refs_0_
  83.1 8.4 %plane1.1.refs_5_ = f32[512,512]{1,0:T(8,128)} custom-call(s32[8]{0:T(128)} %concatenate.33.refs_0_, f32[512,8192]{1,0:T(8,128)} %x3.1, f32[1024,512]{1,0:T(8,128)} %collective-permute-done.5.refs_2_, f32[512,8192]{1,0:T(8,128)} %x3.1, f32[1024,512]{1,0:T(8,128)} %collective-permute-done.6.refs_4_, f32[512,512]{1,0:T(8,128)} %plane0.1.refs_5_), custom_call_target="tpu_custom_call" | custom-call | flops 3221225472 | bytes 8388608 | tf_op jit(solution)/shard_map/plane1/pallas_call | solution.py:112
  91.5 2.8 %collective-permute-start.7 = (f32[2048,256]{1,0:T(8,128)}, f32[2048,256]{1,0:T(8,128)}, u32[]{:S(2)}, u32[]{:S(2)}) collective-permute-start(f32[2048,256]{1,0:T(8,128)} %all-gather.4.cloned.1.call-done.refs_5_), channel_id=1, source_target_pairs={{0,96},{16,48},{32,64},{48,16},{64,32},{80,112},{96,0},{112,80},{1... | collective-permute-start | bytes 6291464 | tf_op jit(solution)/shard_map/ppermute | solution.py:301
  94.3 0.5 fusion.1.refs_0_
  94.8 6.6 %deep1.1.refs_6_ = f32[512,256]{1,0:T(8,128)} custom-call(s32[16]{0:T(128)} %fusion.1.refs_0_, f32[512,8192]{1,0:T(8,128)} %x3.1, f32[512,8192]{1,0:T(8,128)} %x3.1, f32[512,8192]{1,0:T(8,128)} %x3.1, f32[512,8192]{1,0:T(8,128)} %x3.1, f32[2048,256]{1,0:T(8,128)} %collective-permute-done.4.refs_5_, f32[512,256]{1,0:T(8,128)} %deep0.1.refs_6_), custom_call_target="tpu_custom_call" | custom-call | flops 1610612736 | bytes 6291456 | tf_op jit(solution)/shard_map/deep1/pallas_call | solution.py:112
  101.4 11.4 %collective-permute-done.8.refs_2_ = f32[1024,512]{1,0:T(8,128)S(1)} collective-permute-done((f32[1024,512]{1,0:T(8,128)}, f32[1024,512]{1,0:T(8,128)S(1)}, u32[]{:S(2)}, u32[]{:S(2)}) %collective-permute-start.8) | collective-permute-done | bytes 2097184 | tf_op jit(solution)/shard_map/ppermute | solution.py:302
  112.8 1.2 collective-permute-done.9.refs_4_
  114.0 1.8 collective-permute-start.11
  115.8 1.9 collective-permute-start.12
  117.7 0.7 concatenate.34.refs_0_
  118.4 8.7 %plane2.1.refs_5_ = f32[512,512]{1,0:T(8,128)} custom-call(s32[8]{0:T(128)} %concatenate.34.refs_0_, f32[512,8192]{1,0:T(8,128)} %x3.1, f32[1024,512]{1,0:T(8,128)} %copy-done.4, f32[512,8192]{1,0:T(8,128)} %x3.1, f32[1024,512]{1,0:T(8,128)} %collective-permute-done.9.refs_4_, f32[512,512]{1,0:T(8,128)} %plane1.1.refs_5_), custom_call_target="tpu_custom_call" | custom-call | flops 3221225472 | bytes 8388608 | tf_op jit(solution)/shard_map/plane2/pallas_call | solution.py:112
  127.1 7.0 %collective-permute-done.7.refs_5_ = f32[2048,256]{1,0:T(8,128)} collective-permute-done((f32[2048,256]{1,0:T(8,128)}, f32[2048,256]{1,0:T(8,128)}, u32[]{:S(2)}, u32[]{:S(2)}) %collective-permute-start.7) | collective-permute-done | bytes 2097184 | tf_op jit(solution)/shard_map/ppermute | solution.py:301
  134.1 2.5 %collective-permute-start.10 = (f32[2048,256]{1,0:T(8,128)}, f32[2048,256]{1,0:T(8,128)S(1)}, u32[]{:S(2)}, u32[]{:S(2)}) collective-permute-start(f32[2048,256]{1,0:T(8,128)} %collective-permute-done.4.refs_5_), channel_id=1, source_target_pairs={{0,96},{16,48},{32,64},{48,16},{64,32},{80,112},{96,0},{112,80},{1... | collective-permute-start | bytes 6291464 | tf_op jit(solution)/shard_map/ppermute | solution.py:301
  136.7 0.6 concatenate.35.refs_0_
  137.3 0.5 fusion.refs_0_
  137.8 0.6 fusion.3.index_ref
  138.4 0.9 copy.9.scale_ref
  139.3 6.7 %deep2.1.depth_ref = f32[512,256]{1,0:T(8,128)} custom-call(s32[16]{0:T(128)} %fusion.refs_0_, f32[512,8192]{1,0:T(8,128)} %x3.1, f32[512,8192]{1,0:T(8,128)} %x3.1, f32[512,8192]{1,0:T(8,128)} %x3.1, f32[512,8192]{1,0:T(8,128)} %x3.1, f32[2048,256]{1,0:T(8,128)} %collective-permute-done.7.refs_5_, f32[512,256]{1,0:T(8,128)} %deep1.1.refs_6_), custom_call_target="tpu_custom_call" | custom-call | flops 1610612736 | bytes 6291456 | tf_op jit(solution)/shard_map/deep2/pallas_call | solution.py:112
  146.0 17.7 %collective-permute-done.11.refs_2_ = f32[1024,512]{1,0:T(8,128)} collective-permute-done((f32[1024,512]{1,0:T(8,128)}, f32[1024,512]{1,0:T(8,128)}, u32[]{:S(2)}, u32[]{:S(2)}) %collective-permute-start.11) | collective-permute-done | bytes 2097184 | tf_op jit(solution)/shard_map/ppermute | solution.py:302
  163.7 1.2 collective-permute-done.12.refs_4_
  164.9 8.4 %plane3.1.plane_ref = f32[512,512]{1,0:T(8,128)} custom-call(s32[8]{0:T(128)} %concatenate.35.refs_0_, f32[512,8192]{1,0:T(8,128)} %x3.1, f32[1024,512]{1,0:T(8,128)} %collective-permute-done.11.refs_2_, f32[512,8192]{1,0:T(8,128)} %x3.1, f32[1024,512]{1,0:T(8,128)} %collective-permute-done.12.refs_4_, f32[512,512]{1,0:T(8,128)} %plane2.1.refs_5_), custom_call_target="tpu_custom_call" | custom-call | flops 3221225472 | bytes 8388608 | tf_op jit(solution)/shard_map/plane3/pallas_call | solution.py:112
  173.3 13.9 %rest.1.rest_ref = f32[512,256]{1,0:T(8,128)} custom-call(f32[512,8192]{1,0:T(8,128)} %x3.1, f32[4,16,128,256]{3,2,1,0:T(8,128)} %bitcast.43), custom_call_target="tpu_custom_call" | custom-call | flops 6442450944 | bytes 25165824 | tf_op jit(solution)/shard_map/rest/pallas_call | solution.py:141
  187.2 1.3 copy-done.3
  188.6 12.3 %project.1 = (bf16[512,1024]{1,0:T(8,128)(2,1)}, bf16[512,1024]{1,0:T(8,128)(2,1)}, f32[1024,128]{1,0:T(8,128)}) custom-call(s32[16]{0:T(128)} %fusion.3.index_ref, f32[512,8192]{1,0:T(8,128)} %x3.1, f32[512,8192]{1,0:T(8,128)} %x3.1, f32[512,8192]{1,0:T(8,128)} %x3.1, f32[512,8192]{1,0:T(8,128)} %x3.1, f32[2048,256]{1,0:T(8,128)} %copy-done.3, ...), custom_call_target="tpu_custom_call" | custom-call | flops 1610612736 | bytes 6291456 | tf_op jit(solution)/shard_map/project/pallas_call | solution.py:392
  200.8 14.6 %all_to_all.14 = f32[16,64,128]{2,1,0:T(8,128)S(1)} all-to-all(f32[16,64,128]{2,1,0:T(8,128)} %bitcast.48), channel_id=1, replica_groups=mesh['batch'=4,'head'=2,'seq'=16] {'seq'}, dimensions={0} | all-to-all | bytes 1048576 | tf_op jit(solution)/shard_map/all_to_all | solution.py:413
  215.5 13.3 %all_to_all.15 = f32[16,64,128]{2,1,0:T(8,128)S(1)} all-to-all(f32[16,64,128]{2,1,0:T(8,128)S(1)} %broadcast_in_dim.15), channel_id=1, replica_groups=mesh['batch'=4,'head'=2,'seq'=16] {'seq'}, dimensions={0} | all-to-all | bytes 1048576 | tf_op jit(solution)/shard_map/all_to_all | solution.py:415
  228.9 12.2 %factor.1 = (bf16[4,512,128]{2,1,0:T(8,128)(2,1)}, f32[4,128,128]{2,1,0:T(8,128)}) custom-call(f32[1024,128]{1,0:T(8,128)S(1)} %bitcast.42, f32[8,128,128]{2,1,0:T(8,128)S(1)} %copy-done, bf16[512,1024]{1,0:T(8,128)(2,1)S(1)} %copy-done.1, bf16[512,1024]{1,0:T(8,128)(2,1)S(1)} %copy-done.2), custom_call_target="tpu_custom_call" | custom-call | flops 1000000000 | bytes 4194304 | tf_op jit(solution)/shard_map/factor/pallas_call | solution.py:417
  (21 shorter events, 0.1 us)
Async XLA Ops:
  7.2 54.1 %all-gather.4.cloned.1.call-start = ((), (), s32[]{:S(2)}) async-start(), calls=%async_computation.2 | async-start | bytes 2228224 | tf_op jit(solution)/shard_map/all_gather | solution.py:381
  10.1 163.2 %all-gather.6.cloned.1.call-start = ((), (), s32[]{:S(2)}) async-start(), calls=%async_computation.3 | async-start | bytes 8519680 | tf_op jit(solution)/shard_map/all_gather | solution.py:383
  11.0 16.2 %copy-start.5 = (s32[4,2,128,64]{2,3,1,0:T(8,128)S(1)}, s32[4,2,128,64]{2,3,1,0:T(8,128)}, u32[]{:S(2)}) copy-start(s32[4,2,128,64]{2,3,1,0:T(8,128)} %param.9) | copy-start | bytes 786436
  11.0 9.3 %collective-permute-start = (f32[256,512]{1,0:T(8,128)S(1)}, f32[256,512]{1,0:T(8,128)S(1)}, u32[]{:S(2)}, u32[]{:S(2)}) collective-permute-start(f32[256,512]{1,0:T(8,128)S(1)} %get-tuple-element.47), channel_id=1, source_target_pairs={{0,4},{1,5},{2,6},{3,7},{4,0},{5,1},{6,2},{7,3},{8,12},{9,13},{10,... | collective-permute-start | bytes 1572872 | tf_op jit(solution)/shard_map/ppermute | solution.py:302
  12.6 9.2 %collective-permute-start.1 = (f32[256,512]{1,0:T(8,128)S(1)}, f32[256,512]{1,0:T(8,128)S(1)}, u32[]{:S(2)}, u32[]{:S(2)}) collective-permute-start(f32[256,512]{1,0:T(8,128)S(1)} %get-tuple-element.48), channel_id=1, source_target_pairs={{0,1},{1,0},{2,3},{3,2},{4,5},{5,4},{6,7},{7,6},{8,9},{9,8},{10,11... | collective-permute-start | bytes 1572872 | tf_op jit(solution)/shard_map/ppermute | solution.py:302
  22.0 17.7 %copy-start.7 = (s32[8,4]{0,1:T(4,128)S(1)}, s32[8,4]{0,1:T(4,128)}, u32[]{:S(2)}) copy-start(s32[8,4]{0,1:T(4,128)} %param.8) | copy-start | bytes 388
  22.0 18.5 %collective-permute-start.2 = (f32[512,512]{1,0:T(8,128)S(1)}, f32[512,512]{1,0:T(8,128)}, u32[]{:S(2)}, u32[]{:S(2)}) collective-permute-start(f32[512,512]{1,0:T(8,128)S(1)} %get-tuple-element.51), channel_id=1, source_target_pairs={{0,12},{1,13},{2,14},{3,15},{4,8},{5,9},{6,10},{7,11},{8,4},{9,5},... | collective-permute-start | bytes 3145736 | tf_op jit(solution)/shard_map/ppermute | solution.py:302
  24.2 17.5 %collective-permute-start.3 = (f32[512,512]{1,0:T(8,128)S(1)}, f32[512,512]{1,0:T(8,128)}, u32[]{:S(2)}, u32[]{:S(2)}) collective-permute-start(f32[512,512]{1,0:T(8,128)S(1)} %get-tuple-element.52), channel_id=1, source_target_pairs={{0,3},{1,2},{2,1},{3,0},{4,7},{5,6},{6,5},{7,4},{8,11},{9,10},{10,... | collective-permute-start | bytes 3145736 | tf_op jit(solution)/shard_map/ppermute | solution.py:302
  47.2 31.3 %collective-permute-start.5 = (f32[1024,512]{1,0:T(8,128)}, f32[1024,512]{1,0:T(8,128)}, u32[]{:S(2)}, u32[]{:S(2)}) collective-permute-start(f32[1024,512]{1,0:T(8,128)} %pad_maximum_fusion.refs_2_), channel_id=1, source_target_pairs={{0,1},{1,0},{2,3},{3,2},{4,5},{5,4},{6,7},{7,6},{8,9},{9,8},{10,11... | collective-permute-start | bytes 6291464 | tf_op jit(solution)/shard_map/ppermute | solution.py:302
  47.6 31.6 %collective-permute-start.6 = (f32[1024,512]{1,0:T(8,128)}, f32[1024,512]{1,0:T(8,128)}, u32[]{:S(2)}, u32[]{:S(2)}) collective-permute-start(f32[1024,512]{1,0:T(8,128)} %pad_maximum_fusion.1.refs_4_), channel_id=1, source_target_pairs={{0,4},{1,5},{2,6},{3,7},{4,0},{5,1},{6,2},{7,3},{8,12},{9,13},{10,... | collective-permute-start | bytes 6291464 | tf_op jit(solution)/shard_map/ppermute | solution.py:302
  61.2 30.3 %collective-permute-start.4 = (f32[2048,256]{1,0:T(8,128)}, f32[2048,256]{1,0:T(8,128)}, u32[]{:S(2)}, u32[]{:S(2)}) collective-permute-start(f32[2048,256]{1,0:T(8,128)} %all-gather.4.cloned.1.call-done.refs_5_), channel_id=1, source_target_pairs={{0,32},{16,112},{32,0},{48,80},{64,96},{80,48},{96,64},{112,16},{1... | collective-permute-start | bytes 6291464 | tf_op jit(solution)/shard_map/ppermute | solution.py:301
  79.3 33.5 %collective-permute-start.8 = (f32[1024,512]{1,0:T(8,128)}, f32[1024,512]{1,0:T(8,128)S(1)}, u32[]{:S(2)}, u32[]{:S(2)}) collective-permute-start(f32[1024,512]{1,0:T(8,128)} %pad_maximum_fusion.refs_2_), channel_id=1, source_target_pairs={{0,3},{1,2},{2,1},{3,0},{4,7},{5,6},{6,5},{7,4},{8,11},{9,10},{10,... | collective-permute-start | bytes 6291464 | tf_op jit(solution)/shard_map/ppermute | solution.py:302
  80.7 33.3 %collective-permute-start.9 = (f32[1024,512]{1,0:T(8,128)}, f32[1024,512]{1,0:T(8,128)}, u32[]{:S(2)}, u32[]{:S(2)}) collective-permute-start(f32[1024,512]{1,0:T(8,128)} %pad_maximum_fusion.1.refs_4_), channel_id=1, source_target_pairs={{0,12},{1,13},{2,14},{3,15},{4,8},{5,9},{6,10},{7,11},{8,4},{9,5},... | collective-permute-start | bytes 6291464 | tf_op jit(solution)/shard_map/ppermute | solution.py:302
  91.5 42.6 %collective-permute-start.7 = (f32[2048,256]{1,0:T(8,128)}, f32[2048,256]{1,0:T(8,128)}, u32[]{:S(2)}, u32[]{:S(2)}) collective-permute-start(f32[2048,256]{1,0:T(8,128)} %all-gather.4.cloned.1.call-done.refs_5_), channel_id=1, source_target_pairs={{0,96},{16,48},{32,64},{48,16},{64,32},{80,112},{96,0},{112,80},{1... | collective-permute-start | bytes 6291464 | tf_op jit(solution)/shard_map/ppermute | solution.py:301
  112.8 5.6 %copy-start.4 = (f32[1024,512]{1,0:T(8,128)}, f32[1024,512]{1,0:T(8,128)S(1)}, u32[]{:S(2)}) copy-start(f32[1024,512]{1,0:T(8,128)S(1)} %collective-permute-done.8.refs_2_) | copy-start | bytes 6291460
  114.0 49.7 %collective-permute-start.11 = (f32[1024,512]{1,0:T(8,128)}, f32[1024,512]{1,0:T(8,128)}, u32[]{:S(2)}, u32[]{:S(2)}) collective-permute-start(f32[1024,512]{1,0:T(8,128)} %collective-permute-done.5.refs_2_), channel_id=1, source_target_pairs={{0,3},{1,2},{2,1},{3,0},{4,7},{5,6},{6,5},{7,4},{8,11},{9,10},{10,... | collective-permute-start | bytes 6291464 | tf_op jit(solution)/shard_map/ppermute | solution.py:302
  115.8 49.1 %collective-permute-start.12 = (f32[1024,512]{1,0:T(8,128)}, f32[1024,512]{1,0:T(8,128)}, u32[]{:S(2)}, u32[]{:S(2)}) collective-permute-start(f32[1024,512]{1,0:T(8,128)} %collective-permute-done.6.refs_4_), channel_id=1, source_target_pairs={{0,12},{1,13},{2,14},{3,15},{4,8},{5,9},{6,10},{7,11},{8,4},{9,5},... | collective-permute-start | bytes 6291464 | tf_op jit(solution)/shard_map/ppermute | solution.py:302
  118.4 20.0 %copy-start.6 = (f32[512]{0:T(512)S(1)}, f32[512]{0:T(512)}, u32[]{:S(2)}) copy-start(f32[512]{0:T(512)} %param.6) | copy-start | bytes 6148
  134.1 53.1 %collective-permute-start.10 = (f32[2048,256]{1,0:T(8,128)}, f32[2048,256]{1,0:T(8,128)S(1)}, u32[]{:S(2)}, u32[]{:S(2)}) collective-permute-start(f32[2048,256]{1,0:T(8,128)} %collective-permute-done.4.refs_5_), channel_id=1, source_target_pairs={{0,96},{16,48},{32,64},{48,16},{64,32},{80,112},{96,0},{112,80},{1... | collective-permute-start | bytes 6291464 | tf_op jit(solution)/shard_map/ppermute | solution.py:301
  187.2 1.3 copy-start.3
  200.8 28.1 %copy-start = (f32[8,128,128]{2,1,0:T(8,128)S(1)}, f32[8,128,128]{2,1,0:T(8,128)}, u32[]{:S(2)}) copy-start(f32[8,128,128]{2,1,0:T(8,128)} %start.1.start_ref) | copy-start | bytes 1572868
  200.8 28.1 %copy-start.1 = (bf16[512,1024]{1,0:T(8,128)(2,1)S(1)}, bf16[512,1024]{1,0:T(8,128)(2,1)}, u32[]{:S(2)}) copy-start(bf16[512,1024]{1,0:T(8,128)(2,1)} %get-tuple-element.90.high_ref) | copy-start | bytes 3145732
  200.8 28.1 %copy-start.2 = (bf16[512,1024]{1,0:T(8,128)(2,1)S(1)}, bf16[512,1024]{1,0:T(8,128)(2,1)}, u32[]{:S(2)}) copy-start(bf16[512,1024]{1,0:T(8,128)(2,1)} %get-tuple-element.91.low_ref) | copy-start | bytes 3145732
Sparse Core Ops, SparseCore 0:
  10.7 50.4 all-gather.3
  64.1 89.7 all-gather.5

commit v8 on v6

--- a/solution.py
+++ b/solution.py
@@ -12,8 +12,7 @@
 RANK = 64
 RING = 4
 STEPS = 4
-PERMUTED = 512
-DEEP = 256
+PERMUTED = 768
 WIDE = 256
 UNROLL = 4
 VMEM_LIMIT = 56 << 20
@@ -124,52 +123,18 @@
     )(index, *block_operands(hidden, blocks), *([] if total is None else [total]))
 
 
-def accumulate_all_kernel(x_ref, w_ref, out_ref):
-    @pl.when(pl.program_id(0) == 0)
-    def _():
-        out_ref[...] = jnp.zeros_like(out_ref)
-
-    batch, shards_in, quarter, cols = w_ref.shape
-    rows = batch * quarter
-    for s in range(shards_in):
-        out_ref[...] += three_products(x_ref[:, s * rows : s * rows + rows], w_ref[:, s].reshape(rows, cols))
-
-
-def accumulate_all(hidden, weight):
-    tokens = hidden.shape[0]
-    batch, seq, quarter, cols = weight.shape
-    return pl.pallas_call(
-        accumulate_all_kernel,
-        grid=(seq // 2,),
-        in_specs=[
-            pl.BlockSpec((tokens, 2 * batch * quarter), lambda k: (0, k)),
-            pl.BlockSpec((batch, 2, quarter, cols), lambda k: (0, k, 0, 0)),
-        ],
-        out_specs=pl.BlockSpec((tokens, cols), lambda k: (0, 0)),
-        out_shape=jax.ShapeDtypeStruct((tokens, cols), F32),
-        compiler_params=pltpu.CompilerParams(vmem_limit_bytes=VMEM_LIMIT, dimension_semantics=("arbitrary",)),
-        name="rest",
-        cost_estimate=pl.CostEstimate(
-            flops=6 * tokens * weight.size, bytes_accessed=4 * (weight.size + hidden.size), transcendentals=0
-        ),
-    )(hidden, weight)
-
-
-def project_kernel(index_ref, xa, wa, xb, wb, xc0, xc1, xc2, xc3, wc, ab_ref, c_ref, rest_ref, scale_ref, keep_ref,
-                   high_ref, low_ref, gram_ref, ab_acc, c_acc):
+def project_kernel(index_ref, xa, wa, xb, wb, plane_ref, depth_ref, scale_ref, keep_ref, high_ref, low_ref, gram_ref, plane_acc):
     step = pl.program_id(0)
 
     @pl.when(step == 0)
     def _():
-        ab_acc[...] = ab_ref[...]
-        c_acc[...] = c_ref[...]
-
-    ab_acc[...] += three_products(xa[...], wa[...]) + three_products(xb[...], wb[...])
-    c_acc[...] += three_products(jnp.concatenate([xc0[...], xc1[...], xc2[...], xc3[...]], axis=1), wc[...])
+        plane_acc[...] = plane_ref[...]
+
+    plane_acc[...] += three_products(xa[...], wa[...]) + three_products(xb[...], wb[...])
 
     @pl.when(step == STEPS - 1)
     def _():
-        epilogue((ab_acc, c_acc, rest_ref), scale_ref, keep_ref, high_ref, low_ref, gram_ref)
+        epilogue((plane_acc, depth_ref), scale_ref, keep_ref, high_ref, low_ref, gram_ref)
 
 
 def epilogue(parts, scale_ref, keep_ref, high_ref, low_ref, gram_ref):
@@ -336,7 +301,9 @@
     deep2, deep1, plane = barrier((deep2, deep1, plane))
     deep3 = send(deep1, "z", 1)
     depth = multiply(depth, (deep2,), 2)
-    return (*plane3, deep3), (plane, depth), early
+    deep3, depth, plane = barrier((deep3, depth, plane))
+    depth = multiply(depth, (deep3,), 3)
+    return plane3, plane, depth, early
 
 
 def shards(hidden, row_scale, key_value_weight, outlier, sketch_sign_flags):
@@ -367,7 +334,7 @@
     joined = lambda *lists: jnp.concatenate([i for indices in lists for i in indices])
     plane_at = [joined(i) for i in plane_index]
     deep_at = [joined(i) for i in deep_index]
-    last_at = joined(plane_index[3], deep_index[3])
+    last_at = joined(plane_index[3])
     scale = row_scale[:, None]
     keep = jnp.repeat(jnp.repeat((1 - outlier).astype(F32), kv_cols, axis=1), 8, axis=0)
 
@@ -377,17 +344,13 @@
 
     flat = key_value_weight.reshape(rows, cols)
     quarter = rows // RING
-    rest_at = PERMUTED + DEEP
     own = lax.dynamic_slice_in_dim(flat[:, PERMUTED:], plane * quarter, quarter, 0)
-    deep = jnp.broadcast_to(own[:, :DEEP], (seq, quarter, DEEP))
-    deep = lax.all_to_all(deep, "seq", 0, 0).reshape(seq * quarter, DEEP)
-    rest = lax.all_gather(own[:, DEEP:], ("batch", "seq"), axis=0).reshape(RING, seq, quarter, cols - rest_at)
+    deep = lax.all_gather(own, "seq", axis=0, tiled=True)
     early = (start, scale, keep, last_at)
-    (a3, b3, c3), (ab, c), (start, scale, keep, last_at) = gather_blocks(flat[:, :PERMUTED], deep, multiply, early)
-    rest, ab, c = lax.optimization_barrier((rest, ab, c))
-    cd = accumulate_all(hidden, rest)
-
-    last = [(a3, 1), (b3, 1), (c3, RING)]
+    (a3, b3), ab, c, (start, scale, keep, last_at) = gather_blocks(flat[:, :PERMUTED], deep, multiply, early)
+    ab, c = lax.optimization_barrier((ab, c))
+
+    last = [(a3, 1), (b3, 1)]
     specs = block_specs(tokens, last)
     whole = lambda *shape: pl.BlockSpec(shape, lambda j, ix: (0,) * len(shape))
     high, low, gram = pl.pallas_call(
@@ -396,10 +359,10 @@
             num_scalar_prefetch=1,
             grid=(STEPS,),
             in_specs=specs
-            + [whole(tokens, t.shape[1]) for t in (ab, c, cd)]
+            + [whole(tokens, t.shape[1]) for t in (ab, c)]
             + [whole(tokens, 1), whole(8 * groups, cols)],
             out_specs=[whole(tokens, cols), whole(tokens, cols), whole(128 * pairs, 128)],
-            scratch_shapes=[pltpu.VMEM(ab.shape, F32), pltpu.VMEM(c.shape, F32)],
+            scratch_shapes=[pltpu.VMEM(ab.shape, F32)],
         ),
         out_shape=[
             jax.ShapeDtypeStruct((tokens, cols), BF16),
@@ -409,7 +372,7 @@
         compiler_params=pltpu.CompilerParams(vmem_limit_bytes=VMEM_LIMIT, dimension_semantics=("arbitrary",)),
         name="project",
         cost_estimate=cost(tokens, last),
-    )(last_at, *block_operands(hidden, last), ab, c, cd, scale, keep)
+    )(last_at, *block_operands(hidden, last), ab, c, scale, keep)
 
     pieces = lax.all_to_all(gram, "seq", 0, 0, tiled=True)
     piece = jnp.sum(pieces.reshape(seq, 128 * pairs // seq, 128), axis=0)

time: 251 us -> 259 us (1.032)
  waiting for transfers between devices: 58.1 us -> 68.3 us
  starting transfers between devices: 30.4 us -> 26.2 us
  other arithmetic: 9.49 us -> 12.2 us
  Pallas kernels: 98 us -> 95.4 us
    pallas_call x1 -> x0, Pallas kernels: 13.8 us -> none  [accumulate_all(): pl.pallas_call(accumulate_all_kernel, grid=(seq // 2,), in_specs=[pl.Bloc...]
    ppermute x10, waiting for transfers between devices: 55.1 us -> 41.8 us  [send(): return lax.ppermute(v, ('head', 'seq'), plane_pairs(axis, which))]
    ppermute x3, waiting for transfers between devices: 2.9 us -> 15.9 us  [send(): return lax.ppermute(v, ('batch', 'head'), depth_pairs(which))]
    pallas_call x6 -> x7, Pallas kernels: 44.4 us -> 56.7 us  [accumulate(): pl.pallas_call(functools.partial(accumulate_kernel, [parts for _, parts i...]
    all_gather x1, waiting for transfers between devices: 0.01 us -> 10.6 us  [shards(): deep = lax.all_gather(own, 'seq', axis=0, tiled=True)]
    all_to_all x1 -> x0, starting transfers between devices: 6.5 us -> none  [shards(): deep = lax.all_to_all(deep, 'seq', 0, 0).reshape(seq * quarter, DEEP)]
  transfers between devices with their start and end apart: 15 -> 14, of which waited for: 6 -> 9; matrix products, arithmetic and copies ran while one was open for 6% -> 8% of each run, Pallas kernels for 28% -> 26%
where the time goes in v8:
time: 259 us; the launch traced here: 258 us
  Pallas kernels  95.4 us (37%)
  waiting for transfers between devices  68.3 us (26%)
  blocking collectives  31.5 us (12%)
  starting transfers between devices  26.2 us (10%)
  between operations  14.2 us (5%)
  other arithmetic  12.2 us (5%)
  local copies, waits for them, and re-layouts  9.98 us (4%)
    pallas_call x7, Pallas kernels, accumulate(): pl.pallas_call(functools.partial(accumulate_kernel, [parts for _, parts i...  56.7 us
    ppermute x10, waiting for transfers between devices, send(): return lax.ppermute(v, ('head', 'seq'), plane_pairs(axis, which))  41.8 us
    all_to_all x1, blocking collectives, shards(): pieces = lax.all_to_all(gram, 'seq', 0, 0, tiled=True)  17.8 us
    ppermute x3, waiting for transfers between devices, send(): return lax.ppermute(v, ('batch', 'head'), depth_pairs(which))  15.9 us
    ppermute x10, starting transfers between devices, send(): return lax.ppermute(v, ('head', 'seq'), plane_pairs(axis, which))  15.8 us
    pallas_call x1, Pallas kernels, shards(): pl.pallas_call(project_kernel, grid_spec=pltpu.PrefetchScalarGridSpec(num...  15.3 us
    all_to_all x1, blocking collectives, shards(): lax.all_to_all(jnp.broadcast_to(piece, (seq,) + piece.shape), 'seq', 0, 0)  13.7 us
    pallas_call x1, Pallas kernels, shards(): pl.pallas_call(functools.partial(factor_kernel, root_length), out_shape=[...  12.2 us
  transfers between devices with their start and end apart: 14, of which 9 were waited for; matrix products, arithmetic and copies ran while one was open for 8% of the time, Pallas kernels for 26%

profile of v8, /device:TPU:0, one launch (start us, length us, event | category | flops | bytes accessed | tf_op | source)
XLA Modules:
  0.0 257.7 jit_solution(10994900888736359925)
XLA Ops:
  7.2 0.0 all-gather.2.cloned.1.call-start
  7.2 2.1 copy.10
  9.3 0.1 fusion.4
  9.4 1.7 collective-permute-start
  11.1 1.6 collective-permute-start.1
  12.6 8.8 %collective-permute-done = f32[256,768]{1,0:T(8,128)S(1)} collective-permute-done((f32[256,768]{1,0:T(8,128)S(1)}, f32[256,768]{1,0:T(8,128)S(1)}, u32[]{:S(2)}, u32[]{:S(2)}) %collective-permute-start) | collective-permute-done | bytes 786464 | tf_op jit(solution)/shard_map/ppermute | solution.py:269
  21.5 1.6 collective-permute-done.1
  23.0 0.2 pad_maximum_fusion.2
  23.2 2.2 collective-permute-start.2
  25.4 3.0 %collective-permute-start.3 = (f32[512,768]{1,0:T(8,128)S(1)}, f32[512,768]{1,0:T(8,128)}, u32[]{:S(2)}, u32[]{:S(2)}) collective-permute-start(f32[512,768]{1,0:T(8,128)S(1)} %get-tuple-element.50), channel_id=1, source_target_pairs={{0,3},{1,2},{2,1},{3,0},{4,7},{5,6},{6,5},{7,4},{8,11},{9,10},{10,... | collective-permute-start | bytes 4718600 | tf_op jit(solution)/shard_map/ppermute | solution.py:269
  28.4 0.8 slice.17
  29.3 1.6 constant_dynamic-slice_fusion
  30.9 0.0 all-gather.2.cloned.1.call-update
  30.9 1.0 add_convert_fusion
  31.9 1.0 copy.8
  32.9 0.7 concatenate.30.index_ref
  33.6 2.2 pad_maximum_fusion.4.sign_ref
  35.8 11.2 %start.1.start_ref = f32[8,128,128]{2,1,0:T(8,128)} custom-call(f32[8,128,128]{2,1,0:T(8,128)} %pad_maximum_fusion.4.sign_ref), custom_call_target="tpu_custom_call" | custom-call | flops 100000000 | bytes 1000000 | tf_op jit(solution)/shard_map/start/pallas_call | solution.py:319
  47.1 0.1 broadcast_in_dim.13
  47.1 0.7 broadcast_bitcast_fusion.keep_ref
  47.9 0.0 collective-permute-done.2
  47.9 0.5 collective-permute-done.3
  48.4 3.3 %pad_maximum_fusion.1.refs_4_ = f32[1024,768]{1,0:T(8,128)} fusion(f32[512,768]{1,0:T(8,128)} %collective-permute-done.3, f32[512,768]{1,0:T(8,128)S(1)} %get-tuple-element.50), kind=kLoop, calls=%fused_computation.1 | loop fusion | flops 786432 | bytes 6291456 | tf_op jit(solution)/shard_map/concatenate | solution.py:274
  51.7 3.3 %pad_maximum_fusion.refs_2_ = f32[1024,768]{1,0:T(8,128)} fusion(f32[512,768]{1,0:T(8,128)} %collective-permute-done.2, f32[512,768]{1,0:T(8,128)S(1)} %get-tuple-element.49), kind=kLoop, calls=%fused_computation | loop fusion | flops 786432 | bytes 6291456 | tf_op jit(solution)/shard_map/concatenate | solution.py:274
  55.0 0.5 collective-permute-start.4
  55.5 0.6 collective-permute-start.5
  56.1 0.6 concatenate.33.refs_0_
  56.8 9.6 %plane0.1.refs_5_ = f32[512,768]{1,0:T(8,128)} custom-call(s32[8]{0:T(128)} %concatenate.33.refs_0_, f32[512,8192]{1,0:T(8,128)} %xb.1, f32[1024,768]{1,0:T(8,128)} %pad_maximum_fusion.refs_2_, f32[512,8192]{1,0:T(8,128)} %xb.1, f32[1024,768]{1,0:T(8,128)} %pad_maximum_fusion.1.refs_4_), custom_call_target="tpu_custom_call" | custom-call | flops 4831838208 | bytes 10485760 | tf_op jit(solution)/shard_map/plane0/pallas_call | solution.py:111
  66.3 10.6 %all-gather.2.cloned.1.call-done.refs_5_ = f32[2048,256]{1,0:T(8,128)} async-done(((f32[128,256]{1,0:T(8,128)}), f32[2048,256]{1,0:T(8,128)}) %all-gather.2.cloned.1.call-update) | async-done | bytes 2097168 | tf_op jit(solution)/shard_map/all_gather | solution.py:348
  76.9 1.6 collective-permute-start.8
  78.5 0.5 fusion.3.refs_0_
  79.0 6.2 %deep0.1.refs_6_ = f32[512,256]{1,0:T(8,128)} custom-call(s32[16]{0:T(128)} %fusion.3.refs_0_, f32[512,8192]{1,0:T(8,128)} %xb.1, f32[512,8192]{1,0:T(8,128)} %xb.1, f32[512,8192]{1,0:T(8,128)} %xb.1, f32[512,8192]{1,0:T(8,128)} %xb.1, f32[2048,256]{1,0:T(8,128)} %all-gather.2.cloned.1.call-done.refs_5_), custom_call_target="tpu_custom_call" | custom-call | flops 1610612736 | bytes 6291456 | tf_op jit(solution)/shard_map/deep0/pallas_call | solution.py:111
  85.2 15.7 %collective-permute-done.4.refs_2_ = f32[1024,768]{1,0:T(8,128)S(1)} collective-permute-done((f32[1024,768]{1,0:T(8,128)}, f32[1024,768]{1,0:T(8,128)S(1)}, u32[]{:S(2)}, u32[]{:S(2)}) %collective-permute-start.4) | collective-permute-done | bytes 3145760 | tf_op jit(solution)/shard_map/ppermute | solution.py:269
  100.9 0.6 collective-permute-done.5.refs_4_
  101.5 3.4 %collective-permute-start.6 = (f32[1024,768]{1,0:T(8,128)}, f32[1024,768]{1,0:T(8,128)}, u32[]{:S(2)}, u32[]{:S(2)}) collective-permute-start(f32[1024,768]{1,0:T(8,128)} %pad_maximum_fusion.refs_2_), channel_id=1, source_target_pairs={{0,3},{1,2},{2,1},{3,0},{4,7},{5,6},{6,5},{7,4},{8,11},{9,10},{10,... | collective-permute-start | bytes 9437192 | tf_op jit(solution)/shard_map/ppermute | solution.py:269
  104.9 1.3 collective-permute-start.7
  106.2 0.7 concatenate.34.refs_0_
  106.9 0.0 copy-done.3
  106.9 10.4 %plane1.1.refs_5_ = f32[512,768]{1,0:T(8,128)} custom-call(s32[8]{0:T(128)} %concatenate.34.refs_0_, f32[512,8192]{1,0:T(8,128)} %xb.1, f32[1024,768]{1,0:T(8,128)} %copy-done.3, f32[512,8192]{1,0:T(8,128)} %xb.1, f32[1024,768]{1,0:T(8,128)} %collective-permute-done.5.refs_4_, f32[512,768]{1,0:T(8,128)} %plane0.1.refs_5_), custom_call_target="tpu_custom_call" | custom-call | flops 4831838208 | bytes 10485760 | tf_op jit(solution)/shard_map/plane1/pallas_call | solution.py:111
  117.3 0.0 collective-permute-done.8.refs_5_
  117.3 4.4 %collective-permute-start.11 = (f32[2048,256]{1,0:T(8,128)}, f32[2048,256]{1,0:T(8,128)}, u32[]{:S(2)}, u32[]{:S(2)}) collective-permute-start(f32[2048,256]{1,0:T(8,128)} %all-gather.2.cloned.1.call-done.refs_5_), channel_id=1, source_target_pairs={{0,96},{16,48},{32,64},{48,16},{64,32},{80,112},{96,0},{112,80},{1... | collective-permute-start | bytes 6291464 | tf_op jit(solution)/shard_map/ppermute | solution.py:268
  121.7 0.6 fusion.2.refs_0_
  122.3 6.8 %deep1.1.refs_6_ = f32[512,256]{1,0:T(8,128)} custom-call(s32[16]{0:T(128)} %fusion.2.refs_0_, f32[512,8192]{1,0:T(8,128)} %xb.1, f32[512,8192]{1,0:T(8,128)} %xb.1, f32[512,8192]{1,0:T(8,128)} %xb.1, f32[512,8192]{1,0:T(8,128)} %xb.1, f32[2048,256]{1,0:T(8,128)} %collective-permute-done.8.refs_5_, f32[512,256]{1,0:T(8,128)} %deep0.1.refs_6_), custom_call_target="tpu_custom_call" | custom-call | flops 1610612736 | bytes 6291456 | tf_op jit(solution)/shard_map/deep1/pallas_call | solution.py:111
  129.1 11.4 %collective-permute-done.6.refs_2_ = f32[1024,768]{1,0:T(8,128)} collective-permute-done((f32[1024,768]{1,0:T(8,128)}, f32[1024,768]{1,0:T(8,128)}, u32[]{:S(2)}, u32[]{:S(2)}) %collective-permute-start.6) | collective-permute-done | bytes 3145760 | tf_op jit(solution)/shard_map/ppermute | solution.py:269
  140.5 3.2 %collective-permute-done.7.refs_4_ = f32[1024,768]{1,0:T(8,128)} collective-permute-done((f32[1024,768]{1,0:T(8,128)}, f32[1024,768]{1,0:T(8,128)}, u32[]{:S(2)}, u32[]{:S(2)}) %collective-permute-start.7) | collective-permute-done | bytes 3145760 | tf_op jit(solution)/shard_map/ppermute | solution.py:269
  143.7 1.3 collective-permute-start.10
  145.0 0.0 copy-done.4
  145.0 0.3 collective-permute-start.9
  145.3 0.7 concatenate.35.refs_0_
  145.9 10.5 %plane2.1.plane_ref = f32[512,768]{1,0:T(8,128)} custom-call(s32[8]{0:T(128)} %concatenate.35.refs_0_, f32[512,8192]{1,0:T(8,128)} %xb.1, f32[1024,768]{1,0:T(8,128)} %collective-permute-done.6.refs_2_, f32[512,8192]{1,0:T(8,128)} %xb.1, f32[1024,768]{1,0:T(8,128)} %collective-permute-done.7.refs_4_, f32[512,768]{1,0:T(8,128)} %plane1.1.refs_5_), custom_call_target="tpu_custom_call" | custom-call | flops 4831838208 | bytes 10485760 | tf_op jit(solution)/shard_map/plane2/pallas_call | solution.py:111
  156.4 0.0 collective-permute-done.11.refs_5_
  156.4 4.4 %collective-permute-start.12 = (f32[2048,256]{1,0:T(8,128)}, f32[2048,256]{1,0:T(8,128)}, u32[]{:S(2)}, u32[]{:S(2)}) collective-permute-start(f32[2048,256]{1,0:T(8,128)} %collective-permute-done.8.refs_5_), channel_id=1, source_target_pairs={{0,96},{16,48},{32,64},{48,16},{64,32},{80,112},{96,0},{112,80},{1... | collective-permute-start | bytes 6291464 | tf_op jit(solution)/shard_map/ppermute | solution.py:268
  160.9 0.5 fusion.1.refs_0_
  161.4 0.5 fusion.refs_0_
  161.9 0.9 copy.9.scale_ref
  162.8 6.6 %deep2.1.refs_6_ = f32[512,256]{1,0:T(8,128)} custom-call(s32[16]{0:T(128)} %fusion.1.refs_0_, f32[512,8192]{1,0:T(8,128)} %xb.1, f32[512,8192]{1,0:T(8,128)} %xb.1, f32[512,8192]{1,0:T(8,128)} %xb.1, f32[512,8192]{1,0:T(8,128)} %xb.1, f32[2048,256]{1,0:T(8,128)} %collective-permute-done.11.refs_5_, f32[512,256]{1,0:T(8,128)} %deep1.1.refs_6_), custom_call_target="tpu_custom_call" | custom-call | flops 1610612736 | bytes 6291456 | tf_op jit(solution)/shard_map/deep2/pallas_call | solution.py:111
  169.3 15.9 %collective-permute-done.12.refs_5_ = f32[2048,256]{1,0:T(8,128)} collective-permute-done((f32[2048,256]{1,0:T(8,128)}, f32[2048,256]{1,0:T(8,128)}, u32[]{:S(2)}, u32[]{:S(2)}) %collective-permute-start.12) | collective-permute-done | bytes 2097184 | tf_op jit(solution)/shard_map/ppermute | solution.py:268
  185.2 6.5 %deep3.1.depth_ref = f32[512,256]{1,0:T(8,128)} custom-call(s32[16]{0:T(128)} %fusion.refs_0_, f32[512,8192]{1,0:T(8,128)} %xb.1, f32[512,8192]{1,0:T(8,128)} %xb.1, f32[512,8192]{1,0:T(8,128)} %xb.1, f32[512,8192]{1,0:T(8,128)} %xb.1, f32[2048,256]{1,0:T(8,128)} %collective-permute-done.12.refs_5_, f32[512,256]{1,0:T(8,128)} %deep2.1.refs_6_), custom_call_target="tpu_custom_call" | custom-call | flops 1610612736 | bytes 6291456 | tf_op jit(solution)/shard_map/deep3/pallas_call | solution.py:111
  191.7 0.0 collective-permute-done.10.wb
  191.7 0.0 collective-permute-done.9.wa
  191.7 15.3 %project.1 = (bf16[512,1024]{1,0:T(8,128)(2,1)}, bf16[512,1024]{1,0:T(8,128)(2,1)}, f32[1024,128]{1,0:T(8,128)}) custom-call(s32[8]{0:T(128)} %concatenate.30.index_ref, f32[512,8192]{1,0:T(8,128)} %xb.1, f32[1024,768]{1,0:T(8,128)} %collective-permute-done.9.wa, f32[512,8192]{1,0:T(8,128)} %xb.1, f32[1024,768]{1,0:T(8,128)} %collective-permute-done.10.wb, ...), custom_call_target="tpu_custom_call" | custom-call | flops 4831838208 | bytes 10485760 | tf_op jit(solution)/shard_map/project/pallas_call | solution.py:356
  207.1 17.8 %all_to_all.14 = f32[16,64,128]{2,1,0:T(8,128)S(1)} all-to-all(f32[16,64,128]{2,1,0:T(8,128)} %bitcast.46), channel_id=1, replica_groups=mesh['batch'=4,'head'=2,'seq'=16] {'seq'}, dimensions={0} | all-to-all | bytes 1048576 | tf_op jit(solution)/shard_map/all_to_all | solution.py:377
  224.9 13.7 %all_to_all.15 = f32[16,64,128]{2,1,0:T(8,128)S(1)} all-to-all(f32[16,64,128]{2,1,0:T(8,128)S(1)} %broadcast_in_dim.15), channel_id=1, replica_groups=mesh['batch'=4,'head'=2,'seq'=16] {'seq'}, dimensions={0} | all-to-all | bytes 1048576 | tf_op jit(solution)/shard_map/all_to_all | solution.py:379
  238.6 12.2 %factor.1 = (bf16[4,512,128]{2,1,0:T(8,128)(2,1)}, f32[4,128,128]{2,1,0:T(8,128)}) custom-call(f32[1024,128]{1,0:T(8,128)S(1)} %bitcast.41, f32[8,128,128]{2,1,0:T(8,128)S(1)} %copy-done, bf16[512,1024]{1,0:T(8,128)(2,1)S(1)} %copy-done.1, bf16[512,1024]{1,0:T(8,128)(2,1)S(1)} %copy-done.2), custom_call_target="tpu_custom_call" | custom-call | flops 1000000000 | bytes 4194304 | tf_op jit(solution)/shard_map/factor/pallas_call | solution.py:381
  (15 shorter events, 0.1 us)
Async XLA Ops:
  7.2 69.7 %all-gather.2.cloned.1.call-start = ((), (), s32[]{:S(2)}) async-start(), calls=%async_computation.2 | async-start | bytes 2228224 | tf_op jit(solution)/shard_map/all_gather | solution.py:348
  9.4 12.1 %collective-permute-start = (f32[256,768]{1,0:T(8,128)S(1)}, f32[256,768]{1,0:T(8,128)S(1)}, u32[]{:S(2)}, u32[]{:S(2)}) collective-permute-start(f32[256,768]{1,0:T(8,128)S(1)} %get-tuple-element.45), channel_id=1, source_target_pairs={{0,4},{1,5},{2,6},{3,7},{4,0},{5,1},{6,2},{7,3},{8,12},{9,13},{10,... | collective-permute-start | bytes 2359304 | tf_op jit(solution)/shard_map/ppermute | solution.py:269
  11.1 12.0 %collective-permute-start.1 = (f32[256,768]{1,0:T(8,128)S(1)}, f32[256,768]{1,0:T(8,128)S(1)}, u32[]{:S(2)}, u32[]{:S(2)}) collective-permute-start(f32[256,768]{1,0:T(8,128)S(1)} %get-tuple-element.46), channel_id=1, source_target_pairs={{0,1},{1,0},{2,3},{3,2},{4,5},{5,4},{6,7},{7,6},{8,9},{9,8},{10,11... | collective-permute-start | bytes 2359304 | tf_op jit(solution)/shard_map/ppermute | solution.py:269
  23.2 24.6 %collective-permute-start.2 = (f32[512,768]{1,0:T(8,128)S(1)}, f32[512,768]{1,0:T(8,128)}, u32[]{:S(2)}, u32[]{:S(2)}) collective-permute-start(f32[512,768]{1,0:T(8,128)S(1)} %get-tuple-element.49), channel_id=1, source_target_pairs={{0,12},{1,13},{2,14},{3,15},{4,8},{5,9},{6,10},{7,11},{8,4},{9,5},... | collective-permute-start | bytes 4718600 | tf_op jit(solution)/shard_map/ppermute | solution.py:269
  25.4 22.9 %collective-permute-start.3 = (f32[512,768]{1,0:T(8,128)S(1)}, f32[512,768]{1,0:T(8,128)}, u32[]{:S(2)}, u32[]{:S(2)}) collective-permute-start(f32[512,768]{1,0:T(8,128)S(1)} %get-tuple-element.50), channel_id=1, source_target_pairs={{0,3},{1,2},{2,1},{3,0},{4,7},{5,6},{6,5},{7,4},{8,11},{9,10},{10,... | collective-permute-start | bytes 4718600 | tf_op jit(solution)/shard_map/ppermute | solution.py:269
  29.3 17.8 %copy-start.6 = (s32[8,4]{0,1:T(4,128)S(1)}, s32[8,4]{0,1:T(4,128)}, u32[]{:S(2)}) copy-start(s32[8,4]{0,1:T(4,128)} %param.8) | copy-start | bytes 388
  55.0 45.9 %collective-permute-start.4 = (f32[1024,768]{1,0:T(8,128)}, f32[1024,768]{1,0:T(8,128)S(1)}, u32[]{:S(2)}, u32[]{:S(2)}) collective-permute-start(f32[1024,768]{1,0:T(8,128)} %pad_maximum_fusion.refs_2_), channel_id=1, source_target_pairs={{0,1},{1,0},{2,3},{3,2},{4,5},{5,4},{6,7},{7,6},{8,9},{9,8},{10,11... | collective-permute-start | bytes 9437192 | tf_op jit(solution)/shard_map/ppermute | solution.py:269
  55.5 46.0 %collective-permute-start.5 = (f32[1024,768]{1,0:T(8,128)}, f32[1024,768]{1,0:T(8,128)}, u32[]{:S(2)}, u32[]{:S(2)}) collective-permute-start(f32[1024,768]{1,0:T(8,128)} %pad_maximum_fusion.1.refs_4_), channel_id=1, source_target_pairs={{0,4},{1,5},{2,6},{3,7},{4,0},{5,1},{6,2},{7,3},{8,12},{9,13},{10,... | collective-permute-start | bytes 9437192 | tf_op jit(solution)/shard_map/ppermute | solution.py:269
  76.9 40.4 %collective-permute-start.8 = (f32[2048,256]{1,0:T(8,128)}, f32[2048,256]{1,0:T(8,128)}, u32[]{:S(2)}, u32[]{:S(2)}) collective-permute-start(f32[2048,256]{1,0:T(8,128)} %all-gather.2.cloned.1.call-done.refs_5_), channel_id=1, source_target_pairs={{0,32},{16,112},{32,0},{48,80},{64,96},{80,48},{96,64},{112,16},{1... | collective-permute-start | bytes 6291464 | tf_op jit(solution)/shard_map/ppermute | solution.py:268
  100.9 6.0 %copy-start.3 = (f32[1024,768]{1,0:T(8,128)}, f32[1024,768]{1,0:T(8,128)S(1)}, u32[]{:S(2)}) copy-start(f32[1024,768]{1,0:T(8,128)S(1)} %collective-permute-done.4.refs_2_) | copy-start | bytes 9437188
  101.5 39.0 %collective-permute-start.6 = (f32[1024,768]{1,0:T(8,128)}, f32[1024,768]{1,0:T(8,128)}, u32[]{:S(2)}, u32[]{:S(2)}) collective-permute-start(f32[1024,768]{1,0:T(8,128)} %pad_maximum_fusion.refs_2_), channel_id=1, source_target_pairs={{0,3},{1,2},{2,1},{3,0},{4,7},{5,6},{6,5},{7,4},{8,11},{9,10},{10,... | collective-permute-start | bytes 9437192 | tf_op jit(solution)/shard_map/ppermute | solution.py:269
  104.9 38.8 %collective-permute-start.7 = (f32[1024,768]{1,0:T(8,128)}, f32[1024,768]{1,0:T(8,128)}, u32[]{:S(2)}, u32[]{:S(2)}) collective-permute-start(f32[1024,768]{1,0:T(8,128)} %pad_maximum_fusion.1.refs_4_), channel_id=1, source_target_pairs={{0,12},{1,13},{2,14},{3,15},{4,8},{5,9},{6,10},{7,11},{8,4},{9,5},... | collective-permute-start | bytes 9437192 | tf_op jit(solution)/shard_map/ppermute | solution.py:269
  117.3 39.1 %collective-permute-start.11 = (f32[2048,256]{1,0:T(8,128)}, f32[2048,256]{1,0:T(8,128)}, u32[]{:S(2)}, u32[]{:S(2)}) collective-permute-start(f32[2048,256]{1,0:T(8,128)} %all-gather.2.cloned.1.call-done.refs_5_), channel_id=1, source_target_pairs={{0,96},{16,48},{32,64},{48,16},{64,32},{80,112},{96,0},{112,80},{1... | collective-permute-start | bytes 6291464 | tf_op jit(solution)/shard_map/ppermute | solution.py:268
  122.3 22.7 %copy-start.4 = (f32[1024,768]{1,0:T(8,128)S(1)}, f32[1024,768]{1,0:T(8,128)}, u32[]{:S(2)}) copy-start(f32[1024,768]{1,0:T(8,128)} %copy-done.3) | copy-start | bytes 9437188
  143.7 48.0 %collective-permute-start.10 = (f32[1024,768]{1,0:T(8,128)}, f32[1024,768]{1,0:T(8,128)}, u32[]{:S(2)}, u32[]{:S(2)}) collective-permute-start(f32[1024,768]{1,0:T(8,128)} %collective-permute-done.5.refs_4_), channel_id=1, source_target_pairs={{0,12},{1,13},{2,14},{3,15},{4,8},{5,9},{6,10},{7,11},{8,4},{9,5},... | collective-permute-start | bytes 9437192 | tf_op jit(solution)/shard_map/ppermute | solution.py:269
  145.0 46.7 %collective-permute-start.9 = (f32[1024,768]{1,0:T(8,128)S(1)}, f32[1024,768]{1,0:T(8,128)}, u32[]{:S(2)}, u32[]{:S(2)}) collective-permute-start(f32[1024,768]{1,0:T(8,128)S(1)} %copy-done.4), channel_id=1, source_target_pairs={{0,3},{1,2},{2,1},{3,0},{4,7},{5,6},{6,5},{7,4},{8,11},{9,10},{10,... | collective-permute-start | bytes 9437192 | tf_op jit(solution)/shard_map/ppermute | solution.py:269
  145.9 16.0 %copy-start.5 = (f32[512]{0:T(512)S(1)}, f32[512]{0:T(512)}, u32[]{:S(2)}) copy-start(f32[512]{0:T(512)} %param.6) | copy-start | bytes 6148
  156.4 28.7 %collective-permute-start.12 = (f32[2048,256]{1,0:T(8,128)}, f32[2048,256]{1,0:T(8,128)}, u32[]{:S(2)}, u32[]{:S(2)}) collective-permute-start(f32[2048,256]{1,0:T(8,128)} %collective-permute-done.8.refs_5_), channel_id=1, source_target_pairs={{0,96},{16,48},{32,64},{48,16},{64,32},{80,112},{96,0},{112,80},{1... | collective-permute-start | bytes 6291464 | tf_op jit(solution)/shard_map/ppermute | solution.py:268
  207.1 31.6 %copy-start = (f32[8,128,128]{2,1,0:T(8,128)S(1)}, f32[8,128,128]{2,1,0:T(8,128)}, u32[]{:S(2)}) copy-start(f32[8,128,128]{2,1,0:T(8,128)} %start.1.start_ref) | copy-start | bytes 1572868
  207.1 31.6 %copy-start.1 = (bf16[512,1024]{1,0:T(8,128)(2,1)S(1)}, bf16[512,1024]{1,0:T(8,128)(2,1)}, u32[]{:S(2)}) copy-start(bf16[512,1024]{1,0:T(8,128)(2,1)} %get-tuple-element.86.high_ref) | copy-start | bytes 3145732
  207.1 31.6 %copy-start.2 = (bf16[512,1024]{1,0:T(8,128)(2,1)S(1)}, bf16[512,1024]{1,0:T(8,128)(2,1)}, u32[]{:S(2)}) copy-start(bf16[512,1024]{1,0:T(8,128)(2,1)} %get-tuple-element.87.low_ref) | copy-start | bytes 3145732
Sparse Core Ops, SparseCore 0:
  31.0 45.8 all-gather.1

commit v9 on v4

--- a/solution.py
+++ b/solution.py
@@ -15,7 +15,7 @@
 PERMUTED = 512
 DEEP = 256
 WIDE = 256
-UNROLL = 4
+UNROLL = 8
 VMEM_LIMIT = 56 << 20
 F32 = jnp.float32
 BF16 = jnp.bfloat16
@@ -131,8 +131,10 @@
 
     batch, shards_in, quarter, cols = w_ref.shape
     rows = batch * quarter
+    total = 0.0
     for s in range(shards_in):
-        out_ref[...] += three_products(x_ref[:, s * rows : s * rows + rows], w_ref[:, s].reshape(rows, cols))
+        total += three_products(x_ref[:, s * rows : s * rows + rows], w_ref[:, s].reshape(rows, cols))
+    out_ref[...] += total
 
 
 def accumulate_all(hidden, weight):
@@ -140,10 +142,10 @@
     batch, seq, quarter, cols = weight.shape
     return pl.pallas_call(
         accumulate_all_kernel,
-        grid=(seq // 2,),
+        grid=(seq // 4,),
         in_specs=[
-            pl.BlockSpec((tokens, 2 * batch * quarter), lambda k: (0, k)),
-            pl.BlockSpec((batch, 2, quarter, cols), lambda k: (0, k, 0, 0)),
+            pl.BlockSpec((tokens, 4 * batch * quarter), lambda k: (0, k)),
+            pl.BlockSpec((batch, 4, quarter, cols), lambda k: (0, k, 0, 0)),
         ],
         out_specs=pl.BlockSpec((tokens, cols), lambda k: (0, 0)),
         out_shape=jax.ShapeDtypeStruct((tokens, cols), F32),
@@ -202,28 +204,39 @@
 
 
 def inverse_factors(grams):
-    n = len(grams)
+    n = len(grams) // 2
     lane = lax.broadcasted_iota(jnp.int32, (RANK, 128), 1)
     row = lax.broadcasted_iota(jnp.int32, (RANK, 128), 0)
-    unit = jnp.where(lane - RANK == row, 1.0, 0.0).astype(F32)
-    full = jnp.stack([jnp.where(lane < RANK, g, unit) for g in grams])
+    low = lane < RANK
+    full = jnp.stack([jnp.where(low, grams[2 * p], grams[2 * p + 1]) for p in range(n)])
     blocks = [full[:, 8 * i : 8 * i + 8, :] for i in range(RANK // 8)]
-    sub = lax.broadcasted_iota(jnp.int32, (n, 8, 1), 1)
+    lane8 = lax.broadcasted_iota(jnp.int32, (n, 8, 128), 2)
+    sub = lax.broadcasted_iota(jnp.int32, (n, 8, 128), 1)
+    low8, place8 = lane8 < RANK, lane8 % RANK
+
+    def spread(x, at):
+        return jnp.take_along_axis(x.reshape(n * 8, 128), at, axis=1, mode="promise_in_bounds").reshape(n, 8, 128)
+
     for j in range(RANK):
         jb, js = divmod(j, 8)
-        pivot_row = blocks[jb][:, js : js + 1, :]
-        scaled = pivot_row * (1.0 / pivot_row[:, :, j : j + 1])
+        at = jnp.where(low8, j, RANK + j).reshape(n * 8, 128)
+        here = place8 == j
+        pivot_row = jnp.broadcast_to(blocks[jb][:, js : js + 1, :], (n, 8, 128))
+        scaled = jnp.where(here, 1.0, pivot_row) * (1.0 / spread(pivot_row, at))
         for i in range(jb, RANK // 8):
-            column = blocks[i][:, :, j : j + 1]
+            change, gone = spread(blocks[i], at), here
             if i == jb:
-                column = jnp.where(sub > js, column, 0.0)
-            blocks[i] = blocks[i] - column * scaled
+                change, gone = jnp.where(sub > js, change, 0.0), here & (sub > js)
+            blocks[i] = jnp.where(gone, 0.0, blocks[i]) - change * scaled
     full = jnp.concatenate(blocks, axis=1)
+    place = lane % RANK
     out = []
     for p in range(n):
         a = full[p]
-        pivots = jnp.sum(jnp.where(lane == row, a, 0.0), axis=1, keepdims=True)
-        out.append(jnp.where(lane < RANK, 0.0, a) * lax.rsqrt(pivots))
+        for half in (low, ~low):
+            pivots = jnp.sum(jnp.where(half & (place == row), a, 0.0), axis=1, keepdims=True)
+            inverse = jnp.where(place < row, a, jnp.where(place == row, 1.0, 0.0))
+            out.append(jnp.where(half, inverse, 0.0) * lax.rsqrt(pivots))
     return out
 
 

time: 237 us -> 234 us (0.987)
  Pallas kernels: 97.9 us -> 93.7 us
  waiting for transfers between devices: 53.6 us -> 56.6 us
  transfers between devices with their start and end apart: 15 -> 15, of which waited for: 10 -> 11; matrix products, arithmetic and copies ran while one was open for 5% -> 5% of each run, Pallas kernels for 29% -> 28%
where the time goes in v9:
time: 234 us; the launch traced here: 233 us
  Pallas kernels  93.7 us (40%)
  waiting for transfers between devices  56.6 us (24%)
  blocking collectives  28.3 us (12%)
  starting transfers between devices  22.9 us (10%)
  between operations  14.2 us (6%)
  local copies, waits for them, and re-layouts  8.79 us (4%)
  other arithmetic  8.27 us (4%)
    pallas_call x6, Pallas kernels, accumulate(): pl.pallas_call(functools.partial(accumulate_kernel, [parts for _, parts i...  44.3 us
    ppermute x10, waiting for transfers between devices, send(): return lax.ppermute(v, ('head', 'seq'), plane_pairs(axis, which))  29.9 us
    ppermute x10, starting transfers between devices, send(): return lax.ppermute(v, ('head', 'seq'), plane_pairs(axis, which))  16.1 us
    pallas_call x1, Pallas kernels, shards(): pl.pallas_call(project_kernel, grid_spec=pltpu.PrefetchScalarGridSpec(num...  15.3 us
    all_to_all x1, blocking collectives, shards(): pieces = lax.all_to_all(gram, 'seq', 0, 0, tiled=True)  15 us
    all_to_all x1, blocking collectives, shards(): lax.all_to_all(jnp.broadcast_to(piece, (seq,) + piece.shape), 'seq', 0, 0)  13.3 us
    pallas_call x1, Pallas kernels, accumulate_all(): pl.pallas_call(accumulate_all_kernel, grid=(seq // 4,), in_specs=[pl.Bloc...  12.2 us
    pallas_call x1, Pallas kernels, shards(): pl.pallas_call(functools.partial(factor_kernel, root_length), out_shape=[...  12.2 us
  transfers between devices with their start and end apart: 15, of which 11 were waited for; matrix products, arithmetic and copies ran while one was open for 5% of the time, Pallas kernels for 28%

profile of v9, /device:TPU:0, one launch (start us, length us, event | category | flops | bytes accessed | tf_op | source)
XLA Modules:
  0.0 232.7 jit_solution(4059672527966754701)
XLA Ops:
  7.2 0.0 all-gather.4.cloned.1.call-start
  7.2 2.1 copy.10
  9.3 0.1 slice.25
  9.4 0.7 fusion.5
  10.1 0.0 all-gather.4.cloned.1.call-update
  10.1 0.0 all-gather.6.cloned.1.call-start
  10.2 0.7 all-gather.6.cloned.1.call-update
  10.9 0.1 fusion.4
  11.0 0.0 copy-start.5
  11.0 1.7 collective-permute-start
  12.6 1.6 collective-permute-start.1
  14.2 6.0 %collective-permute-done = f32[256,512]{1,0:T(8,128)S(1)} collective-permute-done((f32[256,512]{1,0:T(8,128)S(1)}, f32[256,512]{1,0:T(8,128)S(1)}, u32[]{:S(2)}, u32[]{:S(2)}) %collective-permute-start) | collective-permute-done | bytes 524320 | tf_op jit(solution)/shard_map/ppermute | solution.py:317
  20.2 1.6 collective-permute-done.1
  21.8 0.2 pad_maximum_fusion.2
  22.0 0.0 copy-start.7
  22.0 2.2 collective-permute-start.2
  24.2 3.0 %collective-permute-start.3 = (f32[512,512]{1,0:T(8,128)S(1)}, f32[512,512]{1,0:T(8,128)}, u32[]{:S(2)}, u32[]{:S(2)}) collective-permute-start(f32[512,512]{1,0:T(8,128)S(1)} %get-tuple-element.49), channel_id=1, source_target_pairs={{0,3},{1,2},{2,1},{3,0},{4,7},{5,6},{6,5},{7,4},{8,11},{9,10},{10,... | collective-permute-start | bytes 3145736 | tf_op jit(solution)/shard_map/ppermute | solution.py:317
  27.2 0.2 copy.8
  27.4 0.7 concatenate.30.index_ref
  28.1 1.0 pad_maximum_fusion.4.sign_ref
  29.1 9.8 %start.1.start_ref = f32[8,128,128]{2,1,0:T(8,128)} custom-call(f32[8,128,128]{2,1,0:T(8,128)} %pad_maximum_fusion.4.sign_ref), custom_call_target="tpu_custom_call" | custom-call | flops 100000000 | bytes 1000000 | tf_op jit(solution)/shard_map/start/pallas_call | solution.py:365
  38.9 0.1 broadcast_in_dim.13
  39.0 0.7 broadcast_bitcast_fusion.keep_ref
  39.7 0.6 collective-permute-done.2
  40.3 1.4 collective-permute-done.3
  41.7 2.7 %pad_maximum_fusion.1.refs_4_ = f32[1024,512]{1,0:T(8,128)} fusion(f32[512,512]{1,0:T(8,128)} %collective-permute-done.3, f32[512,512]{1,0:T(8,128)S(1)} %get-tuple-element.49), kind=kLoop, calls=%fused_computation.1 | loop fusion | flops 524288 | bytes 4194304 | tf_op jit(solution)/shard_map/concatenate | solution.py:322
  44.4 2.7 %pad_maximum_fusion.refs_2_ = f32[1024,512]{1,0:T(8,128)} fusion(f32[512,512]{1,0:T(8,128)} %collective-permute-done.2, f32[512,512]{1,0:T(8,128)S(1)} %get-tuple-element.48), kind=kLoop, calls=%fused_computation | loop fusion | flops 524288 | bytes 4194304 | tf_op jit(solution)/shard_map/concatenate | solution.py:322
  47.1 0.5 collective-permute-start.4
  47.6 0.5 collective-permute-start.5
  48.1 0.7 concatenate.33.refs_0_
  48.7 7.9 %plane0.1.refs_5_ = f32[512,512]{1,0:T(8,128)} custom-call(s32[8]{0:T(128)} %concatenate.33.refs_0_, f32[512,8192]{1,0:T(8,128)} %xc3.1, f32[1024,512]{1,0:T(8,128)} %pad_maximum_fusion.refs_2_, f32[512,8192]{1,0:T(8,128)} %xc3.1, f32[1024,512]{1,0:T(8,128)} %pad_maximum_fusion.1.refs_4_), custom_call_target="tpu_custom_call" | custom-call | flops 3221225472 | bytes 8388608 | tf_op jit(solution)/shard_map/plane0/pallas_call | solution.py:112
  56.6 4.6 %all-gather.4.cloned.1.call-done.refs_5_ = f32[2048,256]{1,0:T(8,128)} async-done(((f32[128,256]{1,0:T(8,128)}), f32[2048,256]{1,0:T(8,128)}) %all-gather.4.cloned.1.call-update) | async-done | bytes 2097168 | tf_op jit(solution)/shard_map/all_gather | solution.py:395
  61.2 1.7 collective-permute-start.8
  62.9 0.6 fusion.2.refs_0_
  63.5 6.2 %deep0.1.refs_6_ = f32[512,256]{1,0:T(8,128)} custom-call(s32[16]{0:T(128)} %fusion.2.refs_0_, f32[512,8192]{1,0:T(8,128)} %xc3.1, f32[512,8192]{1,0:T(8,128)} %xc3.1, f32[512,8192]{1,0:T(8,128)} %xc3.1, f32[512,8192]{1,0:T(8,128)} %xc3.1, f32[2048,256]{1,0:T(8,128)} %all-gather.4.cloned.1.call-done.refs_5_), custom_call_target="tpu_custom_call" | custom-call | flops 1610612736 | bytes 6291456 | tf_op jit(solution)/shard_map/deep0/pallas_call | solution.py:112
  69.7 8.7 %collective-permute-done.4.refs_2_ = f32[1024,512]{1,0:T(8,128)} collective-permute-done((f32[1024,512]{1,0:T(8,128)}, f32[1024,512]{1,0:T(8,128)}, u32[]{:S(2)}, u32[]{:S(2)}) %collective-permute-start.4) | collective-permute-done | bytes 2097184 | tf_op jit(solution)/shard_map/ppermute | solution.py:317
  78.5 0.8 collective-permute-done.5.refs_4_
  79.3 1.4 collective-permute-start.6
  80.7 1.8 collective-permute-start.7
  82.5 0.7 concatenate.34.refs_0_
  83.2 8.5 %plane1.1.refs_5_ = f32[512,512]{1,0:T(8,128)} custom-call(s32[8]{0:T(128)} %concatenate.34.refs_0_, f32[512,8192]{1,0:T(8,128)} %xc3.1, f32[1024,512]{1,0:T(8,128)} %collective-permute-done.4.refs_2_, f32[512,8192]{1,0:T(8,128)} %xc3.1, f32[1024,512]{1,0:T(8,128)} %collective-permute-done.5.refs_4_, f32[512,512]{1,0:T(8,128)} %plane0.1.refs_5_), custom_call_target="tpu_custom_call" | custom-call | flops 3221225472 | bytes 8388608 | tf_op jit(solution)/shard_map/plane1/pallas_call | solution.py:112
  91.7 0.0 collective-permute-done.8.refs_5_
  91.7 2.7 %collective-permute-start.11 = (f32[2048,256]{1,0:T(8,128)}, f32[2048,256]{1,0:T(8,128)}, u32[]{:S(2)}, u32[]{:S(2)}) collective-permute-start(f32[2048,256]{1,0:T(8,128)} %all-gather.4.cloned.1.call-done.refs_5_), channel_id=1, source_target_pairs={{0,96},{16,48},{32,64},{48,16},{64,32},{80,112},{96,0},{112,80},{1... | collective-permute-start | bytes 6291464 | tf_op jit(solution)/shard_map/ppermute | solution.py:316
  94.4 0.6 concatenate.35.refs_0_
  95.0 0.5 fusion.1.refs_0_
  95.5 6.6 %deep1.1.refs_6_ = f32[512,256]{1,0:T(8,128)} custom-call(s32[16]{0:T(128)} %fusion.1.refs_0_, f32[512,8192]{1,0:T(8,128)} %xc3.1, f32[512,8192]{1,0:T(8,128)} %xc3.1, f32[512,8192]{1,0:T(8,128)} %xc3.1, f32[512,8192]{1,0:T(8,128)} %xc3.1, f32[2048,256]{1,0:T(8,128)} %collective-permute-done.8.refs_5_, f32[512,256]{1,0:T(8,128)} %deep0.1.refs_6_), custom_call_target="tpu_custom_call" | custom-call | flops 1610612736 | bytes 6291456 | tf_op jit(solution)/shard_map/deep1/pallas_call | solution.py:112
  102.1 10.7 %collective-permute-done.6.refs_2_ = f32[1024,512]{1,0:T(8,128)S(1)} collective-permute-done((f32[1024,512]{1,0:T(8,128)}, f32[1024,512]{1,0:T(8,128)S(1)}, u32[]{:S(2)}, u32[]{:S(2)}) %collective-permute-start.6) | collective-permute-done | bytes 2097184 | tf_op jit(solution)/shard_map/ppermute | solution.py:317
  112.8 1.3 copy-done.4
  114.1 0.0 collective-permute-done.7.refs_4_
  114.1 1.9 collective-permute-start.10
  116.0 1.7 collective-permute-start.9
  117.7 8.4 %plane2.1.ab_ref = f32[512,512]{1,0:T(8,128)} custom-call(s32[8]{0:T(128)} %concatenate.35.refs_0_, f32[512,8192]{1,0:T(8,128)} %xc3.1, f32[1024,512]{1,0:T(8,128)} %copy-done.4, f32[512,8192]{1,0:T(8,128)} %xc3.1, f32[1024,512]{1,0:T(8,128)} %collective-permute-done.7.refs_4_, f32[512,512]{1,0:T(8,128)} %plane1.1.refs_5_), custom_call_target="tpu_custom_call" | custom-call | flops 3221225472 | bytes 8388608 | tf_op jit(solution)/shard_map/plane2/pallas_call | solution.py:112
  126.1 8.3 %collective-permute-done.11.refs_5_ = f32[2048,256]{1,0:T(8,128)} collective-permute-done((f32[2048,256]{1,0:T(8,128)}, f32[2048,256]{1,0:T(8,128)}, u32[]{:S(2)}, u32[]{:S(2)}) %collective-permute-start.11) | collective-permute-done | bytes 2097184 | tf_op jit(solution)/shard_map/ppermute | solution.py:316
  134.4 2.3 collective-permute-start.12
  136.7 0.5 fusion.refs_0_
  137.2 0.9 copy.9.scale_ref
  138.1 6.6 %deep2.1.c_ref = f32[512,256]{1,0:T(8,128)} custom-call(s32[16]{0:T(128)} %fusion.refs_0_, f32[512,8192]{1,0:T(8,128)} %xc3.1, f32[512,8192]{1,0:T(8,128)} %xc3.1, f32[512,8192]{1,0:T(8,128)} %xc3.1, f32[512,8192]{1,0:T(8,128)} %xc3.1, f32[2048,256]{1,0:T(8,128)} %collective-permute-done.11.refs_5_, f32[512,256]{1,0:T(8,128)} %deep1.1.refs_6_), custom_call_target="tpu_custom_call" | custom-call | flops 1610612736 | bytes 6291456 | tf_op jit(solution)/shard_map/deep2/pallas_call | solution.py:112
  144.7 9.6 %all-gather.6.cloned.1.call-done = f32[8192,256]{1,0:T(8,128)} async-done(((f32[128,256]{1,0:T(8,128)}), f32[8192,256]{1,0:T(8,128)}) %all-gather.6.cloned.1.call-update) | async-done | bytes 8388624 | tf_op jit(solution)/shard_map/all_gather | solution.py:397
  154.3 12.2 %rest.1.rest_ref = f32[512,256]{1,0:T(8,128)} custom-call(f32[512,8192]{1,0:T(8,128)} %xc3.1, f32[4,16,128,256]{3,2,1,0:T(8,128)} %bitcast.43), custom_call_target="tpu_custom_call" | custom-call | flops 6442450944 | bytes 25165824 | tf_op jit(solution)/shard_map/rest/pallas_call | solution.py:143
  166.5 3.5 %collective-permute-done.12.wc = f32[2048,256]{1,0:T(8,128)} collective-permute-done((f32[2048,256]{1,0:T(8,128)}, f32[2048,256]{1,0:T(8,128)}, u32[]{:S(2)}, u32[]{:S(2)}) %collective-permute-start.12) | collective-permute-done | bytes 2097184 | tf_op jit(solution)/shard_map/ppermute | solution.py:316
  170.0 15.3 %project.1 = (bf16[512,1024]{1,0:T(8,128)(2,1)}, bf16[512,1024]{1,0:T(8,128)(2,1)}, f32[1024,128]{1,0:T(8,128)}) custom-call(s32[24]{0:T(128)} %concatenate.30.index_ref, f32[512,8192]{1,0:T(8,128)} %xc3.1, f32[1024,512]{1,0:T(8,128)} %collective-permute-done.9.wa, f32[512,8192]{1,0:T(8,128)} %xc3.1, f32[1024,512]{1,0:T(8,128)} %copy-done.3, ...), custom_call_target="tpu_custom_call" | custom-call | flops 4831838208 | bytes 14680064 | tf_op jit(solution)/shard_map/project/pallas_call | solution.py:406
  185.3 15.0 %all_to_all.14 = f32[16,64,128]{2,1,0:T(8,128)S(1)} all-to-all(f32[16,64,128]{2,1,0:T(8,128)} %bitcast.48), channel_id=1, replica_groups=mesh['batch'=4,'head'=2,'seq'=16] {'seq'}, dimensions={0} | all-to-all | bytes 1048576 | tf_op jit(solution)/shard_map/all_to_all | solution.py:427
  200.4 13.3 %all_to_all.15 = f32[16,64,128]{2,1,0:T(8,128)S(1)} all-to-all(f32[16,64,128]{2,1,0:T(8,128)S(1)} %broadcast_in_dim.15), channel_id=1, replica_groups=mesh['batch'=4,'head'=2,'seq'=16] {'seq'}, dimensions={0} | all-to-all | bytes 1048576 | tf_op jit(solution)/shard_map/all_to_all | solution.py:429
  213.8 12.2 %factor.1 = (bf16[4,512,128]{2,1,0:T(8,128)(2,1)}, f32[4,128,128]{2,1,0:T(8,128)}) custom-call(f32[1024,128]{1,0:T(8,128)S(1)} %bitcast.42, f32[8,128,128]{2,1,0:T(8,128)S(1)} %copy-done, bf16[512,1024]{1,0:T(8,128)(2,1)S(1)} %copy-done.1, bf16[512,1024]{1,0:T(8,128)(2,1)S(1)} %copy-done.2), custom_call_target="tpu_custom_call" | custom-call | flops 1000000000 | bytes 4194304 | tf_op jit(solution)/shard_map/factor/pallas_call | solution.py:431
  (20 shorter events, 0.1 us)
Async XLA Ops:
  7.2 54.1 %all-gather.4.cloned.1.call-start = ((), (), s32[]{:S(2)}) async-start(), calls=%async_computation.2 | async-start | bytes 2228224 | tf_op jit(solution)/shard_map/all_gather | solution.py:395
  10.1 144.2 %all-gather.6.cloned.1.call-start = ((), (), s32[]{:S(2)}) async-start(), calls=%async_computation.3 | async-start | bytes 8519680 | tf_op jit(solution)/shard_map/all_gather | solution.py:397
  11.0 16.2 %copy-start.5 = (s32[4,2,128,64]{2,3,1,0:T(8,128)S(1)}, s32[4,2,128,64]{2,3,1,0:T(8,128)}, u32[]{:S(2)}) copy-start(s32[4,2,128,64]{2,3,1,0:T(8,128)} %param.9) | copy-start | bytes 786436
  11.0 9.3 %collective-permute-start = (f32[256,512]{1,0:T(8,128)S(1)}, f32[256,512]{1,0:T(8,128)S(1)}, u32[]{:S(2)}, u32[]{:S(2)}) collective-permute-start(f32[256,512]{1,0:T(8,128)S(1)} %get-tuple-element.44), channel_id=1, source_target_pairs={{0,4},{1,5},{2,6},{3,7},{4,0},{5,1},{6,2},{7,3},{8,12},{9,13},{10,... | collective-permute-start | bytes 1572872 | tf_op jit(solution)/shard_map/ppermute | solution.py:317
  12.6 9.2 %collective-permute-start.1 = (f32[256,512]{1,0:T(8,128)S(1)}, f32[256,512]{1,0:T(8,128)S(1)}, u32[]{:S(2)}, u32[]{:S(2)}) collective-permute-start(f32[256,512]{1,0:T(8,128)S(1)} %get-tuple-element.45), channel_id=1, source_target_pairs={{0,1},{1,0},{2,3},{3,2},{4,5},{5,4},{6,7},{7,6},{8,9},{9,8},{10,11... | collective-permute-start | bytes 1572872 | tf_op jit(solution)/shard_map/ppermute | solution.py:317
  22.0 16.9 %copy-start.7 = (s32[8,4]{0,1:T(4,128)S(1)}, s32[8,4]{0,1:T(4,128)}, u32[]{:S(2)}) copy-start(s32[8,4]{0,1:T(4,128)} %param.8) | copy-start | bytes 388
  22.0 18.3 %collective-permute-start.2 = (f32[512,512]{1,0:T(8,128)S(1)}, f32[512,512]{1,0:T(8,128)}, u32[]{:S(2)}, u32[]{:S(2)}) collective-permute-start(f32[512,512]{1,0:T(8,128)S(1)} %get-tuple-element.48), channel_id=1, source_target_pairs={{0,12},{1,13},{2,14},{3,15},{4,8},{5,9},{6,10},{7,11},{8,4},{9,5},... | collective-permute-start | bytes 3145736 | tf_op jit(solution)/shard_map/ppermute | solution.py:317
  24.2 17.5 %collective-permute-start.3 = (f32[512,512]{1,0:T(8,128)S(1)}, f32[512,512]{1,0:T(8,128)}, u32[]{:S(2)}, u32[]{:S(2)}) collective-permute-start(f32[512,512]{1,0:T(8,128)S(1)} %get-tuple-element.49), channel_id=1, source_target_pairs={{0,3},{1,2},{2,1},{3,0},{4,7},{5,6},{6,5},{7,4},{8,11},{9,10},{10,... | collective-permute-start | bytes 3145736 | tf_op jit(solution)/shard_map/ppermute | solution.py:317
  47.1 31.4 %collective-permute-start.4 = (f32[1024,512]{1,0:T(8,128)}, f32[1024,512]{1,0:T(8,128)}, u32[]{:S(2)}, u32[]{:S(2)}) collective-permute-start(f32[1024,512]{1,0:T(8,128)} %pad_maximum_fusion.refs_2_), channel_id=1, source_target_pairs={{0,1},{1,0},{2,3},{3,2},{4,5},{5,4},{6,7},{7,6},{8,9},{9,8},{10,11... | collective-permute-start | bytes 6291464 | tf_op jit(solution)/shard_map/ppermute | solution.py:317
  47.6 31.7 %collective-permute-start.5 = (f32[1024,512]{1,0:T(8,128)}, f32[1024,512]{1,0:T(8,128)}, u32[]{:S(2)}, u32[]{:S(2)}) collective-permute-start(f32[1024,512]{1,0:T(8,128)} %pad_maximum_fusion.1.refs_4_), channel_id=1, source_target_pairs={{0,4},{1,5},{2,6},{3,7},{4,0},{5,1},{6,2},{7,3},{8,12},{9,13},{10,... | collective-permute-start | bytes 6291464 | tf_op jit(solution)/shard_map/ppermute | solution.py:317
  61.2 30.4 %collective-permute-start.8 = (f32[2048,256]{1,0:T(8,128)}, f32[2048,256]{1,0:T(8,128)}, u32[]{:S(2)}, u32[]{:S(2)}) collective-permute-start(f32[2048,256]{1,0:T(8,128)} %all-gather.4.cloned.1.call-done.refs_5_), channel_id=1, source_target_pairs={{0,32},{16,112},{32,0},{48,80},{64,96},{80,48},{96,64},{112,16},{1... | collective-permute-start | bytes 6291464 | tf_op jit(solution)/shard_map/ppermute | solution.py:316
  79.3 33.5 %collective-permute-start.6 = (f32[1024,512]{1,0:T(8,128)}, f32[1024,512]{1,0:T(8,128)S(1)}, u32[]{:S(2)}, u32[]{:S(2)}) collective-permute-start(f32[1024,512]{1,0:T(8,128)} %pad_maximum_fusion.refs_2_), channel_id=1, source_target_pairs={{0,3},{1,2},{2,1},{3,0},{4,7},{5,6},{6,5},{7,4},{8,11},{9,10},{10,... | collective-permute-start | bytes 6291464 | tf_op jit(solution)/shard_map/ppermute | solution.py:317
  80.7 33.5 %collective-permute-start.7 = (f32[1024,512]{1,0:T(8,128)}, f32[1024,512]{1,0:T(8,128)}, u32[]{:S(2)}, u32[]{:S(2)}) collective-permute-start(f32[1024,512]{1,0:T(8,128)} %pad_maximum_fusion.1.refs_4_), channel_id=1, source_target_pairs={{0,12},{1,13},{2,14},{3,15},{4,8},{5,9},{6,10},{7,11},{8,4},{9,5},... | collective-permute-start | bytes 6291464 | tf_op jit(solution)/shard_map/ppermute | solution.py:317
  91.7 42.8 %collective-permute-start.11 = (f32[2048,256]{1,0:T(8,128)}, f32[2048,256]{1,0:T(8,128)}, u32[]{:S(2)}, u32[]{:S(2)}) collective-permute-start(f32[2048,256]{1,0:T(8,128)} %all-gather.4.cloned.1.call-done.refs_5_), channel_id=1, source_target_pairs={{0,96},{16,48},{32,64},{48,16},{64,32},{80,112},{96,0},{112,80},{1... | collective-permute-start | bytes 6291464 | tf_op jit(solution)/shard_map/ppermute | solution.py:316
  102.1 35.2 %copy-start.6 = (f32[512]{0:T(512)S(1)}, f32[512]{0:T(512)}, u32[]{:S(2)}) copy-start(f32[512]{0:T(512)} %param.6) | copy-start | bytes 6148
  112.8 1.3 copy-start.4
  114.1 52.4 %collective-permute-start.10 = (f32[1024,512]{1,0:T(8,128)}, f32[1024,512]{1,0:T(8,128)S(1)}, u32[]{:S(2)}, u32[]{:S(2)}) collective-permute-start(f32[1024,512]{1,0:T(8,128)} %collective-permute-done.5.refs_4_), channel_id=1, source_target_pairs={{0,12},{1,13},{2,14},{3,15},{4,8},{5,9},{6,10},{7,11},{8,4},{9,5},... | collective-permute-start | bytes 6291464 | tf_op jit(solution)/shard_map/ppermute | solution.py:317
  116.0 50.5 %collective-permute-start.9 = (f32[1024,512]{1,0:T(8,128)}, f32[1024,512]{1,0:T(8,128)}, u32[]{:S(2)}, u32[]{:S(2)}) collective-permute-start(f32[1024,512]{1,0:T(8,128)} %collective-permute-done.4.refs_2_), channel_id=1, source_target_pairs={{0,3},{1,2},{2,1},{3,0},{4,7},{5,6},{6,5},{7,4},{8,11},{9,10},{10,... | collective-permute-start | bytes 6291464 | tf_op jit(solution)/shard_map/ppermute | solution.py:317
  134.4 35.6 %collective-permute-start.12 = (f32[2048,256]{1,0:T(8,128)}, f32[2048,256]{1,0:T(8,128)}, u32[]{:S(2)}, u32[]{:S(2)}) collective-permute-start(f32[2048,256]{1,0:T(8,128)} %collective-permute-done.8.refs_5_), channel_id=1, source_target_pairs={{0,96},{16,48},{32,64},{48,16},{64,32},{80,112},{96,0},{112,80},{1... | collective-permute-start | bytes 6291464 | tf_op jit(solution)/shard_map/ppermute | solution.py:316
  166.5 3.5 %copy-start.3 = (f32[1024,512]{1,0:T(8,128)}, f32[1024,512]{1,0:T(8,128)S(1)}, u32[]{:S(2)}) copy-start(f32[1024,512]{1,0:T(8,128)S(1)} %collective-permute-done.10.wb) | copy-start | bytes 6291460
  185.3 28.5 %copy-start = (f32[8,128,128]{2,1,0:T(8,128)S(1)}, f32[8,128,128]{2,1,0:T(8,128)}, u32[]{:S(2)}) copy-start(f32[8,128,128]{2,1,0:T(8,128)} %start.1.start_ref) | copy-start | bytes 1572868
  185.3 28.5 %copy-start.1 = (bf16[512,1024]{1,0:T(8,128)(2,1)S(1)}, bf16[512,1024]{1,0:T(8,128)(2,1)}, u32[]{:S(2)}) copy-start(bf16[512,1024]{1,0:T(8,128)(2,1)} %get-tuple-element.84.high_ref) | copy-start | bytes 3145732
  185.3 28.5 %copy-start.2 = (bf16[512,1024]{1,0:T(8,128)(2,1)S(1)}, bf16[512,1024]{1,0:T(8,128)(2,1)}, u32[]{:S(2)}) copy-start(bf16[512,1024]{1,0:T(8,128)(2,1)} %get-tuple-element.85.low_ref) | copy-start | bytes 3145732
Sparse Core Ops, SparseCore 0:
  10.7 50.4 all-gather.3
  64.1 90.1 all-gather.5

commit v10 on v9

--- a/solution.py
+++ b/solution.py
@@ -339,11 +339,11 @@
     depth = multiply(None, (deep0,), 0)
     plane1, plane0, plane, depth = barrier((plane1, plane0, plane, depth))
     plane2 = to_y_x(plane0, 1)
+    deep1, deep0, plane1 = barrier((deep1, deep0, plane1))
+    deep2 = send(deep0, "z", 1)
     plane = multiply(plane, plane1, 1)
-    deep1, deep0, plane = barrier((deep1, deep0, plane))
-    deep2 = send(deep0, "z", 1)
     depth = multiply(depth, (deep1,), 1)
-    plane2, plane1, depth = barrier((plane2, plane1, depth))
+    plane2, plane1, plane, depth = barrier((plane2, plane1, plane, depth))
     plane3 = to_y_x(plane1, 1)
     plane = multiply(plane, plane2, 2)
     deep2, deep1, plane = barrier((deep2, deep1, plane))

time: 234 us -> 234 us (level)
  waiting for transfers between devices: 56.6 us -> 53.7 us
  blocking collectives: 28.3 us -> 31.1 us
    ppermute x10, waiting for transfers between devices: 29.9 us -> 24.5 us  [send(): return lax.ppermute(v, ('head', 'seq'), plane_pairs(axis, which))]
  transfers between devices with their start and end apart: 15 -> 15, of which waited for: 11 -> 13; matrix products, arithmetic and copies ran while one was open for 5% -> 5% of each run, Pallas kernels for 28% -> 28%
where the time goes in v10:
time: 234 us; the launch traced here: 233 us
  Pallas kernels  93.6 us (40%)
  waiting for transfers between devices  53.7 us (23%)
  blocking collectives  31.1 us (13%)
  starting transfers between devices  24.3 us (10%)
  between operations  14.2 us (6%)
  other arithmetic  8.24 us (4%)
  local copies, waits for them, and re-layouts  7.97 us (3%)
    pallas_call x6, Pallas kernels, accumulate(): pl.pallas_call(functools.partial(accumulate_kernel, [parts for _, parts i...  44.2 us
    ppermute x10, waiting for transfers between devices, send(): return lax.ppermute(v, ('head', 'seq'), plane_pairs(axis, which))  24.5 us
    all_to_all x1, blocking collectives, shards(): pieces = lax.all_to_all(gram, 'seq', 0, 0, tiled=True)  17.3 us
    ppermute x10, starting transfers between devices, send(): return lax.ppermute(v, ('head', 'seq'), plane_pairs(axis, which))  16.2 us
    pallas_call x1, Pallas kernels, shards(): pl.pallas_call(project_kernel, grid_spec=pltpu.PrefetchScalarGridSpec(num...  15.2 us
    all_to_all x1, blocking collectives, shards(): lax.all_to_all(jnp.broadcast_to(piece, (seq,) + piece.shape), 'seq', 0, 0)  13.8 us
    pallas_call x1, Pallas kernels, accumulate_all(): pl.pallas_call(accumulate_all_kernel, grid=(seq // 4,), in_specs=[pl.Bloc...  12.2 us
    pallas_call x1, Pallas kernels, shards(): pl.pallas_call(functools.partial(factor_kernel, root_length), out_shape=[...  12.2 us
  transfers between devices with their start and end apart: 15, of which 13 were waited for; matrix products, arithmetic and copies ran while one was open for 5% of the time, Pallas kernels for 28%

profile of v10, /device:TPU:0, one launch (start us, length us, event | category | flops | bytes accessed | tf_op | source)
XLA Modules:
  0.0 233.2 jit_solution(8520093260218670644)
XLA Ops:
  7.2 0.0 all-gather.4.cloned.1.call-start
  7.2 2.1 copy.10
  9.3 0.1 slice.25
  9.4 0.7 fusion.5
  10.1 0.0 all-gather.4.cloned.1.call-update
  10.1 0.0 all-gather.6.cloned.1.call-start
  10.2 0.7 all-gather.6.cloned.1.call-update
  10.9 0.1 fusion.4
  11.0 0.0 copy-start.5
  11.0 1.7 collective-permute-start
  12.6 1.6 collective-permute-start.1
  14.2 6.0 %collective-permute-done = f32[256,512]{1,0:T(8,128)S(1)} collective-permute-done((f32[256,512]{1,0:T(8,128)S(1)}, f32[256,512]{1,0:T(8,128)S(1)}, u32[]{:S(2)}, u32[]{:S(2)}) %collective-permute-start) | collective-permute-done | bytes 524320 | tf_op jit(solution)/shard_map/ppermute | solution.py:317
  20.2 1.6 collective-permute-done.1
  21.8 0.2 pad_maximum_fusion.2
  22.0 0.0 copy-start.7
  22.0 2.2 collective-permute-start.2
  24.2 3.0 %collective-permute-start.3 = (f32[512,512]{1,0:T(8,128)S(1)}, f32[512,512]{1,0:T(8,128)}, u32[]{:S(2)}, u32[]{:S(2)}) collective-permute-start(f32[512,512]{1,0:T(8,128)S(1)} %get-tuple-element.51), channel_id=1, source_target_pairs={{0,3},{1,2},{2,1},{3,0},{4,7},{5,6},{6,5},{7,4},{8,11},{9,10},{10,... | collective-permute-start | bytes 3145736 | tf_op jit(solution)/shard_map/ppermute | solution.py:317
  27.2 0.2 copy.8
  27.5 0.7 concatenate.30.index_ref
  28.1 1.0 pad_maximum_fusion.4.sign_ref
  29.1 9.8 %start.1.start_ref = f32[8,128,128]{2,1,0:T(8,128)} custom-call(f32[8,128,128]{2,1,0:T(8,128)} %pad_maximum_fusion.4.sign_ref), custom_call_target="tpu_custom_call" | custom-call | flops 100000000 | bytes 1000000 | tf_op jit(solution)/shard_map/start/pallas_call | solution.py:365
  39.0 0.1 broadcast_in_dim.13
  39.1 0.7 broadcast_bitcast_fusion.keep_ref
  39.8 0.5 collective-permute-done.2
  40.3 1.4 collective-permute-done.3
  41.7 2.7 %pad_maximum_fusion.1.refs_4_ = f32[1024,512]{1,0:T(8,128)} fusion(f32[512,512]{1,0:T(8,128)} %collective-permute-done.3, f32[512,512]{1,0:T(8,128)S(1)} %get-tuple-element.51), kind=kLoop, calls=%fused_computation.1 | loop fusion | flops 524288 | bytes 4194304 | tf_op jit(solution)/shard_map/concatenate | solution.py:322
  44.4 2.7 %pad_maximum_fusion.refs_2_ = f32[1024,512]{1,0:T(8,128)} fusion(f32[512,512]{1,0:T(8,128)} %collective-permute-done.2, f32[512,512]{1,0:T(8,128)S(1)} %get-tuple-element.50), kind=kLoop, calls=%fused_computation | loop fusion | flops 524288 | bytes 4194304 | tf_op jit(solution)/shard_map/concatenate | solution.py:322
  47.1 0.5 collective-permute-start.4
  47.6 0.5 collective-permute-start.5
  48.1 0.6 concatenate.33.refs_0_
  48.7 7.9 %plane0.1.refs_5_ = f32[512,512]{1,0:T(8,128)} custom-call(s32[8]{0:T(128)} %concatenate.33.refs_0_, f32[512,8192]{1,0:T(8,128)} %xc3.1, f32[1024,512]{1,0:T(8,128)} %pad_maximum_fusion.refs_2_, f32[512,8192]{1,0:T(8,128)} %xc3.1, f32[1024,512]{1,0:T(8,128)} %pad_maximum_fusion.1.refs_4_), custom_call_target="tpu_custom_call" | custom-call | flops 3221225472 | bytes 8388608 | tf_op jit(solution)/shard_map/plane0/pallas_call | solution.py:112
  56.6 4.6 %all-gather.4.cloned.1.call-done.refs_5_ = f32[2048,256]{1,0:T(8,128)} async-done(((f32[128,256]{1,0:T(8,128)}), f32[2048,256]{1,0:T(8,128)}) %all-gather.4.cloned.1.call-update) | async-done | bytes 2097168 | tf_op jit(solution)/shard_map/all_gather | solution.py:395
  61.2 1.7 collective-permute-start.8
  62.9 0.5 fusion.2.refs_0_
  63.4 6.3 %deep0.1.refs_6_ = f32[512,256]{1,0:T(8,128)} custom-call(s32[16]{0:T(128)} %fusion.2.refs_0_, f32[512,8192]{1,0:T(8,128)} %xc3.1, f32[512,8192]{1,0:T(8,128)} %xc3.1, f32[512,8192]{1,0:T(8,128)} %xc3.1, f32[512,8192]{1,0:T(8,128)} %xc3.1, f32[2048,256]{1,0:T(8,128)} %all-gather.4.cloned.1.call-done.refs_5_), custom_call_target="tpu_custom_call" | custom-call | flops 1610612736 | bytes 6291456 | tf_op jit(solution)/shard_map/deep0/pallas_call | solution.py:112
  69.7 8.7 %collective-permute-done.4.refs_2_ = f32[1024,512]{1,0:T(8,128)S(1)} collective-permute-done((f32[1024,512]{1,0:T(8,128)}, f32[1024,512]{1,0:T(8,128)S(1)}, u32[]{:S(2)}, u32[]{:S(2)}) %collective-permute-start.4) | collective-permute-done | bytes 2097184 | tf_op jit(solution)/shard_map/ppermute | solution.py:317
  78.4 0.9 collective-permute-done.5.refs_4_
  79.3 1.4 collective-permute-start.6
  80.7 1.7 collective-permute-start.7
  82.4 6.6 %collective-permute-done.8.refs_5_ = f32[2048,256]{1,0:T(8,128)} collective-permute-done((f32[2048,256]{1,0:T(8,128)}, f32[2048,256]{1,0:T(8,128)}, u32[]{:S(2)}, u32[]{:S(2)}) %collective-permute-start.8) | collective-permute-done | bytes 2097184 | tf_op jit(solution)/shard_map/ppermute | solution.py:316
  89.0 2.7 %collective-permute-start.11 = (f32[2048,256]{1,0:T(8,128)}, f32[2048,256]{1,0:T(8,128)}, u32[]{:S(2)}, u32[]{:S(2)}) collective-permute-start(f32[2048,256]{1,0:T(8,128)} %all-gather.4.cloned.1.call-done.refs_5_), channel_id=1, source_target_pairs={{0,96},{16,48},{32,64},{48,16},{64,32},{80,112},{96,0},{112,80},{1... | collective-permute-start | bytes 6291464 | tf_op jit(solution)/shard_map/ppermute | solution.py:316
  91.7 0.7 concatenate.34.refs_0_
  92.4 0.7 concatenate.35.refs_0_
  93.0 0.5 fusion.1.refs_0_
  93.5 6.6 %deep1.1.refs_6_ = f32[512,256]{1,0:T(8,128)} custom-call(s32[16]{0:T(128)} %fusion.1.refs_0_, f32[512,8192]{1,0:T(8,128)} %xc3.1, f32[512,8192]{1,0:T(8,128)} %xc3.1, f32[512,8192]{1,0:T(8,128)} %xc3.1, f32[512,8192]{1,0:T(8,128)} %xc3.1, f32[2048,256]{1,0:T(8,128)} %collective-permute-done.8.refs_5_, f32[512,256]{1,0:T(8,128)} %deep0.1.refs_6_), custom_call_target="tpu_custom_call" | custom-call | flops 1610612736 | bytes 6291456 | tf_op jit(solution)/shard_map/deep1/pallas_call | solution.py:112
  100.1 8.5 %plane1.1.refs_5_ = f32[512,512]{1,0:T(8,128)} custom-call(s32[8]{0:T(128)} %concatenate.34.refs_0_, f32[512,8192]{1,0:T(8,128)} %xc3.1, f32[1024,512]{1,0:T(8,128)} %copy-done.4, f32[512,8192]{1,0:T(8,128)} %xc3.1, f32[1024,512]{1,0:T(8,128)} %collective-permute-done.5.refs_4_, f32[512,512]{1,0:T(8,128)} %plane0.1.refs_5_), custom_call_target="tpu_custom_call" | custom-call | flops 3221225472 | bytes 8388608 | tf_op jit(solution)/shard_map/plane1/pallas_call | solution.py:112
  108.6 4.3 %collective-permute-done.6.refs_2_ = f32[1024,512]{1,0:T(8,128)} collective-permute-done((f32[1024,512]{1,0:T(8,128)}, f32[1024,512]{1,0:T(8,128)}, u32[]{:S(2)}, u32[]{:S(2)}) %collective-permute-start.6) | collective-permute-done | bytes 2097184 | tf_op jit(solution)/shard_map/ppermute | solution.py:317
  112.9 1.1 collective-permute-done.7.refs_4_
  114.0 1.7 collective-permute-start.10
  115.7 2.0 collective-permute-start.9
  117.7 8.4 %plane2.1.ab_ref = f32[512,512]{1,0:T(8,128)} custom-call(s32[8]{0:T(128)} %concatenate.35.refs_0_, f32[512,8192]{1,0:T(8,128)} %xc3.1, f32[1024,512]{1,0:T(8,128)} %collective-permute-done.6.refs_2_, f32[512,8192]{1,0:T(8,128)} %xc3.1, f32[1024,512]{1,0:T(8,128)} %collective-permute-done.7.refs_4_, f32[512,512]{1,0:T(8,128)} %plane1.1.refs_5_), custom_call_target="tpu_custom_call" | custom-call | flops 3221225472 | bytes 8388608 | tf_op jit(solution)/shard_map/plane2/pallas_call | solution.py:112
  126.1 4.6 %collective-permute-done.11.refs_5_ = f32[2048,256]{1,0:T(8,128)} collective-permute-done((f32[2048,256]{1,0:T(8,128)}, f32[2048,256]{1,0:T(8,128)}, u32[]{:S(2)}, u32[]{:S(2)}) %collective-permute-start.11) | collective-permute-done | bytes 2097184 | tf_op jit(solution)/shard_map/ppermute | solution.py:316
  130.7 3.7 %collective-permute-start.12 = (f32[2048,256]{1,0:T(8,128)}, f32[2048,256]{1,0:T(8,128)}, u32[]{:S(2)}, u32[]{:S(2)}) collective-permute-start(f32[2048,256]{1,0:T(8,128)} %collective-permute-done.8.refs_5_), channel_id=1, source_target_pairs={{0,96},{16,48},{32,64},{48,16},{64,32},{80,112},{96,0},{112,80},{1... | collective-permute-start | bytes 6291464 | tf_op jit(solution)/shard_map/ppermute | solution.py:316
  134.4 0.5 fusion.refs_0_
  134.9 0.9 copy.9.scale_ref
  135.8 6.6 %deep2.1.c_ref = f32[512,256]{1,0:T(8,128)} custom-call(s32[16]{0:T(128)} %fusion.refs_0_, f32[512,8192]{1,0:T(8,128)} %xc3.1, f32[512,8192]{1,0:T(8,128)} %xc3.1, f32[512,8192]{1,0:T(8,128)} %xc3.1, f32[512,8192]{1,0:T(8,128)} %xc3.1, f32[2048,256]{1,0:T(8,128)} %collective-permute-done.11.refs_5_, f32[512,256]{1,0:T(8,128)} %deep1.1.refs_6_), custom_call_target="tpu_custom_call" | custom-call | flops 1610612736 | bytes 6291456 | tf_op jit(solution)/shard_map/deep2/pallas_call | solution.py:112
  142.3 11.9 %all-gather.6.cloned.1.call-done = f32[8192,256]{1,0:T(8,128)} async-done(((f32[128,256]{1,0:T(8,128)}), f32[8192,256]{1,0:T(8,128)}) %all-gather.6.cloned.1.call-update) | async-done | bytes 8388624 | tf_op jit(solution)/shard_map/all_gather | solution.py:397
  154.2 12.2 %rest.1.rest_ref = f32[512,256]{1,0:T(8,128)} custom-call(f32[512,8192]{1,0:T(8,128)} %xc3.1, f32[4,16,128,256]{3,2,1,0:T(8,128)} %bitcast.43), custom_call_target="tpu_custom_call" | custom-call | flops 6442450944 | bytes 25165824 | tf_op jit(solution)/shard_map/rest/pallas_call | solution.py:143
  166.4 0.9 collective-permute-done.12.wc
  167.3 0.5 copy-done.3
  167.8 15.2 %project.1 = (bf16[512,1024]{1,0:T(8,128)(2,1)}, bf16[512,1024]{1,0:T(8,128)(2,1)}, f32[1024,128]{1,0:T(8,128)}) custom-call(s32[24]{0:T(128)} %concatenate.30.index_ref, f32[512,8192]{1,0:T(8,128)} %xc3.1, f32[1024,512]{1,0:T(8,128)} %collective-permute-done.9.wa, f32[512,8192]{1,0:T(8,128)} %xc3.1, f32[1024,512]{1,0:T(8,128)} %copy-done.3, ...), custom_call_target="tpu_custom_call" | custom-call | flops 4831838208 | bytes 14680064 | tf_op jit(solution)/shard_map/project/pallas_call | solution.py:406
  183.0 17.3 %all_to_all.14 = f32[16,64,128]{2,1,0:T(8,128)S(1)} all-to-all(f32[16,64,128]{2,1,0:T(8,128)} %bitcast.48), channel_id=1, replica_groups=mesh['batch'=4,'head'=2,'seq'=16] {'seq'}, dimensions={0} | all-to-all | bytes 1048576 | tf_op jit(solution)/shard_map/all_to_all | solution.py:427
  200.4 13.8 %all_to_all.15 = f32[16,64,128]{2,1,0:T(8,128)S(1)} all-to-all(f32[16,64,128]{2,1,0:T(8,128)S(1)} %broadcast_in_dim.15), channel_id=1, replica_groups=mesh['batch'=4,'head'=2,'seq'=16] {'seq'}, dimensions={0} | all-to-all | bytes 1048576 | tf_op jit(solution)/shard_map/all_to_all | solution.py:429
  214.2 12.2 %factor.1 = (bf16[4,512,128]{2,1,0:T(8,128)(2,1)}, f32[4,128,128]{2,1,0:T(8,128)}) custom-call(f32[1024,128]{1,0:T(8,128)S(1)} %bitcast.42, f32[8,128,128]{2,1,0:T(8,128)S(1)} %copy-done, bf16[512,1024]{1,0:T(8,128)(2,1)S(1)} %copy-done.1, bf16[512,1024]{1,0:T(8,128)(2,1)S(1)} %copy-done.2), custom_call_target="tpu_custom_call" | custom-call | flops 1000000000 | bytes 4194304 | tf_op jit(solution)/shard_map/factor/pallas_call | solution.py:431
  (20 shorter events, 0.1 us)
Async XLA Ops:
  7.2 54.1 %all-gather.4.cloned.1.call-start = ((), (), s32[]{:S(2)}) async-start(), calls=%async_computation.2 | async-start | bytes 2228224 | tf_op jit(solution)/shard_map/all_gather | solution.py:395
  10.1 144.1 %all-gather.6.cloned.1.call-start = ((), (), s32[]{:S(2)}) async-start(), calls=%async_computation.3 | async-start | bytes 8519680 | tf_op jit(solution)/shard_map/all_gather | solution.py:397
  11.0 16.2 %copy-start.5 = (s32[4,2,128,64]{2,3,1,0:T(8,128)S(1)}, s32[4,2,128,64]{2,3,1,0:T(8,128)}, u32[]{:S(2)}) copy-start(s32[4,2,128,64]{2,3,1,0:T(8,128)} %param.9) | copy-start | bytes 786436
  11.0 9.3 %collective-permute-start = (f32[256,512]{1,0:T(8,128)S(1)}, f32[256,512]{1,0:T(8,128)S(1)}, u32[]{:S(2)}, u32[]{:S(2)}) collective-permute-start(f32[256,512]{1,0:T(8,128)S(1)} %get-tuple-element.46), channel_id=1, source_target_pairs={{0,4},{1,5},{2,6},{3,7},{4,0},{5,1},{6,2},{7,3},{8,12},{9,13},{10,... | collective-permute-start | bytes 1572872 | tf_op jit(solution)/shard_map/ppermute | solution.py:317
  12.6 9.2 %collective-permute-start.1 = (f32[256,512]{1,0:T(8,128)S(1)}, f32[256,512]{1,0:T(8,128)S(1)}, u32[]{:S(2)}, u32[]{:S(2)}) collective-permute-start(f32[256,512]{1,0:T(8,128)S(1)} %get-tuple-element.47), channel_id=1, source_target_pairs={{0,1},{1,0},{2,3},{3,2},{4,5},{5,4},{6,7},{7,6},{8,9},{9,8},{10,11... | collective-permute-start | bytes 1572872 | tf_op jit(solution)/shard_map/ppermute | solution.py:317
  22.0 17.0 %copy-start.7 = (s32[8,4]{0,1:T(4,128)S(1)}, s32[8,4]{0,1:T(4,128)}, u32[]{:S(2)}) copy-start(s32[8,4]{0,1:T(4,128)} %param.8) | copy-start | bytes 388
  22.0 18.3 %collective-permute-start.2 = (f32[512,512]{1,0:T(8,128)S(1)}, f32[512,512]{1,0:T(8,128)}, u32[]{:S(2)}, u32[]{:S(2)}) collective-permute-start(f32[512,512]{1,0:T(8,128)S(1)} %get-tuple-element.50), channel_id=1, source_target_pairs={{0,12},{1,13},{2,14},{3,15},{4,8},{5,9},{6,10},{7,11},{8,4},{9,5},... | collective-permute-start | bytes 3145736 | tf_op jit(solution)/shard_map/ppermute | solution.py:317
  24.2 17.5 %collective-permute-start.3 = (f32[512,512]{1,0:T(8,128)S(1)}, f32[512,512]{1,0:T(8,128)}, u32[]{:S(2)}, u32[]{:S(2)}) collective-permute-start(f32[512,512]{1,0:T(8,128)S(1)} %get-tuple-element.51), channel_id=1, source_target_pairs={{0,3},{1,2},{2,1},{3,0},{4,7},{5,6},{6,5},{7,4},{8,11},{9,10},{10,... | collective-permute-start | bytes 3145736 | tf_op jit(solution)/shard_map/ppermute | solution.py:317
  47.1 31.3 %collective-permute-start.4 = (f32[1024,512]{1,0:T(8,128)}, f32[1024,512]{1,0:T(8,128)S(1)}, u32[]{:S(2)}, u32[]{:S(2)}) collective-permute-start(f32[1024,512]{1,0:T(8,128)} %pad_maximum_fusion.refs_2_), channel_id=1, source_target_pairs={{0,1},{1,0},{2,3},{3,2},{4,5},{5,4},{6,7},{7,6},{8,9},{9,8},{10,11... | collective-permute-start | bytes 6291464 | tf_op jit(solution)/shard_map/ppermute | solution.py:317
  47.6 31.7 %collective-permute-start.5 = (f32[1024,512]{1,0:T(8,128)}, f32[1024,512]{1,0:T(8,128)}, u32[]{:S(2)}, u32[]{:S(2)}) collective-permute-start(f32[1024,512]{1,0:T(8,128)} %pad_maximum_fusion.1.refs_4_), channel_id=1, source_target_pairs={{0,4},{1,5},{2,6},{3,7},{4,0},{5,1},{6,2},{7,3},{8,12},{9,13},{10,... | collective-permute-start | bytes 6291464 | tf_op jit(solution)/shard_map/ppermute | solution.py:317
  61.2 27.7 %collective-permute-start.8 = (f32[2048,256]{1,0:T(8,128)}, f32[2048,256]{1,0:T(8,128)}, u32[]{:S(2)}, u32[]{:S(2)}) collective-permute-start(f32[2048,256]{1,0:T(8,128)} %all-gather.4.cloned.1.call-done.refs_5_), channel_id=1, source_target_pairs={{0,32},{16,112},{32,0},{48,80},{64,96},{80,48},{96,64},{112,16},{1... | collective-permute-start | bytes 6291464 | tf_op jit(solution)/shard_map/ppermute | solution.py:316
  78.4 21.7 %copy-start.4 = (f32[1024,512]{1,0:T(8,128)}, f32[1024,512]{1,0:T(8,128)S(1)}, u32[]{:S(2)}) copy-start(f32[1024,512]{1,0:T(8,128)S(1)} %collective-permute-done.4.refs_2_) | copy-start | bytes 6291460
  79.3 33.6 %collective-permute-start.6 = (f32[1024,512]{1,0:T(8,128)}, f32[1024,512]{1,0:T(8,128)}, u32[]{:S(2)}, u32[]{:S(2)}) collective-permute-start(f32[1024,512]{1,0:T(8,128)} %pad_maximum_fusion.refs_2_), channel_id=1, source_target_pairs={{0,3},{1,2},{2,1},{3,0},{4,7},{5,6},{6,5},{7,4},{8,11},{9,10},{10,... | collective-permute-start | bytes 6291464 | tf_op jit(solution)/shard_map/ppermute | solution.py:317
  80.7 33.3 %collective-permute-start.7 = (f32[1024,512]{1,0:T(8,128)}, f32[1024,512]{1,0:T(8,128)}, u32[]{:S(2)}, u32[]{:S(2)}) collective-permute-start(f32[1024,512]{1,0:T(8,128)} %pad_maximum_fusion.1.refs_4_), channel_id=1, source_target_pairs={{0,12},{1,13},{2,14},{3,15},{4,8},{5,9},{6,10},{7,11},{8,4},{9,5},... | collective-permute-start | bytes 6291464 | tf_op jit(solution)/shard_map/ppermute | solution.py:317
  89.0 41.7 %collective-permute-start.11 = (f32[2048,256]{1,0:T(8,128)}, f32[2048,256]{1,0:T(8,128)}, u32[]{:S(2)}, u32[]{:S(2)}) collective-permute-start(f32[2048,256]{1,0:T(8,128)} %all-gather.4.cloned.1.call-done.refs_5_), channel_id=1, source_target_pairs={{0,96},{16,48},{32,64},{48,16},{64,32},{80,112},{96,0},{112,80},{1... | collective-permute-start | bytes 6291464 | tf_op jit(solution)/shard_map/ppermute | solution.py:316
  108.6 26.3 %copy-start.6 = (f32[512]{0:T(512)S(1)}, f32[512]{0:T(512)}, u32[]{:S(2)}) copy-start(f32[512]{0:T(512)} %param.6) | copy-start | bytes 6148
  114.0 52.5 %collective-permute-start.10 = (f32[1024,512]{1,0:T(8,128)}, f32[1024,512]{1,0:T(8,128)S(1)}, u32[]{:S(2)}, u32[]{:S(2)}) collective-permute-start(f32[1024,512]{1,0:T(8,128)} %collective-permute-done.5.refs_4_), channel_id=1, source_target_pairs={{0,12},{1,13},{2,14},{3,15},{4,8},{5,9},{6,10},{7,11},{8,4},{9,5},... | collective-permute-start | bytes 6291464 | tf_op jit(solution)/shard_map/ppermute | solution.py:317
  115.7 50.8 %collective-permute-start.9 = (f32[1024,512]{1,0:T(8,128)}, f32[1024,512]{1,0:T(8,128)}, u32[]{:S(2)}, u32[]{:S(2)}) collective-permute-start(f32[1024,512]{1,0:T(8,128)} %copy-done.4), channel_id=1, source_target_pairs={{0,3},{1,2},{2,1},{3,0},{4,7},{5,6},{6,5},{7,4},{8,11},{9,10},{10,... | collective-permute-start | bytes 6291464 | tf_op jit(solution)/shard_map/ppermute | solution.py:317
  130.7 36.6 %collective-permute-start.12 = (f32[2048,256]{1,0:T(8,128)}, f32[2048,256]{1,0:T(8,128)}, u32[]{:S(2)}, u32[]{:S(2)}) collective-permute-start(f32[2048,256]{1,0:T(8,128)} %collective-permute-done.8.refs_5_), channel_id=1, source_target_pairs={{0,96},{16,48},{32,64},{48,16},{64,32},{80,112},{96,0},{112,80},{1... | collective-permute-start | bytes 6291464 | tf_op jit(solution)/shard_map/ppermute | solution.py:316
  166.4 1.3 copy-start.3
  183.0 31.2 %copy-start = (f32[8,128,128]{2,1,0:T(8,128)S(1)}, f32[8,128,128]{2,1,0:T(8,128)}, u32[]{:S(2)}) copy-start(f32[8,128,128]{2,1,0:T(8,128)} %start.1.start_ref) | copy-start | bytes 1572868
  183.0 31.2 %copy-start.1 = (bf16[512,1024]{1,0:T(8,128)(2,1)S(1)}, bf16[512,1024]{1,0:T(8,128)(2,1)}, u32[]{:S(2)}) copy-start(bf16[512,1024]{1,0:T(8,128)(2,1)} %get-tuple-element.88.high_ref) | copy-start | bytes 3145732
  183.0 31.2 %copy-start.2 = (bf16[512,1024]{1,0:T(8,128)(2,1)S(1)}, bf16[512,1024]{1,0:T(8,128)(2,1)}, u32[]{:S(2)}) copy-start(bf16[512,1024]{1,0:T(8,128)(2,1)} %get-tuple-element.89.low_ref) | copy-start | bytes 3145732
Sparse Core Ops, SparseCore 0:
  10.7 50.4 all-gather.3
  64.1 90.0 all-gather.5
